TPU v7x, 256 devices: a whole 4x4x8 slice. The times are simulated.
256 devices in a mesh: lat: 4 (over x_lo, core), lon: 64 (over x_hi, y, z).
Axes of the slice: x: 4 (x_hi: 2, x_lo: 2; x = x_hi * 2 + x_lo), y: 4, z: 8, core: 2. Of those that a mesh axis runs over, the one named last changes fastest.
Arguments:
- queries: bfloat16 [64, 1024, 1536], P('lat', 'lon'), may hold values from -12 to 12
- key_tokens: bfloat16 [64, 1024, 1536], P('lat', 'lon'), may hold values from -4 to 4
- value_tokens: bfloat16 [64, 1024, 1536], P('lat', 'lon'), may hold values from -6 to 6
- block_lists: int32 [8, 64, 8], P('lat', 'lon'), may hold values from 0 to 9, as said below
- band_rows: int32 [4, 1024], P('lat', 'lon'), may hold values from 0 to 255, as said below
Outputs:
- attended: bfloat16 [64, 1024, 1536], P('lat', 'lon')
Inputs may be any that keep to these rules, and one draw needn't show every extreme that they name: `block_lists`: entry 0 of the list of query block b of a tile is its own block, 4 + b; the other entries are distinct candidate numbers, also distinct from entry 0. `band_rows`: the 16 token numbers of each tile are distinct.
All inputs are finite; a program needn't handle non-finite values.
Results may differ from a plain program's by a relative error of at most 0.0047.
Values may be sent and summed in bfloat16 or wider, within the bound.
No kernel may reach another device: no remote copies, remote signals or barrier semaphores. Data moves between devices by JAX's collectives and lax.ppermute only.
A program may use at most 128 MiB of HBM per device.

v0:
```python
import jax
import jax.numpy as jnp
from jax import lax
from jax.sharding import PartitionSpec as P

H = 24
HD = 64
BR = 8
BW = 16


def from_behind(value, axis, steps):
    count = lax.axis_size(axis)
    pairs = [(source, (source + steps) % count) for source in range(count)]
    return lax.ppermute(value, axis, pairs)


def block_attention(q_rows, key_set, value_set, live_mask):
    count = q_rows.shape[0]
    q_heads = q_rows.reshape(count, H, HD)
    k_heads = key_set.reshape(key_set.shape[0], H, HD)
    v_heads = value_set.reshape(value_set.shape[0], H, HD)
    scores = jnp.einsum(
        "qhd,khd->hqk", q_heads, k_heads, preferred_element_type=jnp.float32
    ) * HD ** (-0.5)
    scores = jnp.where(live_mask[None, None, :], scores, -jnp.inf)
    row_max = jnp.max(scores, axis=-1, keepdims=True)
    exp_scores = jnp.exp(scores - row_max)
    totals = jnp.sum(exp_scores, axis=-1)
    weights = exp_scores.astype(jnp.bfloat16)
    mixture = jnp.einsum("hqk,khd->qhd", weights, v_heads, preferred_element_type=jnp.float32)
    mixture = mixture / jnp.transpose(totals)[:, :, None]
    return mixture.reshape(count, H * HD).astype(jnp.bfloat16)


def local(queries, key_tokens, value_tokens, block_lists, band_rows):
    tile_lat, tile_lon, feature = queries.shape
    block_len = BR * BW
    tile_blocks = tile_lat // BR
    lat_size = lax.axis_size("lat")
    west_two = from_behind((key_tokens, value_tokens), "lon", 2)
    west_one = from_behind((key_tokens, value_tokens), "lon", 1)
    east_one = from_behind((key_tokens, value_tokens), "lon", -1)
    east_two = from_behind((key_tokens, value_tokens), "lon", -2)
    sources = (west_two, west_one, (key_tokens, value_tokens), east_one, east_two)
    cand_keys = jnp.concatenate(
        [entry[0].reshape(tile_blocks, block_len, feature) for entry in sources], 0
    )
    cand_values = jnp.concatenate(
        [entry[1].reshape(tile_blocks, block_len, feature) for entry in sources], 0
    )
    picked_keys = key_tokens.reshape(tile_lat * tile_lon, feature)[band_rows[0]]
    picked_values = value_tokens.reshape(tile_lat * tile_lon, feature)[band_rows[0]]
    band_keys, band_values = (
        lax.all_gather(picked_keys, "lon", axis=0, tiled=True),
        lax.all_gather(picked_values, "lon", axis=0, tiled=True),
    )
    lat_at = lax.axis_index("lat")
    is_polar = (lat_at == 0) | (lat_at == lat_size - 1)
    listed_all = block_lists[:, 0, :]
    band_live = jnp.ones((band_keys.shape[0],), jnp.bool_)
    query_blocks = queries.reshape(tile_blocks, block_len, feature)

    def one_block(inputs):
        q_rows, listed = inputs
        near_keys = cand_keys[listed].reshape(-1, feature)
        near_values = cand_values[listed].reshape(-1, feature)
        near_live = jnp.ones((near_keys.shape[0],), jnp.bool_)

        def with_band():
            key_set = jnp.concatenate([near_keys, band_keys], 0)
            value_set = jnp.concatenate([near_values, band_values], 0)
            live_mask = jnp.concatenate([near_live, band_live], 0)
            return block_attention(q_rows, key_set, value_set, live_mask)

        def near_only():
            return block_attention(q_rows, near_keys, near_values, near_live)

        return lax.cond(is_polar, with_band, near_only)

    results = lax.map(one_block, (query_blocks, listed_all))
    return results.reshape(tile_lat, tile_lon, feature)


def solution(mesh):
    return jax.shard_map(
        local,
        mesh=mesh,
        in_specs=(
            P("lat", "lon", None),
            P("lat", "lon", None),
            P("lat", "lon", None),
            P("lat", "lon", None),
            P("lat", "lon"),
        ),
        out_specs=P("lat", "lon", None),
        check_vma=False,
    )
```

profile of v0, /device:TPU:0, one launch (start us, length us, event | category | flops | bytes accessed | tf_op | source)
XLA Modules:
  0.0 463.8 jit_solution(9054206073713176776)
XLA Ops:
  19.5 6.7 %collective-permute-start.2 = (bf16[16,16,1536]{2,1,0:T(8,128)(2,1)}, bf16[16,16,1536]{2,1,0:T(8,128)(2,1)S(1)}, u32[]{:S(2)}, u32[]{:S(2)}) collective-permute-start(bf16[16,16,1536]{2,1,0:T(8,128)(2,1)} %param.10), channel_id=1, source_target_pairs={{0,63},{1,0},{2,1},{3,2},{4,3},{5,4},{6,5},{7,6},{8,7},{9,8},{10,9... | collective-permute-start | bytes 2359304 | tf_op jit(solution)/shard_map/ppermute | solution.py:15
  26.3 22.0 %collective-permute-done.4 = bf16[16,16,1536]{2,1,0:T(8,128)(2,1)} collective-permute-done((bf16[16,16,1536]{2,1,0:T(8,128)(2,1)}, bf16[16,16,1536]{2,1,0:T(8,128)(2,1)}, u32[]{:S(2)}, u32[]{:S(2)}) %collective-permute-start.4) | collective-permute-done | bytes 786464 | tf_op jit(solution)/shard_map/ppermute | solution.py:15
  48.3 28.5 %collective-permute-start.6 = (bf16[16,16,1536]{2,1,0:T(8,128)(2,1)}, bf16[16,16,1536]{2,1,0:T(8,128)(2,1)S(1)}, u32[]{:S(2)}, u32[]{:S(2)}) collective-permute-start(bf16[16,16,1536]{2,1,0:T(8,128)(2,1)} %param.11), channel_id=1, source_target_pairs={{0,63},{1,0},{2,1},{3,2},{4,3},{5,4},{6,5},{7,6},{8,7},{9,8},{10,9... | collective-permute-start | bytes 2359304 | tf_op jit(solution)/shard_map/ppermute | solution.py:15
  78.9 5.0 %collective-permute-done = bf16[16,16,1536]{2,1,0:T(8,128)(2,1)} collective-permute-done((bf16[16,16,1536]{2,1,0:T(8,128)(2,1)}, bf16[16,16,1536]{2,1,0:T(8,128)(2,1)}, u32[]{:S(2)}, u32[]{:S(2)}) %collective-permute-start) | collective-permute-done | bytes 786464 | tf_op jit(solution)/shard_map/ppermute | solution.py:15
  83.9 12.7 %collective-permute-start.7 = (bf16[16,16,1536]{2,1,0:T(8,128)(2,1)}, bf16[16,16,1536]{2,1,0:T(8,128)(2,1)S(1)}, u32[]{:S(2)}, u32[]{:S(2)}) collective-permute-start(bf16[16,16,1536]{2,1,0:T(8,128)(2,1)} %param.11), channel_id=1, source_target_pairs={{0,62},{1,63},{2,0},{3,1},{4,2},{5,3},{6,4},{7,5},{8,6},{9,7},{10,... | collective-permute-start | bytes 2359304 | tf_op jit(solution)/shard_map/ppermute | solution.py:15
  98.8 13.4 %collective-permute-done.5 = bf16[16,16,1536]{2,1,0:T(8,128)(2,1)} collective-permute-done((bf16[16,16,1536]{2,1,0:T(8,128)(2,1)}, bf16[16,16,1536]{2,1,0:T(8,128)(2,1)}, u32[]{:S(2)}, u32[]{:S(2)}) %collective-permute-start.5) | collective-permute-done | bytes 786464 | tf_op jit(solution)/shard_map/ppermute | solution.py:15
  119.4 31.3 %collective-permute-done.7 = bf16[16,16,1536]{2,1,0:T(8,128)(2,1)S(1)} collective-permute-done((bf16[16,16,1536]{2,1,0:T(8,128)(2,1)}, bf16[16,16,1536]{2,1,0:T(8,128)(2,1)S(1)}, u32[]{:S(2)}, u32[]{:S(2)}) %collective-permute-start.7) | collective-permute-done | bytes 786464 | tf_op jit(solution)/shard_map/ppermute | solution.py:15
  154.4 14.3 %collective-permute-done.3 = bf16[16,16,1536]{2,1,0:T(8,128)(2,1)S(1)} collective-permute-done((bf16[16,16,1536]{2,1,0:T(8,128)(2,1)S(1)}, bf16[16,16,1536]{2,1,0:T(8,128)(2,1)S(1)}, u32[]{:S(2)}, u32[]{:S(2)}) %collective-permute-start.3) | collective-permute-done | bytes 786464 | tf_op jit(solution)/shard_map/ppermute | solution.py:15
  169.6 27.1 %all-gather.7.cloned.1.call-done = bf16[1024,1536]{1,0:T(8,128)(2,1)} async-done(((bf16[16,1536]{1,0:T(8,128)(2,1)}), bf16[1024,1536]{1,0:T(8,128)(2,1)}) %all-gather.7.cloned.1.call-update) | async-done | bytes 3145744 | tf_op jit(solution)/shard_map/all_gather | solution.py:55
  201.4 117.6 %all-gather.5.cloned.1.call-done = bf16[1024,1536]{1,0:T(8,128)(2,1)} async-done(((bf16[16,1536]{1,0:T(8,128)(2,1)}), bf16[1024,1536]{1,0:T(8,128)(2,1)}) %all-gather.5.cloned.1.call-update) | async-done | bytes 3145744 | tf_op jit(solution)/shard_map/all_gather | solution.py:56
  323.7 133.2 %while.10 = (s32[]{:T(128)}, bf16[2,128,1536]{2,1,0:T(8,128)(2,1)}, pred[]{:T(512)}, bf16[2,128,1536]{2,1,0:T(8,128)(2,1)}, s32[2,8]{1,0:T(2,128)S(1)}, /*index=...) while((s32[]{:T(128)}, bf16[2,128,1536]{2,1,0:T(8,128)(2,1)}, ...), condition=%wide.region_7.8_spmd, body=%wide.region_0.7_spmd.sunk | while | flops 1686498304 | bytes 169148896 | solution.py:81
  332.4 55.2 %conditional.7 = (bf16[1,128,1536]{1,2,0:T(8,128)(2,1)S(1)}) conditional(s32[]{:T(128)} %convert_element_type.36, (bf16[128,1536]{0,1:T(8,128)(2,1)S(1)}, bf16[8,128,1536]{2,1,0:T(8,128)(2,1)}, bf16[8,128,1536]{2,1,0:T(8,128)(2,1)S(1)}) %tuple.53, (bf16[8,128,1536]{2,1,0:T(8,128)(2,1)S(1)}, bf16[1024,1536]{0,1:T(8,128)(2,1)}, ...), branch_computations={%region_1.3_spmd, %region_4.6_spmd} | conditional | flops 1686497280 | bytes 151842912
  332.4 5.0 %copy.14 = bf16[8,128,1536]{1,0,2:T(8,128)(2,1)} copy(bf16[8,128,1536]{2,1,0:T(8,128)(2,1)} %get-tuple-element.102) | data formatting | bytes 6291456 | tf_op jit(solution)/shard_map
  337.4 5.8 %concatenate.17 = bf16[1024,24,64]{0,2,1:T(8,128)(2,1)} reshape(bf16[8,128,1536]{1,0,2:T(8,128)(2,1)} %copy.14) | data formatting | bytes 6291456 | tf_op jit(solution)/shard_map/while/body/eval_jaxpr/cond/branch_1_fun/concatenate | solution.py:71
  346.6 6.0 %concatenate.2 = bf16[1024,24,64]{0,2,1:T(8,128)(2,1)} reshape(bf16[8,128,1536]{1,0,2:T(8,128)(2,1)} %copy.13) | data formatting | bytes 6291456 | tf_op jit(solution)/shard_map/while/body/eval_jaxpr/cond/branch_1_fun/concatenate | solution.py:72
  352.5 11.8 %bitcast_reduce_fusion = (f32[24,128]{1,0:T(8,128)S(1)}, f32[24,2048,128]{2,1,0:T(8,128)}) fusion(bf16[128,24,64]{0,2,1:T(8,128)(2,1)S(1)} %bitcast.100, bf16[1024,24,64]{0,2,1:T(8,128)(2,1)} %bitcast.96, bf16[1024,24,64]{0,2,1:T(8,128)(2,1)S(1)} %copy-done.2), kind=kOutput, calls=%fused_computation.15 | convolution fusion | flops 830469120 | bytes 31862784 | tf_op jit(solution)/shard_map/while/body/eval_jaxpr/cond/branch_1_fun/qhd,khd->hqk/dot_general | solution.py:23
  364.4 11.7 %fusion.14 = f32[24,128]{1,0:T(8,128)S(1)} fusion(f32[24,2048,128]{2,1,0:T(8,128)} %get-tuple-element.135, f32[24,128]{1,0:T(8,128)S(1)} %get-tuple-element.134), kind=kLoop, calls=%fused_computation.17 | loop fusion | flops 18871296 | bytes 25190400 | tf_op jit(solution)/shard_map/while/body/eval_jaxpr/cond/branch_1_fun/reduce_sum | solution.py:29
  376.1 11.5 %fusion.32 = bf16[128,24,64]{0,2,1:T(8,128)(2,1)S(1)} fusion(f32[24,2048,128]{2,1,0:T(8,128)} %get-tuple-element.135, f32[24,128]{1,0:T(8,128)S(1)} %get-tuple-element.134, bf16[1024,24,64]{0,2,1:T(8,128)(2,1)S(1)} %bitcast.103, bf16[1024,24,64]{0,2,1:T(8,128)(2,1)S(1)} %copy-done.4, f32[128,24]{0,1:T(8,128)S(1)} %bitcast.113), kind=kOutput, calls=%fused_computation.30 | convolution fusion | flops 837156864 | bytes 31875072 | tf_op jit(solution)/shard_map/while/body/eval_jaxpr/cond/branch_1_fun/hqk,khd->qhd/dot_general | solution.py:31
  399.0 55.2 %conditional.7 = (bf16[1,128,1536]{1,2,0:T(8,128)(2,1)S(1)}) conditional(s32[]{:T(128)} %convert_element_type.36, (bf16[128,1536]{0,1:T(8,128)(2,1)S(1)}, bf16[8,128,1536]{2,1,0:T(8,128)(2,1)}, bf16[8,128,1536]{2,1,0:T(8,128)(2,1)S(1)}) %tuple.53, (bf16[8,128,1536]{2,1,0:T(8,128)(2,1)S(1)}, bf16[1024,1536]{0,1:T(8,128)(2,1)}, ...), branch_computations={%region_1.3_spmd, %region_4.6_spmd} | conditional | flops 1686497280 | bytes 151842912
  404.0 5.8 %concatenate.17 = bf16[1024,24,64]{0,2,1:T(8,128)(2,1)} reshape(bf16[8,128,1536]{1,0,2:T(8,128)(2,1)} %copy.14) | data formatting | bytes 6291456 | tf_op jit(solution)/shard_map/while/body/eval_jaxpr/cond/branch_1_fun/concatenate | solution.py:71
  413.2 6.0 %concatenate.2 = bf16[1024,24,64]{0,2,1:T(8,128)(2,1)} reshape(bf16[8,128,1536]{1,0,2:T(8,128)(2,1)} %copy.13) | data formatting | bytes 6291456 | tf_op jit(solution)/shard_map/while/body/eval_jaxpr/cond/branch_1_fun/concatenate | solution.py:72
  419.2 11.8 %bitcast_reduce_fusion = (f32[24,128]{1,0:T(8,128)S(1)}, f32[24,2048,128]{2,1,0:T(8,128)}) fusion(bf16[128,24,64]{0,2,1:T(8,128)(2,1)S(1)} %bitcast.100, bf16[1024,24,64]{0,2,1:T(8,128)(2,1)} %bitcast.96, bf16[1024,24,64]{0,2,1:T(8,128)(2,1)S(1)} %copy-done.2), kind=kOutput, calls=%fused_computation.15 | convolution fusion | flops 830469120 | bytes 31862784 | tf_op jit(solution)/shard_map/while/body/eval_jaxpr/cond/branch_1_fun/qhd,khd->hqk/dot_general | solution.py:23
  431.0 11.7 %fusion.14 = f32[24,128]{1,0:T(8,128)S(1)} fusion(f32[24,2048,128]{2,1,0:T(8,128)} %get-tuple-element.135, f32[24,128]{1,0:T(8,128)S(1)} %get-tuple-element.134), kind=kLoop, calls=%fused_computation.17 | loop fusion | flops 18871296 | bytes 25190400 | tf_op jit(solution)/shard_map/while/body/eval_jaxpr/cond/branch_1_fun/reduce_sum | solution.py:29
  442.7 11.5 %fusion.32 = bf16[128,24,64]{0,2,1:T(8,128)(2,1)S(1)} fusion(f32[24,2048,128]{2,1,0:T(8,128)} %get-tuple-element.135, f32[24,128]{1,0:T(8,128)S(1)} %get-tuple-element.134, bf16[1024,24,64]{0,2,1:T(8,128)(2,1)S(1)} %bitcast.103, bf16[1024,24,64]{0,2,1:T(8,128)(2,1)S(1)} %copy-done.4, f32[128,24]{0,1:T(8,128)S(1)} %bitcast.113), kind=kOutput, calls=%fused_computation.30 | convolution fusion | flops 837156864 | bytes 31875072 | tf_op jit(solution)/shard_map/while/body/eval_jaxpr/cond/branch_1_fun/hqk,khd->qhd/dot_general | solution.py:31
  (70 shorter events, 73.0 us)
Async XLA Ops:
  6.5 105.6 %copy-start.8 = (bf16[16,16,1536]{2,1,0:T(8,128)(2,1)S(1)}, bf16[16,16,1536]{2,1,0:T(8,128)(2,1)}, u32[]{:S(2)}) copy-start(bf16[16,16,1536]{2,1,0:T(8,128)(2,1)} %param.10) | copy-start | bytes 2359300
  6.5 110.9 %copy-start.7 = (bf16[16,16,1536]{2,1,0:T(8,128)(2,1)S(1)}, bf16[16,16,1536]{2,1,0:T(8,128)(2,1)}, u32[]{:S(2)}) copy-start(bf16[16,16,1536]{2,1,0:T(8,128)(2,1)} %param.11) | copy-start | bytes 2359300
  6.5 190.2 %all-gather.7.cloned.1.call-start = ((), (), s32[]{:S(2)}) async-start(), calls=%async_computation.1 | async-start | bytes 3194880 | tf_op jit(solution)/shard_map/all_gather | solution.py:55
  9.8 309.2 %all-gather.5.cloned.1.call-start = ((), (), s32[]{:S(2)}) async-start(), calls=%async_computation | async-start | bytes 3194880 | tf_op jit(solution)/shard_map/all_gather | solution.py:56
  12.4 35.9 %collective-permute-start.4 = (bf16[16,16,1536]{2,1,0:T(8,128)(2,1)}, bf16[16,16,1536]{2,1,0:T(8,128)(2,1)}, u32[]{:S(2)}, u32[]{:S(2)}) collective-permute-start(bf16[16,16,1536]{2,1,0:T(8,128)(2,1)} %param.11), channel_id=1, source_target_pairs={{0,2},{1,3},{2,4},{3,5},{4,6},{5,7},{6,8},{7,9},{8,10},{9,11},{10,... | collective-permute-start | bytes 2359304 | tf_op jit(solution)/shard_map/ppermute | solution.py:15
  14.0 69.9 %collective-permute-start = (bf16[16,16,1536]{2,1,0:T(8,128)(2,1)}, bf16[16,16,1536]{2,1,0:T(8,128)(2,1)}, u32[]{:S(2)}, u32[]{:S(2)}) collective-permute-start(bf16[16,16,1536]{2,1,0:T(8,128)(2,1)} %param.10), channel_id=1, source_target_pairs={{0,2},{1,3},{2,4},{3,5},{4,6},{5,7},{6,8},{7,9},{8,10},{9,11},{10,... | collective-permute-start | bytes 2359304 | tf_op jit(solution)/shard_map/ppermute | solution.py:15
  18.5 93.6 %collective-permute-start.5 = (bf16[16,16,1536]{2,1,0:T(8,128)(2,1)}, bf16[16,16,1536]{2,1,0:T(8,128)(2,1)}, u32[]{:S(2)}, u32[]{:S(2)}) collective-permute-start(bf16[16,16,1536]{2,1,0:T(8,128)(2,1)} %param.11), channel_id=1, source_target_pairs={{0,1},{1,2},{2,3},{3,4},{4,5},{5,6},{6,7},{7,8},{8,9},{9,10},{10,1... | collective-permute-start | bytes 2359304 | tf_op jit(solution)/shard_map/ppermute | solution.py:15
  19.5 134.0 %collective-permute-start.2 = (bf16[16,16,1536]{2,1,0:T(8,128)(2,1)}, bf16[16,16,1536]{2,1,0:T(8,128)(2,1)S(1)}, u32[]{:S(2)}, u32[]{:S(2)}) collective-permute-start(bf16[16,16,1536]{2,1,0:T(8,128)(2,1)} %param.10), channel_id=1, source_target_pairs={{0,63},{1,0},{2,1},{3,2},{4,3},{5,4},{6,5},{7,6},{8,7},{9,8},{10,9... | collective-permute-start | bytes 2359304 | tf_op jit(solution)/shard_map/ppermute | solution.py:15
  26.3 125.3 %collective-permute-start.1 = (bf16[16,16,1536]{2,1,0:T(8,128)(2,1)}, bf16[16,16,1536]{2,1,0:T(8,128)(2,1)S(1)}, u32[]{:S(2)}, u32[]{:S(2)}) collective-permute-start(bf16[16,16,1536]{2,1,0:T(8,128)(2,1)} %param.10), channel_id=1, source_target_pairs={{0,1},{1,2},{2,3},{3,4},{4,5},{5,6},{6,7},{7,8},{8,9},{9,10},{10,1... | collective-permute-start | bytes 2359304 | tf_op jit(solution)/shard_map/ppermute | solution.py:15
  48.3 70.1 %collective-permute-start.6 = (bf16[16,16,1536]{2,1,0:T(8,128)(2,1)}, bf16[16,16,1536]{2,1,0:T(8,128)(2,1)S(1)}, u32[]{:S(2)}, u32[]{:S(2)}) collective-permute-start(bf16[16,16,1536]{2,1,0:T(8,128)(2,1)} %param.11), channel_id=1, source_target_pairs={{0,63},{1,0},{2,1},{3,2},{4,3},{5,4},{6,5},{7,6},{8,7},{9,8},{10,9... | collective-permute-start | bytes 2359304 | tf_op jit(solution)/shard_map/ppermute | solution.py:15
  83.9 66.7 %collective-permute-start.7 = (bf16[16,16,1536]{2,1,0:T(8,128)(2,1)}, bf16[16,16,1536]{2,1,0:T(8,128)(2,1)S(1)}, u32[]{:S(2)}, u32[]{:S(2)}) collective-permute-start(bf16[16,16,1536]{2,1,0:T(8,128)(2,1)} %param.11), channel_id=1, source_target_pairs={{0,62},{1,63},{2,0},{3,1},{4,2},{5,3},{6,4},{7,5},{8,6},{9,7},{10,... | collective-permute-start | bytes 2359304 | tf_op jit(solution)/shard_map/ppermute | solution.py:15
  112.1 56.6 %collective-permute-start.3 = (bf16[16,16,1536]{2,1,0:T(8,128)(2,1)S(1)}, bf16[16,16,1536]{2,1,0:T(8,128)(2,1)S(1)}, u32[]{:S(2)}, u32[]{:S(2)}) collective-permute-start(bf16[16,16,1536]{2,1,0:T(8,128)(2,1)S(1)} %copy-done.8), channel_id=1, source_target_pairs={{0,62},{1,63},{2,0},{3,1},{4,2},{5,3},{6,4},{7,5},{8,6},{9,7},{10,... | collective-permute-start | bytes 2359304 | tf_op jit(solution)/shard_map/ppermute | solution.py:15
  201.4 122.3 %copy-start.9 = (s32[2,1,8]{2,1,0:T(1,128)S(1)}, s32[2,1,8]{2,1,0:T(1,128)}, u32[]{:S(2)}) copy-start(s32[2,1,8]{2,1,0:T(1,128)} %param.12) | copy-start | bytes 196
  346.6 6.0 %copy-start.2 = (bf16[1024,24,64]{0,2,1:T(8,128)(2,1)S(1)}, bf16[1024,24,64]{0,2,1:T(8,128)(2,1)}, u32[]{:S(2)}) copy-start(bf16[1024,24,64]{0,2,1:T(8,128)(2,1)} %concatenate.17) | copy-start | bytes 9437188 | tf_op jit(solution)/shard_map/conditional.1
  364.4 11.7 %copy-start.4 = (bf16[1024,24,64]{0,2,1:T(8,128)(2,1)S(1)}, bf16[1024,24,64]{0,2,1:T(8,128)(2,1)}, u32[]{:S(2)}) copy-start(bf16[1024,24,64]{0,2,1:T(8,128)(2,1)} %concatenate.2) | copy-start | bytes 9437188 | tf_op jit(solution)/shard_map/conditional.1
  364.4 11.7 %copy-start.6 = (bf16[1024,1536]{0,1:T(8,128)(2,1)S(1)}, bf16[1024,1536]{0,1:T(8,128)(2,1)}, u32[]{:S(2)}) copy-start(bf16[1024,1536]{0,1:T(8,128)(2,1)} %get-tuple-element.72) | copy-start | bytes 9437188 | tf_op jit(solution)/shard_map/conditional.1
  387.6 0.8 copy-start.5
  413.2 6.0 %copy-start.2 = (bf16[1024,24,64]{0,2,1:T(8,128)(2,1)S(1)}, bf16[1024,24,64]{0,2,1:T(8,128)(2,1)}, u32[]{:S(2)}) copy-start(bf16[1024,24,64]{0,2,1:T(8,128)(2,1)} %concatenate.17) | copy-start | bytes 9437188 | tf_op jit(solution)/shard_map/conditional.1
  431.0 11.7 %copy-start.4 = (bf16[1024,24,64]{0,2,1:T(8,128)(2,1)S(1)}, bf16[1024,24,64]{0,2,1:T(8,128)(2,1)}, u32[]{:S(2)}) copy-start(bf16[1024,24,64]{0,2,1:T(8,128)(2,1)} %concatenate.2) | copy-start | bytes 9437188 | tf_op jit(solution)/shard_map/conditional.1
  431.0 11.7 %copy-start.6 = (bf16[1024,1536]{0,1:T(8,128)(2,1)S(1)}, bf16[1024,1536]{0,1:T(8,128)(2,1)}, u32[]{:S(2)}) copy-start(bf16[1024,1536]{0,1:T(8,128)(2,1)} %get-tuple-element.72) | copy-start | bytes 9437188 | tf_op jit(solution)/shard_map/conditional.1
  454.2 0.8 copy-start.5
Sparse Core Ops, SparseCore 0:
  11.0 185.6 all-gather.6
  200.4 118.5 all-gather.4
where the time goes:
time: 467 us; the launch traced here: 464 us
  waiting for transfers between devices  231 us (49%)
  local copies, waits for them, and re-layouts  90.3 us (19%)
  starting transfers between devices  58.3 us (12%)
  matrix products  46.7 us (10%)
  other arithmetic  24.1 us (5%)
  between operations  13.4 us (3%)
    all_gather x1, waiting for transfers between devices, local(): lax.all_gather(picked_values, 'lon', axis=0, tiled=True)  118 us
    ppermute x8, waiting for transfers between devices, from_behind(): return lax.ppermute(value, axis, pairs)  86 us
    ppermute x8, starting transfers between devices, from_behind(): return lax.ppermute(value, axis, pairs)  58.3 us
    all_gather x1, waiting for transfers between devices, local(): lax.all_gather(picked_keys, 'lon', axis=0, tiled=True)  27.1 us
    dot_general x2, matrix products, block_attention(): jnp.einsum('qhd,khd->hqk', q_heads, k_heads, preferred_element_type=jnp.f...  23.7 us
    reduce_sum x2, other arithmetic, block_attention(): totals = jnp.sum(exp_scores, axis=-1)  23.3 us
    dot_general x2, matrix products, block_attention(): jnp.einsum('hqk,khd->qhd', weights, v_heads, preferred_element_type=jnp.f...  23 us
    another operation x16, local copies, waits for them, and re-layouts  16.8 us
  transfers between devices with their start and end apart: 10, of which 7 were waited for; matrix products, arithmetic and copies ran while one was open for 4% of the time, Pallas kernels for 0%

commit v1 on v0

v1 whole, which is shorter than its diff:
```python
import functools

import jax
import jax.numpy as jnp
from jax import lax
from jax.experimental import pallas as pl
from jax.experimental.pallas import tpu as pltpu
from jax.sharding import PartitionSpec as P

H = 24
HD = 64
BS = 128
TILE = 256
D = 1536
PAIR = 2 * HD
NB = 8
CAND = 10
N_LON = 64
LOG2E = 1.4426950408889634
CHUNK_PAIRS = (3, 3, 3, 3)
POLAR_LATS = (0, 3)


def step_lon(value, steps):
    pairs = [(source, (source + steps) % N_LON) for source in range(N_LON)]
    return lax.ppermute(value, "lon", pairs)


def polar_move(value, target_of):
    pairs = [
        (lat * N_LON + source, lat * N_LON + target_of(source))
        for lat in POLAR_LATS
        for source in range(N_LON)
    ]
    return lax.ppermute(value, ("lat", "lon"), pairs)


def along_z(steps):
    return lambda lon: (lon & ~7) | ((lon + steps) & 7)


def along_y(steps):
    return lambda lon: (lon & ~24) | ((lon + 8 * steps) & 24)


def across_x(lon):
    return lon ^ 32


def gather_band(picked):
    near = jnp.stack([picked, polar_move(picked, along_z(1)), polar_move(picked, along_z(-1))])
    row = jnp.concatenate([near, polar_move(near, along_z(3)), polar_move(near[:2], along_z(-3))])
    row = row.reshape(-1, row.shape[-1])
    both = jnp.concatenate([row, polar_move(row, across_x)])
    return (
        both,
        polar_move(both, along_y(1)),
        polar_move(both, along_y(-1)),
        polar_move(both, along_y(2)),
    )


def attend(queries, keys, values):
    scores = lax.dot_general(
        queries, keys, (((1,), (1,)), ((), ())), preferred_element_type=jnp.float32
    )
    row_max = jnp.max(scores, axis=1, keepdims=True)
    weights = jnp.exp2((scores - row_max) * LOG2E).astype(jnp.bfloat16)
    wide = jnp.concatenate([values, jnp.ones_like(values)], 1)
    mixed = jnp.dot(weights, wide, preferred_element_type=jnp.float32)
    return mixed[:, :PAIR] / mixed[:, PAIR:]


def attention_kernel(lists_ref, polar_ref, *refs):
    q_ref, tiles = refs[0], refs[1:6]
    band_k, band_v = refs[6:10], refs[10:14]
    out_ref, k_all, v_all = refs[-3:]
    for at, tile in enumerate(tiles):
        for block in range(2):
            rows = pl.ds(block * BS, BS)
            k_all[2 * at + block] = tile[0, rows, :]
            v_all[2 * at + block] = tile[1, rows, :]
    low = lax.broadcasted_iota(jnp.int32, (BS, PAIR), 1) < HD

    def run(with_band):
        for block in range(2):
            rows = pl.ds(block * BS, BS)
            q = q_ref[rows, :] * jnp.bfloat16(HD ** -0.5)
            zero = jnp.zeros_like(q)
            stacked = jnp.concatenate([jnp.where(low, q, zero), jnp.where(low, zero, q)], 0)
            picks = [lists_ref[block * NB + j] for j in range(NB)]
            keys = [k_all[pick] for pick in picks]
            values = [v_all[pick] for pick in picks]
            if with_band:
                keys += [ref[...] for ref in band_k]
                values += [ref[...] for ref in band_v]
            mixed = attend(stacked, jnp.concatenate(keys, 0), jnp.concatenate(values, 0))
            out_ref[rows, :] = jnp.where(low, mixed[:BS], mixed[BS:]).astype(out_ref.dtype)

    @pl.when(polar_ref[0] == 1)
    def _():
        run(True)

    @pl.when(polar_ref[0] == 0)
    def _():
        run(False)


def chunk_attention(first, count, lists, polar, queries, tiles, band, out):
    def of_chunk(p, lists_ref, polar_ref):
        return 0, 0, p

    def of_whole(p, lists_ref, polar_ref):
        return 0, first + p

    def of_band_k(p, lists_ref, polar_ref):
        return 0, (first + p) * polar_ref[0]

    def of_band_v(p, lists_ref, polar_ref):
        return 0, (D // PAIR + first + p) * polar_ref[0]

    whole = pl.BlockSpec((TILE, PAIR), of_whole)
    in_specs = (
        [whole]
        + [pl.BlockSpec((2, TILE, PAIR), of_chunk)] * 5
        + [pl.BlockSpec((TILE, PAIR), of_band_k)] * 4
        + [pl.BlockSpec((TILE, PAIR), of_band_v)] * 4
    )
    args = [lists, polar, queries, *tiles, *band, *band]
    aliases = {}
    if out is not None:
        in_specs.append(pl.BlockSpec(memory_space=pl.ANY))
        aliases = {len(args): 0}
        args.append(out)
    return pl.pallas_call(
        attention_kernel,
        out_shape=jax.ShapeDtypeStruct((TILE, D), jnp.bfloat16),
        grid_spec=pltpu.PrefetchScalarGridSpec(
            num_scalar_prefetch=2,
            grid=(count,),
            in_specs=in_specs,
            out_specs=whole,
            scratch_shapes=[pltpu.VMEM((CAND, BS, PAIR), jnp.bfloat16)] * 2,
        ),
        input_output_aliases=aliases,
        compiler_params=pltpu.CompilerParams(vmem_limit_bytes=48 << 20),
        cost_estimate=pl.CostEstimate(
            flops=count * 4 * TILE * 2048 * PAIR * 2,
            transcendentals=count * 2 * TILE * 2048,
            bytes_accessed=count * 14 * TILE * PAIR * 2,
        ),
        name=f"attention_{first}",
    )(*args)


def local(queries, key_tokens, value_tokens, block_lists, band_rows):
    q_rows = queries.reshape(TILE, D)
    k_rows = key_tokens.reshape(TILE, D)
    v_rows = value_tokens.reshape(TILE, D)
    lists = block_lists.reshape(2 * NB)
    lat_at = lax.axis_index("lat")
    polar = ((lat_at == 0) | (lat_at == lax.axis_size("lat") - 1)).astype(jnp.int32).reshape(1)
    picked = jnp.concatenate([k_rows[band_rows[0]], v_rows[band_rows[0]]], 1)
    chunks, at = [], 0
    for count in CHUNK_PAIRS:
        part = slice(at * PAIR, (at + count) * PAIR)
        own = jnp.stack([k_rows[:, part], v_rows[:, part]])
        west_one, east_one = step_lon(own, 1), step_lon(own, -1)
        west_two, east_two = step_lon(west_one, 1), step_lon(east_one, -1)
        chunks.append((at, count, (west_two, west_one, own, east_one, east_two)))
        at += count
    band = gather_band(picked)
    out = None
    for first, count, tiles in chunks:
        out = chunk_attention(first, count, lists, polar, q_rows, tiles, band, out)
    return out.reshape(queries.shape)


def solution(mesh):
    return jax.shard_map(
        local,
        mesh=mesh,
        in_specs=(
            P("lat", "lon", None),
            P("lat", "lon", None),
            P("lat", "lon", None),
            P("lat", "lon", None),
            P("lat", "lon"),
        ),
        out_specs=P("lat", "lon", None),
        check_vma=False,
    )
```

time: 467 us -> 202 us (0.43)
  waiting for transfers between devices: 231 us -> 35.8 us
  local copies, waits for them, and re-layouts: 90.3 us -> 13.6 us
  starting transfers between devices: 58.3 us -> 114 us
  matrix products: 46.7 us -> 0 us
  Pallas kernels: 0 us -> 35.8 us
  other arithmetic: 24.1 us -> 1.59 us
  between operations: 13.4 us -> 0.48 us
    all_gather x2 -> x0, waiting for transfers between devices: 145 us -> none  [the longest x1 118 us: local(): lax.all_gather(picked_values, 'lon', axis=0, tiled=True)]
    ppermute x8 -> x24, starting transfers between devices: 58.3 us -> 114 us  [the longest x16 66.2 us: step_lon(): return lax.ppermute(value, 'lon', pairs)]
    ppermute x8 -> x24, waiting for transfers between devices: 86 us -> 35.8 us  [the longest x16 20.5 us: step_lon(): return lax.ppermute(value, 'lon', pairs)]
    dot_general x4 -> x0, matrix products: 46.7 us -> none  [the longest x2 23.7 us: block_attention(): jnp.einsum('qhd,khd->hqk', q_heads, k_heads, preferred_element_type=jnp.f...]
    pallas_call x0 -> x4, Pallas kernels: none -> 35.8 us  [chunk_attention(): pl.pallas_call(attention_kernel, out_shape=jax.ShapeDtypeStruct((TILE, D)...]
    concatenate x6 -> x2, local copies, waits for them, and re-layouts: 25.5 us -> 0.02 us  [the longest x1 0.01 us: gather_band(): jnp.concatenate([near, polar_move(near, along_z(3)), polar_move(near[:2],...]
    reduce_sum x2 -> x0, other arithmetic: 23.3 us -> none  [block_attention(): totals = jnp.sum(exp_scores, axis=-1)]
    another operation x16 -> x2, local copies, waits for them, and re-layouts: 16.8 us -> 0.16 us  [local(): own = jnp.stack([k_rows[:, part], v_rows[:, part]])]
  transfers between devices with their start and end apart: 10 -> 24, of which waited for: 7 -> 10; matrix products, arithmetic and copies ran while one was open for 4% -> 1% of each run, Pallas kernels for 0% -> 13%
where the time goes in v1:
time: 202 us; the launch traced here: 201 us
  starting transfers between devices  114 us (56%)
  waiting for transfers between devices  35.8 us (18%)
  Pallas kernels  35.8 us (18%)
  local copies, waits for them, and re-layouts  13.6 us (7%)
    ppermute x16, starting transfers between devices, step_lon(): return lax.ppermute(value, 'lon', pairs)  66.2 us
    ppermute x8, starting transfers between devices, polar_move(): return lax.ppermute(value, ('lat', 'lon'), pairs)  47.5 us
    pallas_call x4, Pallas kernels, chunk_attention(): pl.pallas_call(attention_kernel, out_shape=jax.ShapeDtypeStruct((TILE, D)...  35.8 us
    ppermute x16, waiting for transfers between devices, step_lon(): return lax.ppermute(value, 'lon', pairs)  20.5 us
    ppermute x8, waiting for transfers between devices, polar_move(): return lax.ppermute(value, ('lat', 'lon'), pairs)  15.3 us
    unnamed x60, local copies, waits for them, and re-layouts  9.54 us
  transfers between devices with their start and end apart: 24, of which 10 were waited for; matrix products, arithmetic and copies ran while one was open for 1% of the time, Pallas kernels for 13%

profile of v1, /device:TPU:0, one launch (start us, length us, event | category | flops | bytes accessed | tf_op | source)
XLA Modules:
  0.0 201.1 jit_solution(2502375454047391711)
XLA Ops:
  4.5 2.1 %collective-permute-start.4 = (bf16[16,3072]{1,0:T(8,128)(2,1)S(1)}, bf16[16,3072]{1,0:T(8,128)(2,1)S(1)}, u32[]{:S(2)}, u32[]{:S(2)}) collective-permute-start(bf16[16,3072]{1,0:T(8,128)(2,1)S(1)} %constant_dynamic-update-slice_fusion), channel_id=1, source_target_pairs={{0,1},{1,2},{2,3},{3,4},{4,5},{5,6},{6,7},{7,0},{8,9},{9,10},{10,1... | collective-permute-start | bytes 294920 | tf_op jit(solution)/shard_map/ppermute | solution.py:35
  6.6 5.9 %collective-permute-start.5 = (bf16[16,3072]{1,0:T(8,128)(2,1)S(1)}, bf16[16,3072]{1,0:T(8,128)(2,1)S(1)}, u32[]{:S(2)}, u32[]{:S(2)}) collective-permute-start(bf16[16,3072]{1,0:T(8,128)(2,1)S(1)} %constant_dynamic-update-slice_fusion), channel_id=1, source_target_pairs={{0,7},{1,0},{2,1},{3,2},{4,3},{5,4},{6,5},{7,6},{8,15},{9,8},{10,9... | collective-permute-start | bytes 294920 | tf_op jit(solution)/shard_map/ppermute | solution.py:35
  14.7 8.6 %collective-permute-start.6 = (bf16[3,16,3072]{2,1,0:T(8,128)(2,1)S(1)}, bf16[3,16,3072]{2,1,0:T(8,128)(2,1)S(1)}, u32[]{:S(2)}, u32[]{:S(2)}) collective-permute-start(bf16[3,16,3072]{2,1,0:T(8,128)(2,1)S(1)} %pad_maximum_fusion.5), channel_id=1, source_target_pairs={{0,3},{1,4},{2,5},{3,6},{4,7},{5,0},{6,1},{7,2},{8,11},{9,12},{10,... | collective-permute-start | bytes 884744 | tf_op jit(solution)/shard_map/ppermute | solution.py:35
  25.3 10.6 %collective-permute-done.6 = bf16[3,16,3072]{2,1,0:T(8,128)(2,1)S(1)} collective-permute-done((bf16[3,16,3072]{2,1,0:T(8,128)(2,1)S(1)}, bf16[3,16,3072]{2,1,0:T(8,128)(2,1)S(1)}, u32[]{:S(2)}, u32[]{:S(2)}) %collective-permute-start.6) | collective-permute-done | bytes 294944 | tf_op jit(solution)/shard_map/ppermute | solution.py:35
  35.9 2.6 %collective-permute-done.7 = bf16[2,16,3072]{2,1,0:T(8,128)(2,1)S(1)} collective-permute-done((bf16[2,16,3072]{2,1,0:T(8,128)(2,1)S(1)}, bf16[2,16,3072]{2,1,0:T(8,128)(2,1)S(1)}, u32[]{:S(2)}, u32[]{:S(2)}) %collective-permute-start.7) | collective-permute-done | bytes 196640 | tf_op jit(solution)/shard_map/ppermute | solution.py:35
  38.5 5.0 %collective-permute-start.8 = (bf16[128,3072]{1,0:T(8,128)(2,1)S(1)}, bf16[128,3072]{1,0:T(8,128)(2,1)S(1)}, u32[]{:S(2)}, u32[]{:S(2)}) collective-permute-start(bf16[128,3072]{1,0:T(8,128)(2,1)S(1)} %bitcast.42), channel_id=1, source_target_pairs={{0,32},{1,33},{2,34},{3,35},{4,36},{5,37},{6,38},{7,39},{8,40},{9,... | collective-permute-start | bytes 2359304 | tf_op jit(solution)/shard_map/ppermute | solution.py:35
  44.8 6.8 %collective-permute-start.22 = (bf16[2,256,384]{2,1,0:T(8,128)(2,1)S(1)}, bf16[2,256,384]{2,1,0:T(8,128)(2,1)S(1)}, u32[]{:S(2)}, u32[]{:S(2)}) collective-permute-start(bf16[2,256,384]{2,1,0:T(8,128)(2,1)S(1)} %pad_maximum_fusion.4.refs_3_), channel_id=1, source_target_pairs={{0,63},{1,0},{2,1},{3,2},{4,3},{5,4},{6,5},{7,6},{8,7},{9,8},{10,9... | collective-permute-start | bytes 1179656 | tf_op jit(solution)/shard_map/ppermute | solution.py:26
  51.7 7.7 %collective-permute-start.18 = (bf16[2,256,384]{2,1,0:T(8,128)(2,1)S(1)}, bf16[2,256,384]{2,1,0:T(8,128)(2,1)}, u32[]{:S(2)}, u32[]{:S(2)}) collective-permute-start(bf16[2,256,384]{2,1,0:T(8,128)(2,1)S(1)} %pad_maximum_fusion.3.refs_3_), channel_id=1, source_target_pairs={{0,63},{1,0},{2,1},{3,2},{4,3},{5,4},{6,5},{7,6},{8,7},{9,8},{10,9... | collective-permute-start | bytes 1179656 | tf_op jit(solution)/shard_map/ppermute | solution.py:26
  60.5 19.4 %collective-permute-start.10 = (bf16[256,3072]{1,0:T(8,128)(2,1)S(1)}, bf16[256,3072]{1,0:T(8,128)(2,1)S(1)}, u32[]{:S(2)}, u32[]{:S(2)}) collective-permute-start(bf16[256,3072]{1,0:T(8,128)(2,1)S(1)} %pad_maximum_fusion.refs_6_.refs_10_), channel_id=1, source_target_pairs={{0,24},{1,25},{2,26},{3,27},{4,28},{5,29},{6,30},{7,31},{8,0},{9,1... | collective-permute-start | bytes 4718600 | tf_op jit(solution)/shard_map/ppermute | solution.py:35
  81.8 2.8 %collective-permute-start.9 = (bf16[256,3072]{1,0:T(8,128)(2,1)S(1)}, bf16[256,3072]{1,0:T(8,128)(2,1)S(1)}, u32[]{:S(2)}, u32[]{:S(2)}) collective-permute-start(bf16[256,3072]{1,0:T(8,128)(2,1)S(1)} %pad_maximum_fusion.refs_6_.refs_10_), channel_id=1, source_target_pairs={{0,8},{1,9},{2,10},{3,11},{4,12},{5,13},{6,14},{7,15},{8,16},{9,17... | collective-permute-start | bytes 4718600 | tf_op jit(solution)/shard_map/ppermute | solution.py:35
  84.6 8.5 %collective-permute-start.14 = (bf16[2,256,384]{2,1,0:T(8,128)(2,1)S(1)}, bf16[2,256,384]{2,1,0:T(8,128)(2,1)}, u32[]{:S(2)}, u32[]{:S(2)}) collective-permute-start(bf16[2,256,384]{2,1,0:T(8,128)(2,1)S(1)} %pad_maximum_fusion.2.refs_3_), channel_id=1, source_target_pairs={{0,63},{1,0},{2,1},{3,2},{4,3},{5,4},{6,5},{7,6},{8,7},{9,8},{10,9... | collective-permute-start | bytes 1179656 | tf_op jit(solution)/shard_map/ppermute | solution.py:26
  93.2 5.6 %collective-permute-done.14.refs_4_ = bf16[2,256,384]{2,1,0:T(8,128)(2,1)} collective-permute-done((bf16[2,256,384]{2,1,0:T(8,128)(2,1)S(1)}, bf16[2,256,384]{2,1,0:T(8,128)(2,1)}, u32[]{:S(2)}, u32[]{:S(2)}) %collective-permute-start.14) | collective-permute-done | bytes 393248 | tf_op jit(solution)/shard_map/ppermute | solution.py:26
  98.8 8.3 %collective-permute-start.2 = (bf16[2,256,384]{2,1,0:T(8,128)(2,1)S(1)}, bf16[2,256,384]{2,1,0:T(8,128)(2,1)S(1)}, u32[]{:S(2)}, u32[]{:S(2)}) collective-permute-start(bf16[2,256,384]{2,1,0:T(8,128)(2,1)S(1)} %pad_maximum_fusion.1.refs_3_), channel_id=1, source_target_pairs={{0,63},{1,0},{2,1},{3,2},{4,3},{5,4},{6,5},{7,6},{8,7},{9,8},{10,9... | collective-permute-start | bytes 1179656 | tf_op jit(solution)/shard_map/ppermute | solution.py:26
  107.9 3.5 %collective-permute-done.refs_2_ = bf16[2,256,384]{2,1,0:T(8,128)(2,1)S(1)} collective-permute-done((bf16[2,256,384]{2,1,0:T(8,128)(2,1)S(1)}, bf16[2,256,384]{2,1,0:T(8,128)(2,1)S(1)}, u32[]{:S(2)}, u32[]{:S(2)}) %collective-permute-start) | collective-permute-done | bytes 393248 | tf_op jit(solution)/shard_map/ppermute | solution.py:26
  111.3 6.2 %collective-permute-done.2.refs_4_ = bf16[2,256,384]{2,1,0:T(8,128)(2,1)S(1)} collective-permute-done((bf16[2,256,384]{2,1,0:T(8,128)(2,1)S(1)}, bf16[2,256,384]{2,1,0:T(8,128)(2,1)S(1)}, u32[]{:S(2)}, u32[]{:S(2)}) %collective-permute-start.2) | collective-permute-done | bytes 393248 | tf_op jit(solution)/shard_map/ppermute | solution.py:26
  117.6 9.8 %collective-permute-start.23 = (bf16[2,256,384]{2,1,0:T(8,128)(2,1)S(1)}, bf16[2,256,384]{2,1,0:T(8,128)(2,1)S(1)}, u32[]{:S(2)}, u32[]{:S(2)}) collective-permute-start(bf16[2,256,384]{2,1,0:T(8,128)(2,1)S(1)} %collective-permute-done.22.refs_4_), channel_id=1, source_target_pairs={{0,63},{1,0},{2,1},{3,2},{4,3},{5,4},{6,5},{7,6},{8,7},{9,8},{10,9... | collective-permute-start | bytes 1179656 | tf_op jit(solution)/shard_map/ppermute | solution.py:26
  128.8 3.8 %collective-permute-done.23.refs_5_ = bf16[2,256,384]{2,1,0:T(8,128)(2,1)S(1)} collective-permute-done((bf16[2,256,384]{2,1,0:T(8,128)(2,1)S(1)}, bf16[2,256,384]{2,1,0:T(8,128)(2,1)S(1)}, u32[]{:S(2)}, u32[]{:S(2)}) %collective-permute-start.23) | collective-permute-done | bytes 393248 | tf_op jit(solution)/shard_map/ppermute | solution.py:26
  133.4 8.3 %collective-permute-start.19 = (bf16[2,256,384]{2,1,0:T(8,128)(2,1)}, bf16[2,256,384]{2,1,0:T(8,128)(2,1)}, u32[]{:S(2)}, u32[]{:S(2)}) collective-permute-start(bf16[2,256,384]{2,1,0:T(8,128)(2,1)} %collective-permute-done.18.refs_4_), channel_id=1, source_target_pairs={{0,63},{1,0},{2,1},{3,2},{4,3},{5,4},{6,5},{7,6},{8,7},{9,8},{10,9... | collective-permute-start | bytes 1179656 | tf_op jit(solution)/shard_map/ppermute | solution.py:26
  143.2 7.8 %collective-permute-start.15 = (bf16[2,256,384]{2,1,0:T(8,128)(2,1)}, bf16[2,256,384]{2,1,0:T(8,128)(2,1)}, u32[]{:S(2)}, u32[]{:S(2)}) collective-permute-start(bf16[2,256,384]{2,1,0:T(8,128)(2,1)} %collective-permute-done.14.refs_4_), channel_id=1, source_target_pairs={{0,63},{1,0},{2,1},{3,2},{4,3},{5,4},{6,5},{7,6},{8,7},{9,8},{10,9... | collective-permute-start | bytes 1179656 | tf_op jit(solution)/shard_map/ppermute | solution.py:26
  152.3 7.7 %collective-permute-start.3 = (bf16[2,256,384]{2,1,0:T(8,128)(2,1)}, bf16[2,256,384]{2,1,0:T(8,128)(2,1)S(1)}, u32[]{:S(2)}, u32[]{:S(2)}) collective-permute-start(bf16[2,256,384]{2,1,0:T(8,128)(2,1)} %copy-done.15), channel_id=1, source_target_pairs={{0,63},{1,0},{2,1},{3,2},{4,3},{5,4},{6,5},{7,6},{8,7},{9,8},{10,9... | collective-permute-start | bytes 1179656 | tf_op jit(solution)/shard_map/ppermute | solution.py:26
  165.1 8.9 %attention_0.1.refs_14_ = bf16[256,1536]{1,0:T(8,128)(2,1)} custom-call(s32[16]{0:T(128)S(1)} %reshape.51.lists_ref, s32[1]{0:T(128)} %bitcast.polar_ref, bf16[256,1536]{1,0:T(8,128)(2,1)S(1)} %bitcast.32, bf16[2,256,384]{2,1,0:T(8,128)(2,1)S(1)} %copy-done.18, bf16[2,256,384]{2,1,0:T(8,128)(2,1)S(1)} %copy-done.8, ...), custom_call_target="tpu_custom_call" | custom-call | flops 1610612736 | bytes 2752512 | tf_op jit(solution)/shard_map/attention_0/pallas_call | solution.py:135
  174.0 8.9 %attention_3.1.refs_14_ = bf16[256,1536]{1,0:T(8,128)(2,1)} custom-call(s32[16]{0:T(128)S(1)} %reshape.51.lists_ref, s32[1]{0:T(128)} %bitcast.polar_ref, bf16[256,1536]{1,0:T(8,128)(2,1)S(1)} %bitcast.33, bf16[2,256,384]{2,1,0:T(8,128)(2,1)S(1)} %copy-done.20, bf16[2,256,384]{2,1,0:T(8,128)(2,1)S(1)} %copy-done.10, ...), custom_call_target="tpu_custom_call", output_to_operand_aliasing={{}: (16, {})} | custom-call | flops 1610612736 | bytes 2752512 | tf_op jit(solution)/shard_map/attention_3/pallas_call | solution.py:135
  183.0 8.9 %attention_6.1.refs_14_ = bf16[256,1536]{1,0:T(8,128)(2,1)} custom-call(s32[16]{0:T(128)S(1)} %reshape.51.lists_ref, s32[1]{0:T(128)} %bitcast.polar_ref, bf16[256,1536]{1,0:T(8,128)(2,1)S(1)} %bitcast.34, bf16[2,256,384]{2,1,0:T(8,128)(2,1)} %collective-permute-done.13.refs_1_, ...), custom_call_target="tpu_custom_call", output_to_operand_aliasing={{}: (16, {})} | custom-call | flops 1610612736 | bytes 2752512 | tf_op jit(solution)/shard_map/attention_6/pallas_call | solution.py:135
  191.9 9.1 %attention_9.1 = bf16[256,1536]{1,0:T(8,128)(2,1)} custom-call(s32[16]{0:T(128)S(1)} %reshape.51.lists_ref, s32[1]{0:T(128)} %bitcast.polar_ref, bf16[256,1536]{1,0:T(8,128)(2,1)S(1)} %bitcast.35, bf16[2,256,384]{2,1,0:T(8,128)(2,1)S(1)} %collective-permute-done.1.refs_1_, bf16[2,256,384]{2,1,0:T(8,128)(2,1)S(1)} %copy-done.14, ...), custom_call_target="tpu_custom_call", output_to_operand_aliasing={{}: (16, {})} | custom-call | flops 1610612736 | bytes 2752512 | tf_op jit(solution)/shard_map/attention_9/pallas_call | solution.py:135
  (105 shorter events, 23.9 us)
Async XLA Ops:
  4.5 8.6 %collective-permute-start.4 = (bf16[16,3072]{1,0:T(8,128)(2,1)S(1)}, bf16[16,3072]{1,0:T(8,128)(2,1)S(1)}, u32[]{:S(2)}, u32[]{:S(2)}) collective-permute-start(bf16[16,3072]{1,0:T(8,128)(2,1)S(1)} %constant_dynamic-update-slice_fusion), channel_id=1, source_target_pairs={{0,1},{1,2},{2,3},{3,4},{4,5},{5,6},{6,7},{7,0},{8,9},{9,10},{10,1... | collective-permute-start | bytes 294920 | tf_op jit(solution)/shard_map/ppermute | solution.py:35
  6.6 8.1 %collective-permute-start.5 = (bf16[16,3072]{1,0:T(8,128)(2,1)S(1)}, bf16[16,3072]{1,0:T(8,128)(2,1)S(1)}, u32[]{:S(2)}, u32[]{:S(2)}) collective-permute-start(bf16[16,3072]{1,0:T(8,128)(2,1)S(1)} %constant_dynamic-update-slice_fusion), channel_id=1, source_target_pairs={{0,7},{1,0},{2,1},{3,2},{4,3},{5,4},{6,5},{7,6},{8,15},{9,8},{10,9... | collective-permute-start | bytes 294920 | tf_op jit(solution)/shard_map/ppermute | solution.py:35
  14.7 21.2 %collective-permute-start.6 = (bf16[3,16,3072]{2,1,0:T(8,128)(2,1)S(1)}, bf16[3,16,3072]{2,1,0:T(8,128)(2,1)S(1)}, u32[]{:S(2)}, u32[]{:S(2)}) collective-permute-start(bf16[3,16,3072]{2,1,0:T(8,128)(2,1)S(1)} %pad_maximum_fusion.5), channel_id=1, source_target_pairs={{0,3},{1,4},{2,5},{3,6},{4,7},{5,0},{6,1},{7,2},{8,11},{9,12},{10,... | collective-permute-start | bytes 884744 | tf_op jit(solution)/shard_map/ppermute | solution.py:35
  23.3 15.2 %collective-permute-start.7 = (bf16[2,16,3072]{2,1,0:T(8,128)(2,1)S(1)}, bf16[2,16,3072]{2,1,0:T(8,128)(2,1)S(1)}, u32[]{:S(2)}, u32[]{:S(2)}) collective-permute-start(bf16[2,16,3072]{2,1,0:T(8,128)(2,1)S(1)} %pad_maximum_fusion.6), channel_id=1, source_target_pairs={{0,5},{1,6},{2,7},{3,0},{4,1},{5,2},{6,3},{7,4},{8,13},{9,14},{10,... | collective-permute-start | bytes 589832 | tf_op jit(solution)/shard_map/ppermute | solution.py:35
  38.5 21.0 %collective-permute-start.8 = (bf16[128,3072]{1,0:T(8,128)(2,1)S(1)}, bf16[128,3072]{1,0:T(8,128)(2,1)S(1)}, u32[]{:S(2)}, u32[]{:S(2)}) collective-permute-start(bf16[128,3072]{1,0:T(8,128)(2,1)S(1)} %bitcast.42), channel_id=1, source_target_pairs={{0,32},{1,33},{2,34},{3,35},{4,36},{5,37},{6,38},{7,39},{8,40},{9,... | collective-permute-start | bytes 2359304 | tf_op jit(solution)/shard_map/ppermute | solution.py:35
  43.8 16.7 %collective-permute-start.20 = (bf16[2,256,384]{2,1,0:T(8,128)(2,1)S(1)}, bf16[2,256,384]{2,1,0:T(8,128)(2,1)S(1)}, u32[]{:S(2)}, u32[]{:S(2)}) collective-permute-start(bf16[2,256,384]{2,1,0:T(8,128)(2,1)S(1)} %pad_maximum_fusion.4.refs_3_), channel_id=1, source_target_pairs={{0,1},{1,2},{2,3},{3,4},{4,5},{5,6},{6,7},{7,8},{8,9},{9,10},{10,1... | collective-permute-start | bytes 1179656 | tf_op jit(solution)/shard_map/ppermute | solution.py:26
  44.8 35.1 %collective-permute-start.22 = (bf16[2,256,384]{2,1,0:T(8,128)(2,1)S(1)}, bf16[2,256,384]{2,1,0:T(8,128)(2,1)S(1)}, u32[]{:S(2)}, u32[]{:S(2)}) collective-permute-start(bf16[2,256,384]{2,1,0:T(8,128)(2,1)S(1)} %pad_maximum_fusion.4.refs_3_), channel_id=1, source_target_pairs={{0,63},{1,0},{2,1},{3,2},{4,3},{5,4},{6,5},{7,6},{8,7},{9,8},{10,9... | collective-permute-start | bytes 1179656 | tf_op jit(solution)/shard_map/ppermute | solution.py:26
  51.7 30.1 %collective-permute-start.16 = (bf16[2,256,384]{2,1,0:T(8,128)(2,1)S(1)}, bf16[2,256,384]{2,1,0:T(8,128)(2,1)S(1)}, u32[]{:S(2)}, u32[]{:S(2)}) collective-permute-start(bf16[2,256,384]{2,1,0:T(8,128)(2,1)S(1)} %pad_maximum_fusion.3.refs_3_), channel_id=1, source_target_pairs={{0,1},{1,2},{2,3},{3,4},{4,5},{5,6},{6,7},{7,8},{8,9},{9,10},{10,1... | collective-permute-start | bytes 1179656 | tf_op jit(solution)/shard_map/ppermute | solution.py:26
  51.7 32.8 %collective-permute-start.18 = (bf16[2,256,384]{2,1,0:T(8,128)(2,1)S(1)}, bf16[2,256,384]{2,1,0:T(8,128)(2,1)}, u32[]{:S(2)}, u32[]{:S(2)}) collective-permute-start(bf16[2,256,384]{2,1,0:T(8,128)(2,1)S(1)} %pad_maximum_fusion.3.refs_3_), channel_id=1, source_target_pairs={{0,63},{1,0},{2,1},{3,2},{4,3},{5,4},{6,5},{7,6},{8,7},{9,8},{10,9... | collective-permute-start | bytes 1179656 | tf_op jit(solution)/shard_map/ppermute | solution.py:26
  59.6 33.6 %collective-permute-start.12 = (bf16[2,256,384]{2,1,0:T(8,128)(2,1)S(1)}, bf16[2,256,384]{2,1,0:T(8,128)(2,1)}, u32[]{:S(2)}, u32[]{:S(2)}) collective-permute-start(bf16[2,256,384]{2,1,0:T(8,128)(2,1)S(1)} %pad_maximum_fusion.2.refs_3_), channel_id=1, source_target_pairs={{0,1},{1,2},{2,3},{3,4},{4,5},{5,6},{6,7},{7,8},{8,9},{9,10},{10,1... | collective-permute-start | bytes 1179656 | tf_op jit(solution)/shard_map/ppermute | solution.py:26
  60.5 82.7 %collective-permute-start.10 = (bf16[256,3072]{1,0:T(8,128)(2,1)S(1)}, bf16[256,3072]{1,0:T(8,128)(2,1)S(1)}, u32[]{:S(2)}, u32[]{:S(2)}) collective-permute-start(bf16[256,3072]{1,0:T(8,128)(2,1)S(1)} %pad_maximum_fusion.refs_6_.refs_10_), channel_id=1, source_target_pairs={{0,24},{1,25},{2,26},{3,27},{4,28},{5,29},{6,30},{7,31},{8,0},{9,1... | collective-permute-start | bytes 4718600 | tf_op jit(solution)/shard_map/ppermute | solution.py:35
  79.8 72.4 %collective-permute-start.11 = (bf16[256,3072]{1,0:T(8,128)(2,1)S(1)}, bf16[256,3072]{1,0:T(8,128)(2,1)}, u32[]{:S(2)}, u32[]{:S(2)}) collective-permute-start(bf16[256,3072]{1,0:T(8,128)(2,1)S(1)} %pad_maximum_fusion.refs_6_.refs_10_), channel_id=1, source_target_pairs={{0,16},{1,17},{2,18},{3,19},{4,20},{5,21},{6,22},{7,23},{8,24},{9,... | collective-permute-start | bytes 4718600 | tf_op jit(solution)/shard_map/ppermute | solution.py:35
  81.8 70.5 %collective-permute-start.9 = (bf16[256,3072]{1,0:T(8,128)(2,1)S(1)}, bf16[256,3072]{1,0:T(8,128)(2,1)S(1)}, u32[]{:S(2)}, u32[]{:S(2)}) collective-permute-start(bf16[256,3072]{1,0:T(8,128)(2,1)S(1)} %pad_maximum_fusion.refs_6_.refs_10_), channel_id=1, source_target_pairs={{0,8},{1,9},{2,10},{3,11},{4,12},{5,13},{6,14},{7,15},{8,16},{9,17... | collective-permute-start | bytes 4718600 | tf_op jit(solution)/shard_map/ppermute | solution.py:35
  84.6 14.2 %collective-permute-start.14 = (bf16[2,256,384]{2,1,0:T(8,128)(2,1)S(1)}, bf16[2,256,384]{2,1,0:T(8,128)(2,1)}, u32[]{:S(2)}, u32[]{:S(2)}) collective-permute-start(bf16[2,256,384]{2,1,0:T(8,128)(2,1)S(1)} %pad_maximum_fusion.2.refs_3_), channel_id=1, source_target_pairs={{0,63},{1,0},{2,1},{3,2},{4,3},{5,4},{6,5},{7,6},{8,7},{9,8},{10,9... | collective-permute-start | bytes 1179656 | tf_op jit(solution)/shard_map/ppermute | solution.py:26
  93.1 18.2 %collective-permute-start = (bf16[2,256,384]{2,1,0:T(8,128)(2,1)S(1)}, bf16[2,256,384]{2,1,0:T(8,128)(2,1)S(1)}, u32[]{:S(2)}, u32[]{:S(2)}) collective-permute-start(bf16[2,256,384]{2,1,0:T(8,128)(2,1)S(1)} %pad_maximum_fusion.1.refs_3_), channel_id=1, source_target_pairs={{0,1},{1,2},{2,3},{3,4},{4,5},{5,6},{6,7},{7,8},{8,9},{9,10},{10,1... | collective-permute-start | bytes 1179656 | tf_op jit(solution)/shard_map/ppermute | solution.py:26
  98.8 18.7 %collective-permute-start.2 = (bf16[2,256,384]{2,1,0:T(8,128)(2,1)S(1)}, bf16[2,256,384]{2,1,0:T(8,128)(2,1)S(1)}, u32[]{:S(2)}, u32[]{:S(2)}) collective-permute-start(bf16[2,256,384]{2,1,0:T(8,128)(2,1)S(1)} %pad_maximum_fusion.1.refs_3_), channel_id=1, source_target_pairs={{0,63},{1,0},{2,1},{3,2},{4,3},{5,4},{6,5},{7,6},{8,7},{9,8},{10,9... | collective-permute-start | bytes 1179656 | tf_op jit(solution)/shard_map/ppermute | solution.py:26
  111.3 16.7 %collective-permute-start.21 = (bf16[2,256,384]{2,1,0:T(8,128)(2,1)S(1)}, bf16[2,256,384]{2,1,0:T(8,128)(2,1)S(1)}, u32[]{:S(2)}, u32[]{:S(2)}) collective-permute-start(bf16[2,256,384]{2,1,0:T(8,128)(2,1)S(1)} %collective-permute-done.20.refs_2_), channel_id=1, source_target_pairs={{0,1},{1,2},{2,3},{3,4},{4,5},{5,6},{6,7},{7,8},{8,9},{9,10},{10,1... | collective-permute-start | bytes 1179656 | tf_op jit(solution)/shard_map/ppermute | solution.py:26
  117.6 15.1 %collective-permute-start.23 = (bf16[2,256,384]{2,1,0:T(8,128)(2,1)S(1)}, bf16[2,256,384]{2,1,0:T(8,128)(2,1)S(1)}, u32[]{:S(2)}, u32[]{:S(2)}) collective-permute-start(bf16[2,256,384]{2,1,0:T(8,128)(2,1)S(1)} %collective-permute-done.22.refs_4_), channel_id=1, source_target_pairs={{0,63},{1,0},{2,1},{3,2},{4,3},{5,4},{6,5},{7,6},{8,7},{9,8},{10,9... | collective-permute-start | bytes 1179656 | tf_op jit(solution)/shard_map/ppermute | solution.py:26
  128.8 13.6 %collective-permute-start.17 = (bf16[2,256,384]{2,1,0:T(8,128)(2,1)S(1)}, bf16[2,256,384]{2,1,0:T(8,128)(2,1)S(1)}, u32[]{:S(2)}, u32[]{:S(2)}) collective-permute-start(bf16[2,256,384]{2,1,0:T(8,128)(2,1)S(1)} %collective-permute-done.16.refs_2_), channel_id=1, source_target_pairs={{0,1},{1,2},{2,3},{3,4},{4,5},{5,6},{6,7},{7,8},{8,9},{9,10},{10,1... | collective-permute-start | bytes 1179656 | tf_op jit(solution)/shard_map/ppermute | solution.py:26
  133.4 40.6 %collective-permute-start.19 = (bf16[2,256,384]{2,1,0:T(8,128)(2,1)}, bf16[2,256,384]{2,1,0:T(8,128)(2,1)}, u32[]{:S(2)}, u32[]{:S(2)}) collective-permute-start(bf16[2,256,384]{2,1,0:T(8,128)(2,1)} %collective-permute-done.18.refs_4_), channel_id=1, source_target_pairs={{0,63},{1,0},{2,1},{3,2},{4,3},{5,4},{6,5},{7,6},{8,7},{9,8},{10,9... | collective-permute-start | bytes 1179656 | tf_op jit(solution)/shard_map/ppermute | solution.py:26
  143.2 39.8 %collective-permute-start.13 = (bf16[2,256,384]{2,1,0:T(8,128)(2,1)}, bf16[2,256,384]{2,1,0:T(8,128)(2,1)}, u32[]{:S(2)}, u32[]{:S(2)}) collective-permute-start(bf16[2,256,384]{2,1,0:T(8,128)(2,1)} %collective-permute-done.12.refs_2_), channel_id=1, source_target_pairs={{0,1},{1,2},{2,3},{3,4},{4,5},{5,6},{6,7},{7,8},{8,9},{9,10},{10,1... | collective-permute-start | bytes 1179656 | tf_op jit(solution)/shard_map/ppermute | solution.py:26
  143.2 39.8 %collective-permute-start.15 = (bf16[2,256,384]{2,1,0:T(8,128)(2,1)}, bf16[2,256,384]{2,1,0:T(8,128)(2,1)}, u32[]{:S(2)}, u32[]{:S(2)}) collective-permute-start(bf16[2,256,384]{2,1,0:T(8,128)(2,1)} %collective-permute-done.14.refs_4_), channel_id=1, source_target_pairs={{0,63},{1,0},{2,1},{3,2},{4,3},{5,4},{6,5},{7,6},{8,7},{9,8},{10,9... | collective-permute-start | bytes 1179656 | tf_op jit(solution)/shard_map/ppermute | solution.py:26
  152.2 39.6 %collective-permute-start.1 = (bf16[2,256,384]{2,1,0:T(8,128)(2,1)}, bf16[2,256,384]{2,1,0:T(8,128)(2,1)S(1)}, u32[]{:S(2)}, u32[]{:S(2)}) collective-permute-start(bf16[2,256,384]{2,1,0:T(8,128)(2,1)} %copy-done.13), channel_id=1, source_target_pairs={{0,1},{1,2},{2,3},{3,4},{4,5},{5,6},{6,7},{7,8},{8,9},{9,10},{10,1... | collective-permute-start | bytes 1179656 | tf_op jit(solution)/shard_map/ppermute | solution.py:26
  152.3 39.6 %collective-permute-start.3 = (bf16[2,256,384]{2,1,0:T(8,128)(2,1)}, bf16[2,256,384]{2,1,0:T(8,128)(2,1)S(1)}, u32[]{:S(2)}, u32[]{:S(2)}) collective-permute-start(bf16[2,256,384]{2,1,0:T(8,128)(2,1)} %copy-done.15), channel_id=1, source_target_pairs={{0,63},{1,0},{2,1},{3,2},{4,3},{5,4},{6,5},{7,6},{8,7},{9,8},{10,9... | collective-permute-start | bytes 1179656 | tf_op jit(solution)/shard_map/ppermute | solution.py:26
  (27 other events, 499.5 us)

commit v2 on v1

v2 whole, which is shorter than its diff:
```python
import jax
import jax.numpy as jnp
from jax import lax
from jax.experimental import pallas as pl
from jax.experimental.pallas import tpu as pltpu
from jax.sharding import PartitionSpec as P

H = 24
HD = 64
BS = 128
TILE = 256
D = 1536
PAIR = 2 * HD
NB = 8
CAND = 10
N_LON = 64
LOG2E = 1.4426950408889634
STEP = 2 * PAIR
POLAR_LATS = (0, 3)


def step_lon(value, steps):
    pairs = [(source, (source + steps) % N_LON) for source in range(N_LON)]
    return lax.ppermute(value, "lon", pairs)


def core_move(value, toward_polar):
    pairs = [
        (side, home) if toward_polar else (home, side)
        for polar_lat, side_lat in ((0, 1), (3, 2))
        for home, side in (
            (polar_lat * N_LON + lon, side_lat * N_LON + lon) for lon in range(N_LON)
        )
    ]
    return lax.ppermute(value, ("lat", "lon"), pairs)


def share(value, groups):
    copies = jnp.broadcast_to(value, (8,) + value.shape)
    got = lax.all_to_all(copies, "lon", 0, 0, axis_index_groups=groups)
    return got.reshape((-1,) + value.shape[1:])


Z_LINES = [[first + z for z in range(8)] for first in range(0, N_LON, 8)]


def move(value, target_of):
    return lax.ppermute(value, "lon", [(lon, target_of(lon)) for lon in range(N_LON)])


def along_y(steps):
    return lambda lon: (lon & ~24) | ((lon + 8 * steps) & 24)


def across_x(lon):
    return lon ^ 32


def attend(queries, keys, values):
    scores = lax.dot_general(
        queries, keys, (((1,), (1,)), ((), ())), preferred_element_type=jnp.float32
    )
    row_max = jnp.max(scores, axis=1, keepdims=True)
    weights = jnp.exp2((scores - row_max) * LOG2E).astype(jnp.bfloat16)
    wide = jnp.concatenate([values, jnp.ones_like(values)], 1)
    mixed = jnp.dot(weights, wide, preferred_element_type=jnp.float32)
    return mixed[:, :PAIR] / mixed[:, PAIR:]


def attention_kernel(lists_ref, polar_ref, *refs):
    q_ref, k_tiles, v_tiles = refs[0], refs[1:6], refs[6:11]
    band_k, band_v = refs[11:16], refs[16:21]
    out_ref, k_all, v_all = refs[21:]
    for at in range(5):
        for block in range(2):
            rows = pl.ds(block * BS, BS)
            k_all[2 * at + block] = k_tiles[at][rows, :]
            v_all[2 * at + block] = v_tiles[at][rows, :]
    low = lax.broadcasted_iota(jnp.int32, (BS, PAIR), 1) < HD

    def run(with_band):
        for part in range(STEP // PAIR):
            lanes = slice(part * PAIR, (part + 1) * PAIR)
            for block in range(2):
                rows = pl.ds(block * BS, BS)
                q = q_ref[rows, lanes] * jnp.bfloat16(HD ** -0.5)
                zero = jnp.zeros_like(q)
                stacked = jnp.concatenate([jnp.where(low, q, zero), jnp.where(low, zero, q)], 0)
                picks = [lists_ref[block * NB + j] for j in range(NB)]
                keys = [k_all[pick, :, lanes] for pick in picks]
                values = [v_all[pick, :, lanes] for pick in picks]
                if with_band:
                    keys += [ref[:, lanes] for ref in band_k]
                    values += [ref[:, lanes] for ref in band_v]
                mixed = attend(stacked, jnp.concatenate(keys, 0), jnp.concatenate(values, 0))
                out_ref[rows, lanes] = jnp.where(low, mixed[:BS], mixed[BS:]).astype(out_ref.dtype)

    @pl.when(polar_ref[0] == 1)
    def _():
        run(True)

    @pl.when(polar_ref[0] == 0)
    def _():
        run(False)


def attention(lists, polar, queries, keys, values, band_k, band_v):
    column = pl.BlockSpec((TILE, STEP), lambda p, lists_ref, polar_ref: (0, p))
    band = [
        pl.BlockSpec((part.shape[0], STEP), lambda p, lists_ref, polar_ref: (0, p * polar_ref[0]))
        for part in band_k
    ]
    return pl.pallas_call(
        attention_kernel,
        out_shape=jax.ShapeDtypeStruct((TILE, D), jnp.bfloat16),
        grid_spec=pltpu.PrefetchScalarGridSpec(
            num_scalar_prefetch=2,
            grid=(D // STEP,),
            in_specs=[column] * 11 + band * 2,
            out_specs=column,
            scratch_shapes=[pltpu.VMEM((10, BS, STEP), jnp.bfloat16)] * 2,
        ),
        compiler_params=pltpu.CompilerParams(vmem_limit_bytes=60 << 20),
        cost_estimate=pl.CostEstimate(
            flops=4 * TILE * 2048 * D, transcendentals=0, bytes_accessed=TILE * D * 30
        ),
        name="attention",
    )(lists, polar, queries, *keys, *values, *band_k, *band_v)


def local(queries, key_tokens, value_tokens, block_lists, band_rows):
    q = queries.reshape(TILE, D)
    k = key_tokens.reshape(TILE, D)
    v = value_tokens.reshape(TILE, D)
    lists = block_lists.reshape(2 * NB)
    lat_at = lax.axis_index("lat")
    is_polar = (lat_at == 0) | (lat_at == lax.axis_size("lat") - 1)
    polar = is_polar.astype(jnp.int32).reshape(1)
    fence = lax.optimization_barrier

    picked = jnp.where(is_polar, k[band_rows[0]], core_move(v[band_rows[0]], False))
    k_west, k_east = step_lon(k, 1), step_lon(k, -1)
    k_west, k_east, v_sent = fence((k_west, k_east, v))
    v_west, v_east = step_lon(v_sent, 1), step_lon(v_sent, -1)
    k_west, k_east, v_west, v_east = fence((k_west, k_east, v_west, v_east))
    k_west2, k_east2 = step_lon(k_west, 1), step_lon(k_east, -1)
    v_west, v_east, k_west2, k_east2 = fence((v_west, v_east, k_west2, k_east2))
    v_west2, v_east2 = step_lon(v_west, 1), step_lon(v_east, -1)

    line = share(picked, Z_LINES)
    both = jnp.concatenate([line, move(line, across_x)], 0)
    south, north = move(both, along_y(1)), move(both, along_y(-1))
    z_at = lax.axis_index("lon") & 7
    first = jnp.where(z_at == 0, north[:BS], south[:BS])
    second = jnp.where(z_at == 7, south[BS:], north[BS:])
    south2 = move(first, lambda lon: along_y(-1 if lon & 7 == 0 else 1)(lon))
    north2 = move(second, lambda lon: along_y(1 if lon & 7 == 7 else -1)(lon))
    band = [both, south, north, south2, north2]
    band_v = [core_move(part, True) for part in band]
    out = attention(
        lists,
        polar,
        q,
        (k_west2, k_west, k, k_east, k_east2),
        (v_west2, v_west, v, v_east, v_east2),
        band,
        band_v,
    )
    return out.reshape(queries.shape)


def solution(mesh):
    return jax.shard_map(
        local,
        mesh=mesh,
        in_specs=(
            P("lat", "lon", None),
            P("lat", "lon", None),
            P("lat", "lon", None),
            P("lat", "lon", None),
            P("lat", "lon"),
        ),
        out_specs=P("lat", "lon", None),
        check_vma=False,
    )
```

time: 202 us -> 162 us (0.80)
  starting transfers between devices: 114 us -> 44.3 us
  waiting for transfers between devices: 35.8 us -> 84.6 us
  Pallas kernels: 35.8 us -> 23.5 us
  local copies, waits for them, and re-layouts: 13.6 us -> 7.24 us
    ppermute x16 -> x8, starting transfers between devices: 66.2 us -> 19.4 us  [step_lon(): return lax.ppermute(value, 'lon', pairs)]
    ppermute x8 -> x11, starting transfers between devices: 47.5 us -> 17.7 us  [the longest x5 9.72 us: move(): lax.ppermute(value, 'lon', [(lon, target_of(lon)) for lon in range(N_LON)])]
    ppermute x8 -> x11, waiting for transfers between devices: 15.3 us -> 41.7 us  [the longest x5 40.5 us: move(): lax.ppermute(value, 'lon', [(lon, target_of(lon)) for lon in range(N_LON)])]
    ppermute x16 -> x8, waiting for transfers between devices: 20.5 us -> 35.9 us  [step_lon(): return lax.ppermute(value, 'lon', pairs)]
    pallas_call x4 -> x1, Pallas kernels: 35.8 us -> 23.5 us  [attention(): pl.pallas_call(attention_kernel, out_shape=jax.ShapeDtypeStruct((TILE, D)...]
    unnamed x60 -> x33, local copies, waits for them, and re-layouts: 9.54 us -> 2.06 us
    all_to_all x0 -> x1, starting transfers between devices: none -> 7.18 us  [share(): got = lax.all_to_all(copies, 'lon', 0, 0, axis_index_groups=groups)]
    all_to_all x0 -> x1, waiting for transfers between devices: none -> 6.94 us  [share(): got = lax.all_to_all(copies, 'lon', 0, 0, axis_index_groups=groups)]
  transfers between devices with their start and end apart: 24 -> 20, of which waited for: 10 -> 11; matrix products, arithmetic and copies ran while one was open for 1% -> 2% of each run, Pallas kernels for 13% -> 0%
where the time goes in v2:
time: 162 us
  waiting for transfers between devices  84.6 us (52%)
  starting transfers between devices  44.3 us (27%)
  Pallas kernels  23.5 us (15%)
  local copies, waits for them, and re-layouts  7.24 us (4%)
    ppermute x5, waiting for transfers between devices, move(): lax.ppermute(value, 'lon', [(lon, target_of(lon)) for lon in range(N_LON)])  40.5 us
    ppermute x8, waiting for transfers between devices, step_lon(): return lax.ppermute(value, 'lon', pairs)  35.9 us
    pallas_call x1, Pallas kernels, attention(): pl.pallas_call(attention_kernel, out_shape=jax.ShapeDtypeStruct((TILE, D)...  23.5 us
    ppermute x8, starting transfers between devices, step_lon(): return lax.ppermute(value, 'lon', pairs)  19.4 us
    ppermute x5, starting transfers between devices, move(): lax.ppermute(value, 'lon', [(lon, target_of(lon)) for lon in range(N_LON)])  9.72 us
    ppermute x6, starting transfers between devices, core_move(): return lax.ppermute(value, ('lat', 'lon'), pairs)  8.01 us
    all_to_all x1, starting transfers between devices, share(): got = lax.all_to_all(copies, 'lon', 0, 0, axis_index_groups=groups)  7.18 us
    all_to_all x1, waiting for transfers between devices, share(): got = lax.all_to_all(copies, 'lon', 0, 0, axis_index_groups=groups)  6.94 us
  transfers between devices with their start and end apart: 20, of which 11 were waited for; matrix products, arithmetic and copies ran while one was open for 2% of the time, Pallas kernels for 0%

profile of v2, /device:TPU:0, one launch (start us, length us, event | category | flops | bytes accessed | tf_op | source)
XLA Modules:
  0.0 161.6 jit_solution(9948798412219588094)
XLA Ops:
  0.7 1.9 %gather_fusion.1 = bf16[16,1536]{1,0:T(8,128)(2,1)S(1)} fusion(bf16[256,1536]{1,0:T(8,128)(2,1)} %bitcast.3.refs_8_, s32[1024]{0:T(1024)S(1)} %pad_clamp_fusion), kind=kCustom, calls=%fused_computation.1 | custom fusion | bytes 98368 | tf_op jit(solution)/shard_map/gather | solution.py:141
  2.5 1.3 collective-permute-start.8
  3.9 1.9 %gather_fusion = bf16[16,1536]{1,0:T(8,128)(2,1)S(1)} fusion(bf16[256,1536]{1,0:T(8,128)(2,1)} %bitcast.10, s32[1024]{0:T(1024)S(1)} %pad_clamp_fusion), kind=kCustom, calls=%fused_computation | custom fusion | bytes 98368 | tf_op jit(solution)/shard_map/gather | solution.py:141
  6.5 7.2 %all-to-all-start = ((bf16[8,16,1536]{2,1,0:T(8,128)(2,1)}), bf16[8,16,1536]{2,1,0:T(8,128)(2,1)S(1)}, u32[]{:S(2)}, u32[]{:S(2)}) async-start(bf16[8,16,1536]{2,1,0:T(8,128)(2,1)} %broadcast_in_dim.2), calls=%async_computation | async-start | bytes 786432 | tf_op jit(solution)/shard_map/all_to_all | solution.py:40
  13.7 8.1 %collective-permute-start.1 = (bf16[256,1536]{1,0:T(8,128)(2,1)S(1)}, bf16[256,1536]{1,0:T(8,128)(2,1)S(1)}, u32[]{:S(2)}, u32[]{:S(2)}) collective-permute-start(bf16[256,1536]{1,0:T(8,128)(2,1)S(1)} %bitcast.12), channel_id=1, source_target_pairs={{0,63},{1,0},{2,1},{3,2},{4,3},{5,4},{6,5},{7,6},{8,7},{9,8},{10,9... | collective-permute-start | bytes 2359304 | tf_op jit(solution)/shard_map/ppermute | solution.py:24
  21.9 6.9 %all-to-all-done = bf16[8,16,1536]{2,1,0:T(8,128)(2,1)S(1)} async-done(((bf16[8,16,1536]{2,1,0:T(8,128)(2,1)}), bf16[8,16,1536]{2,1,0:T(8,128)(2,1)S(1)}, u32[]{:S(2)}, u32[]{:S(2)}) %all-to-all-start) | async-done | bytes 393248 | tf_op jit(solution)/shard_map/all_to_all | solution.py:40
  28.8 3.0 %collective-permute-start.9 = (bf16[128,1536]{1,0:T(8,128)(2,1)S(1)}, bf16[128,1536]{1,0:T(8,128)(2,1)S(1)}, u32[]{:S(2)}, u32[]{:S(2)}) collective-permute-start(bf16[128,1536]{1,0:T(8,128)(2,1)S(1)} %bitcast.14), channel_id=1, source_target_pairs={{0,32},{1,33},{2,34},{3,35},{4,36},{5,37},{6,38},{7,39},{8,40},{9,... | collective-permute-start | bytes 1179656 | tf_op jit(solution)/shard_map/ppermute | solution.py:48
  31.8 9.1 %collective-permute-done.1.refs_4_ = bf16[256,1536]{1,0:T(8,128)(2,1)S(1)} collective-permute-done((bf16[256,1536]{1,0:T(8,128)(2,1)S(1)}, bf16[256,1536]{1,0:T(8,128)(2,1)S(1)}, u32[]{:S(2)}, u32[]{:S(2)}) %collective-permute-start.1) | collective-permute-done | bytes 786464 | tf_op jit(solution)/shard_map/ppermute | solution.py:24
  40.9 6.4 %collective-permute-done.refs_2_ = bf16[256,1536]{1,0:T(8,128)(2,1)S(1)} collective-permute-done((bf16[256,1536]{1,0:T(8,128)(2,1)S(1)}, bf16[256,1536]{1,0:T(8,128)(2,1)S(1)}, u32[]{:S(2)}, u32[]{:S(2)}) %collective-permute-start) | collective-permute-done | bytes 786464 | tf_op jit(solution)/shard_map/ppermute | solution.py:24
  49.4 6.5 %collective-permute-start.11 = (bf16[256,1536]{1,0:T(8,128)(2,1)S(1)}, bf16[256,1536]{1,0:T(8,128)(2,1)S(1)}, u32[]{:S(2)}, u32[]{:S(2)}) collective-permute-start(bf16[256,1536]{1,0:T(8,128)(2,1)S(1)} %pad_maximum_fusion.refs_11_), channel_id=1, source_target_pairs={{0,24},{1,25},{2,26},{3,27},{4,28},{5,29},{6,30},{7,31},{8,0},{9,1... | collective-permute-start | bytes 2359304 | tf_op jit(solution)/shard_map/ppermute | solution.py:48
  55.9 1.4 collective-permute-start.14
  57.3 8.0 %collective-permute-done.3.refs_9_ = bf16[256,1536]{1,0:T(8,128)(2,1)} collective-permute-done((bf16[256,1536]{1,0:T(8,128)(2,1)}, bf16[256,1536]{1,0:T(8,128)(2,1)}, u32[]{:S(2)}, u32[]{:S(2)}) %collective-permute-start.3) | collective-permute-done | bytes 786464 | tf_op jit(solution)/shard_map/ppermute | solution.py:24
  65.4 7.5 %collective-permute-done.2.refs_7_ = bf16[256,1536]{1,0:T(8,128)(2,1)} collective-permute-done((bf16[256,1536]{1,0:T(8,128)(2,1)}, bf16[256,1536]{1,0:T(8,128)(2,1)}, u32[]{:S(2)}, u32[]{:S(2)}) %collective-permute-start.2) | collective-permute-done | bytes 786464 | tf_op jit(solution)/shard_map/ppermute | solution.py:24
  72.9 7.7 %collective-permute-start.5 = (bf16[256,1536]{1,0:T(8,128)(2,1)S(1)}, bf16[256,1536]{1,0:T(8,128)(2,1)S(1)}, u32[]{:S(2)}, u32[]{:S(2)}) collective-permute-start(bf16[256,1536]{1,0:T(8,128)(2,1)S(1)} %copy-done.5), channel_id=1, source_target_pairs={{0,63},{1,0},{2,1},{3,2},{4,3},{5,4},{6,5},{7,6},{8,7},{9,8},{10,9... | collective-permute-start | bytes 2359304 | tf_op jit(solution)/shard_map/ppermute | solution.py:24
  80.7 1.3 collective-permute-start.16
  81.9 24.4 %collective-permute-done.10.refs_12_ = bf16[256,1536]{1,0:T(8,128)(2,1)S(1)} collective-permute-done((bf16[256,1536]{1,0:T(8,128)(2,1)S(1)}, bf16[256,1536]{1,0:T(8,128)(2,1)S(1)}, u32[]{:S(2)}, u32[]{:S(2)}) %collective-permute-start.10) | collective-permute-done | bytes 786464 | tf_op jit(solution)/shard_map/ppermute | solution.py:48
  108.7 9.8 %collective-permute-done.13.refs_15_ = bf16[128,1536]{1,0:T(8,128)(2,1)S(1)} collective-permute-done((bf16[128,1536]{1,0:T(8,128)(2,1)S(1)}, bf16[128,1536]{1,0:T(8,128)(2,1)S(1)}, u32[]{:S(2)}, u32[]{:S(2)}) %collective-permute-start.13) | collective-permute-done | bytes 393248 | tf_op jit(solution)/shard_map/ppermute | solution.py:48
  118.6 1.4 collective-permute-start.7
  120.0 6.2 %collective-permute-done.12.refs_14_ = bf16[128,1536]{1,0:T(8,128)(2,1)} collective-permute-done((bf16[128,1536]{1,0:T(8,128)(2,1)S(1)}, bf16[128,1536]{1,0:T(8,128)(2,1)}, u32[]{:S(2)}, u32[]{:S(2)}) %collective-permute-start.12) | collective-permute-done | bytes 393248 | tf_op jit(solution)/shard_map/ppermute | solution.py:48
  126.1 1.3 collective-permute-start.18
  128.4 1.5 collective-permute-start.17
  132.9 1.9 %collective-permute-done.6.refs_6_ = bf16[256,1536]{1,0:T(8,128)(2,1)S(1)} collective-permute-done((bf16[256,1536]{1,0:T(8,128)(2,1)}, bf16[256,1536]{1,0:T(8,128)(2,1)S(1)}, u32[]{:S(2)}, u32[]{:S(2)}) %collective-permute-start.6) | collective-permute-done | bytes 786464 | tf_op jit(solution)/shard_map/ppermute | solution.py:24
  134.9 3.0 %collective-permute-done.7.refs_10_ = bf16[256,1536]{1,0:T(8,128)(2,1)} collective-permute-done((bf16[256,1536]{1,0:T(8,128)(2,1)}, bf16[256,1536]{1,0:T(8,128)(2,1)}, u32[]{:S(2)}, u32[]{:S(2)}) %collective-permute-start.7) | collective-permute-done | bytes 786464 | tf_op jit(solution)/shard_map/ppermute | solution.py:24
  137.9 23.5 %attention.1 = bf16[256,1536]{1,0:T(8,128)(2,1)} custom-call(s32[16]{0:T(128)} %reshape.51.lists_ref, s32[1]{0:T(128)} %bitcast.polar_ref, bf16[256,1536]{1,0:T(8,128)(2,1)} %bitcast.16, bf16[256,1536]{1,0:T(8,128)(2,1)} %copy-done.8, bf16[256,1536]{1,0:T(8,128)(2,1)} %copy-done.6, bf16[256,1536]{1,0:T(8,128)(2,1)} %bitcast.11, bf16[256,1536]{1,0:T(8,128)(2,1)} %copy-done.4, ...), custom_call_target="tpu_custom_call" | custom-call | flops 3221225472 | bytes 11796480 | tf_op jit(solution)/shard_map/attention/pallas_call | solution.py:113
  (60 shorter events, 9.8 us)
Async XLA Ops:
  2.5 3.2 %collective-permute-start.8 = (bf16[16,1536]{1,0:T(8,128)(2,1)S(1)}, bf16[16,1536]{1,0:T(8,128)(2,1)S(1)}, u32[]{:S(2)}, u32[]{:S(2)}) collective-permute-start(bf16[16,1536]{1,0:T(8,128)(2,1)S(1)} %gather_fusion.1), channel_id=1, source_target_pairs={{0,64},{1,65},{2,66},{3,67},{4,68},{5,69},{6,70},{7,71},{8,72},{9,... | collective-permute-start | bytes 147464 | tf_op jit(solution)/shard_map/ppermute | solution.py:35
  6.5 22.3 %all-to-all-start = ((bf16[8,16,1536]{2,1,0:T(8,128)(2,1)}), bf16[8,16,1536]{2,1,0:T(8,128)(2,1)S(1)}, u32[]{:S(2)}, u32[]{:S(2)}) async-start(bf16[8,16,1536]{2,1,0:T(8,128)(2,1)} %broadcast_in_dim.2), calls=%async_computation | async-start | bytes 786432 | tf_op jit(solution)/shard_map/all_to_all | solution.py:40
  13.7 27.2 %collective-permute-start.1 = (bf16[256,1536]{1,0:T(8,128)(2,1)S(1)}, bf16[256,1536]{1,0:T(8,128)(2,1)S(1)}, u32[]{:S(2)}, u32[]{:S(2)}) collective-permute-start(bf16[256,1536]{1,0:T(8,128)(2,1)S(1)} %bitcast.12), channel_id=1, source_target_pairs={{0,63},{1,0},{2,1},{3,2},{4,3},{5,4},{6,5},{7,6},{8,7},{9,8},{10,9... | collective-permute-start | bytes 2359304 | tf_op jit(solution)/shard_map/ppermute | solution.py:24
  21.9 25.4 %collective-permute-start = (bf16[256,1536]{1,0:T(8,128)(2,1)S(1)}, bf16[256,1536]{1,0:T(8,128)(2,1)S(1)}, u32[]{:S(2)}, u32[]{:S(2)}) collective-permute-start(bf16[256,1536]{1,0:T(8,128)(2,1)S(1)} %bitcast.13), channel_id=1, source_target_pairs={{0,1},{1,2},{2,3},{3,4},{4,5},{5,6},{6,7},{7,8},{8,9},{9,10},{10,1... | collective-permute-start | bytes 2359304 | tf_op jit(solution)/shard_map/ppermute | solution.py:24
  28.8 20.5 %collective-permute-start.9 = (bf16[128,1536]{1,0:T(8,128)(2,1)S(1)}, bf16[128,1536]{1,0:T(8,128)(2,1)S(1)}, u32[]{:S(2)}, u32[]{:S(2)}) collective-permute-start(bf16[128,1536]{1,0:T(8,128)(2,1)S(1)} %bitcast.14), channel_id=1, source_target_pairs={{0,32},{1,33},{2,34},{3,35},{4,36},{5,37},{6,38},{7,39},{8,40},{9,... | collective-permute-start | bytes 1179656 | tf_op jit(solution)/shard_map/ppermute | solution.py:48
  47.3 18.1 %collective-permute-start.3 = (bf16[256,1536]{1,0:T(8,128)(2,1)}, bf16[256,1536]{1,0:T(8,128)(2,1)}, u32[]{:S(2)}, u32[]{:S(2)}) collective-permute-start(bf16[256,1536]{1,0:T(8,128)(2,1)} %bitcast.3.refs_8_), channel_id=1, source_target_pairs={{0,63},{1,0},{2,1},{3,2},{4,3},{5,4},{6,5},{7,6},{8,7},{9,8},{10,9... | collective-permute-start | bytes 2359304 | tf_op jit(solution)/shard_map/ppermute | solution.py:24
  48.5 24.4 %collective-permute-start.2 = (bf16[256,1536]{1,0:T(8,128)(2,1)}, bf16[256,1536]{1,0:T(8,128)(2,1)}, u32[]{:S(2)}, u32[]{:S(2)}) collective-permute-start(bf16[256,1536]{1,0:T(8,128)(2,1)} %bitcast.3.refs_8_), channel_id=1, source_target_pairs={{0,1},{1,2},{2,3},{3,4},{4,5},{5,6},{6,7},{7,8},{8,9},{9,10},{10,1... | collective-permute-start | bytes 2359304 | tf_op jit(solution)/shard_map/ppermute | solution.py:24
  49.3 23.6 %copy-start.5 = (bf16[256,1536]{1,0:T(8,128)(2,1)S(1)}, bf16[256,1536]{1,0:T(8,128)(2,1)}, u32[]{:S(2)}) copy-start(bf16[256,1536]{1,0:T(8,128)(2,1)} %copy-done.4) | copy-start | bytes 2359300
  49.4 57.1 %copy-start = (bf16[256,1536]{1,0:T(8,128)(2,1)}, bf16[256,1536]{1,0:T(8,128)(2,1)S(1)}, u32[]{:S(2)}) copy-start(bf16[256,1536]{1,0:T(8,128)(2,1)S(1)} %pad_maximum_fusion.refs_11_) | copy-start | bytes 2359300
  49.4 31.3 %collective-permute-start.11 = (bf16[256,1536]{1,0:T(8,128)(2,1)S(1)}, bf16[256,1536]{1,0:T(8,128)(2,1)S(1)}, u32[]{:S(2)}, u32[]{:S(2)}) collective-permute-start(bf16[256,1536]{1,0:T(8,128)(2,1)S(1)} %pad_maximum_fusion.refs_11_), channel_id=1, source_target_pairs={{0,24},{1,25},{2,26},{3,27},{4,28},{5,29},{6,30},{7,31},{8,0},{9,1... | collective-permute-start | bytes 2359304 | tf_op jit(solution)/shard_map/ppermute | solution.py:48
  55.9 50.5 %collective-permute-start.10 = (bf16[256,1536]{1,0:T(8,128)(2,1)S(1)}, bf16[256,1536]{1,0:T(8,128)(2,1)S(1)}, u32[]{:S(2)}, u32[]{:S(2)}) collective-permute-start(bf16[256,1536]{1,0:T(8,128)(2,1)S(1)} %pad_maximum_fusion.refs_11_), channel_id=1, source_target_pairs={{0,8},{1,9},{2,10},{3,11},{4,12},{5,13},{6,14},{7,15},{8,16},{9,17... | collective-permute-start | bytes 2359304 | tf_op jit(solution)/shard_map/ppermute | solution.py:48
  55.9 74.4 %copy-start.15 = (s32[2,1,8]{2,1,0:T(1,128)S(1)}, s32[2,1,8]{2,1,0:T(1,128)}, u32[]{:S(2)}) copy-start(s32[2,1,8]{2,1,0:T(1,128)} %param.8) | copy-start | bytes 196
  55.9 52.7 %collective-permute-start.14 = (bf16[256,1536]{1,0:T(8,128)(2,1)S(1)}, bf16[256,1536]{1,0:T(8,128)(2,1)S(1)}, u32[]{:S(2)}, u32[]{:S(2)}) collective-permute-start(bf16[256,1536]{1,0:T(8,128)(2,1)S(1)} %pad_maximum_fusion.refs_11_), channel_id=1, source_target_pairs={{64,0},{65,1},{66,2},{67,3},{68,4},{69,5},{70,6},{71,7},{72,8},{73... | collective-permute-start | bytes 2359304 | tf_op jit(solution)/shard_map/ppermute | solution.py:35
  72.9 33.7 %collective-permute-start.4 = (bf16[256,1536]{1,0:T(8,128)(2,1)}, bf16[256,1536]{1,0:T(8,128)(2,1)S(1)}, u32[]{:S(2)}, u32[]{:S(2)}) collective-permute-start(bf16[256,1536]{1,0:T(8,128)(2,1)} %copy-done.6), channel_id=1, source_target_pairs={{0,1},{1,2},{2,3},{3,4},{4,5},{5,6},{6,7},{7,8},{8,9},{9,10},{10,1... | collective-permute-start | bytes 2359304 | tf_op jit(solution)/shard_map/ppermute | solution.py:24
  72.9 33.8 %collective-permute-start.5 = (bf16[256,1536]{1,0:T(8,128)(2,1)S(1)}, bf16[256,1536]{1,0:T(8,128)(2,1)S(1)}, u32[]{:S(2)}, u32[]{:S(2)}) collective-permute-start(bf16[256,1536]{1,0:T(8,128)(2,1)S(1)} %copy-done.5), channel_id=1, source_target_pairs={{0,63},{1,0},{2,1},{3,2},{4,3},{5,4},{6,5},{7,6},{8,7},{9,8},{10,9... | collective-permute-start | bytes 2359304 | tf_op jit(solution)/shard_map/ppermute | solution.py:24
  80.7 25.8 %copy-start.1 = (bf16[256,1536]{1,0:T(8,128)(2,1)}, bf16[256,1536]{1,0:T(8,128)(2,1)S(1)}, u32[]{:S(2)}) copy-start(bf16[256,1536]{1,0:T(8,128)(2,1)S(1)} %collective-permute-done.11.refs_13_) | copy-start | bytes 2359300
  80.7 46.8 %collective-permute-start.16 = (bf16[256,1536]{1,0:T(8,128)(2,1)S(1)}, bf16[256,1536]{1,0:T(8,128)(2,1)S(1)}, u32[]{:S(2)}, u32[]{:S(2)}) collective-permute-start(bf16[256,1536]{1,0:T(8,128)(2,1)S(1)} %collective-permute-done.11.refs_13_), channel_id=1, source_target_pairs={{64,0},{65,1},{66,2},{67,3},{68,4},{69,5},{70,6},{71,7},{72,8},{73... | collective-permute-start | bytes 2359304 | tf_op jit(solution)/shard_map/ppermute | solution.py:35
  106.5 12.1 %collective-permute-start.13 = (bf16[128,1536]{1,0:T(8,128)(2,1)S(1)}, bf16[128,1536]{1,0:T(8,128)(2,1)S(1)}, u32[]{:S(2)}, u32[]{:S(2)}) collective-permute-start(bf16[128,1536]{1,0:T(8,128)(2,1)S(1)} %get-tuple-element.27), channel_id=1, source_target_pairs={{0,24},{1,25},{2,26},{3,27},{4,28},{5,29},{6,30},{7,15},{8,0},{9,1... | collective-permute-start | bytes 1179656 | tf_op jit(solution)/shard_map/ppermute | solution.py:48
  106.6 19.5 %collective-permute-start.12 = (bf16[128,1536]{1,0:T(8,128)(2,1)S(1)}, bf16[128,1536]{1,0:T(8,128)(2,1)}, u32[]{:S(2)}, u32[]{:S(2)}) collective-permute-start(bf16[128,1536]{1,0:T(8,128)(2,1)S(1)} %get-tuple-element.28), channel_id=1, source_target_pairs={{0,24},{1,9},{2,10},{3,11},{4,12},{5,13},{6,14},{7,15},{8,0},{9,17... | collective-permute-start | bytes 1179656 | tf_op jit(solution)/shard_map/ppermute | solution.py:48
  107.3 25.6 %collective-permute-start.15 = (bf16[256,1536]{1,0:T(8,128)(2,1)S(1)}, bf16[256,1536]{1,0:T(8,128)(2,1)S(1)}, u32[]{:S(2)}, u32[]{:S(2)}) collective-permute-start(bf16[256,1536]{1,0:T(8,128)(2,1)S(1)} %collective-permute-done.10.refs_12_), channel_id=1, source_target_pairs={{64,0},{65,1},{66,2},{67,3},{68,4},{69,5},{70,6},{71,7},{72,8},{73... | collective-permute-start | bytes 2359304 | tf_op jit(solution)/shard_map/ppermute | solution.py:35
  108.6 26.2 %collective-permute-start.6 = (bf16[256,1536]{1,0:T(8,128)(2,1)}, bf16[256,1536]{1,0:T(8,128)(2,1)S(1)}, u32[]{:S(2)}, u32[]{:S(2)}) collective-permute-start(bf16[256,1536]{1,0:T(8,128)(2,1)} %collective-permute-done.2.refs_7_), channel_id=1, source_target_pairs={{0,1},{1,2},{2,3},{3,4},{4,5},{5,6},{6,7},{7,8},{8,9},{9,10},{10,1... | collective-permute-start | bytes 2359304 | tf_op jit(solution)/shard_map/ppermute | solution.py:24
  118.6 19.3 %collective-permute-start.7 = (bf16[256,1536]{1,0:T(8,128)(2,1)}, bf16[256,1536]{1,0:T(8,128)(2,1)}, u32[]{:S(2)}, u32[]{:S(2)}) collective-permute-start(bf16[256,1536]{1,0:T(8,128)(2,1)} %collective-permute-done.3.refs_9_), channel_id=1, source_target_pairs={{0,63},{1,0},{2,1},{3,2},{4,3},{5,4},{6,5},{7,6},{8,7},{9,8},{10,9... | collective-permute-start | bytes 2359304 | tf_op jit(solution)/shard_map/ppermute | solution.py:24
  126.1 5.5 %collective-permute-start.18 = (bf16[128,1536]{1,0:T(8,128)(2,1)S(1)}, bf16[128,1536]{1,0:T(8,128)(2,1)}, u32[]{:S(2)}, u32[]{:S(2)}) collective-permute-start(bf16[128,1536]{1,0:T(8,128)(2,1)S(1)} %collective-permute-done.13.refs_15_), channel_id=1, source_target_pairs={{64,0},{65,1},{66,2},{67,3},{68,4},{69,5},{70,6},{71,7},{72,8},{73... | collective-permute-start | bytes 1179656 | tf_op jit(solution)/shard_map/ppermute | solution.py:35
  128.4 4.6 %collective-permute-start.17 = (bf16[128,1536]{1,0:T(8,128)(2,1)}, bf16[128,1536]{1,0:T(8,128)(2,1)S(1)}, u32[]{:S(2)}, u32[]{:S(2)}) collective-permute-start(bf16[128,1536]{1,0:T(8,128)(2,1)} %collective-permute-done.12.refs_14_), channel_id=1, source_target_pairs={{64,0},{65,1},{66,2},{67,3},{68,4},{69,5},{70,6},{71,7},{72,8},{73... | collective-permute-start | bytes 1179656 | tf_op jit(solution)/shard_map/ppermute | solution.py:35
  (12 other events, 112.3 us)

commit v3 on v2

v3 whole, which is shorter than its diff:
```python
import jax
import jax.numpy as jnp
from jax import lax
from jax.experimental import pallas as pl
from jax.experimental.pallas import tpu as pltpu
from jax.sharding import PartitionSpec as P

H = 24
HD = 64
BS = 128
TILE = 256
D = 1536
PAIR = 2 * HD
NB = 8
CAND = 10
N_LON = 64
LOG2E = 1.4426950408889634
STEP = 2 * PAIR
TOTALS = 32
POLAR_LATS = (0, 3)
POLAR_LATS = (0, 3)


def step_lon(value, steps):
    pairs = [(source, (source + steps) % N_LON) for source in range(N_LON)]
    return lax.ppermute(value, "lon", pairs)


def core_move(value, toward_polar):
    pairs = [
        (side, home) if toward_polar else (home, side)
        for polar_lat, side_lat in ((0, 1), (3, 2))
        for home, side in (
            (polar_lat * N_LON + lon, side_lat * N_LON + lon) for lon in range(N_LON)
        )
    ]
    return lax.ppermute(value, ("lat", "lon"), pairs)


def share(value, groups):
    copies = jnp.broadcast_to(value, (8,) + value.shape)
    got = lax.all_to_all(copies, "lon", 0, 0, axis_index_groups=groups)
    return got.reshape((-1,) + value.shape[1:])


Z_LINES = [[first + z for z in range(8)] for first in range(0, N_LON, 8)]


def move(value, target_of):
    return lax.ppermute(value, "lon", [(lon, target_of(lon)) for lon in range(N_LON)])


def polar_move(value, target_of):
    pairs = [
        (lat * N_LON + lon, lat * N_LON + target_of(lon))
        for lat in POLAR_LATS
        for lon in range(N_LON)
    ]
    return lax.ppermute(value, ("lat", "lon"), pairs)


def along_y(steps):
    return lambda lon: (lon & ~24) | ((lon + 8 * steps) & 24)


def across_x(lon):
    return lon ^ 32


def low_lanes():
    return lax.broadcasted_iota(jnp.int32, (BS, PAIR), 1) < HD


def attend(q, keys, values, low):
    q = q * jnp.bfloat16(HD ** -0.5)
    zero = jnp.zeros_like(q)
    stacked = jnp.concatenate([jnp.where(low, q, zero), jnp.where(low, zero, q)], 0)
    keys, values = jnp.concatenate(keys, 0), jnp.concatenate(values, 0)
    scores = lax.dot_general(
        stacked, keys, (((1,), (1,)), ((), ())), preferred_element_type=jnp.float32
    )
    row_max = jnp.max(scores, axis=1, keepdims=True)
    weights = jnp.exp2((scores - row_max) * LOG2E).astype(jnp.bfloat16)
    wide = jnp.concatenate([values, jnp.ones_like(values)], 1)
    mixed = jnp.dot(weights, wide, preferred_element_type=jnp.float32)
    acc = jnp.where(low, mixed[:BS, :PAIR], mixed[BS:, :PAIR])
    total = jnp.where(low, mixed[:BS, PAIR:], mixed[BS:, PAIR:])
    return acc, total, row_max


def pack(stat, head, total, row_max):
    lane = lax.broadcasted_iota(jnp.int32, (BS, PAIR), 1)
    stat = jnp.where(lane == head, row_max[:BS], stat)
    stat = jnp.where(lane == head + 1, row_max[BS:], stat)
    stat = jnp.where(lane == head + TOTALS, total[:, :1], stat)
    return jnp.where(lane == head + 1 + TOTALS, total[:, HD:HD + 1], stat)


def band_kernel(polar_ref, q_own, q_other, *refs):
    band_k, band_v = refs[0:5], refs[5:10]
    outs, stats = refs[10:12], refs[12:14]
    at = pl.program_id(0)

    @pl.when(polar_ref[0] == 1)
    def _():
        low = low_lanes()
        for q_ref, out_ref, stat_ref in zip((q_own, q_other), outs, stats):
            for block in range(2):
                rows = pl.ds(block * BS, BS)
                stat = jnp.where(at == 0, 0.0, stat_ref[rows, :])
                for part in range(STEP // PAIR):
                    lanes = slice(part * PAIR, (part + 1) * PAIR)
                    acc, total, row_max = attend(
                        q_ref[rows, lanes],
                        [ref[:, lanes] for ref in band_k],
                        [ref[:, lanes] for ref in band_v],
                        low,
                    )
                    out_ref[rows, lanes] = (acc / total).astype(out_ref.dtype)
                    stat = pack(stat, 2 * (at * (STEP // PAIR) + part), total, row_max)
                stat_ref[rows, :] = stat


def near_kernel(lists_ref, *refs):
    q_ref, k_tiles, v_tiles = refs[0], refs[1:6], refs[6:11]
    out_ref, stat_ref, k_all, v_all = refs[11:]
    at = pl.program_id(0)
    for tile in range(5):
        for block in range(2):
            rows = pl.ds(block * BS, BS)
            k_all[2 * tile + block] = k_tiles[tile][rows, :]
            v_all[2 * tile + block] = v_tiles[tile][rows, :]
    low = low_lanes()
    for block in range(2):
        rows = pl.ds(block * BS, BS)
        stat = jnp.where(at == 0, 0.0, stat_ref[rows, :])
        picks = [lists_ref[block * NB + j] for j in range(NB)]
        for part in range(STEP // PAIR):
            lanes = slice(part * PAIR, (part + 1) * PAIR)
            acc, total, row_max = attend(
                q_ref[rows, lanes],
                [k_all[pick, :, lanes] for pick in picks],
                [v_all[pick, :, lanes] for pick in picks],
                low,
            )
            out_ref[rows, lanes] = acc / total
            stat = pack(stat, 2 * (at * (STEP // PAIR) + part), total, row_max)
        stat_ref[rows, :] = stat


def spread(share, at):
    high = share.astype(jnp.bfloat16)
    rest = share - high.astype(jnp.float32)
    middle = rest.astype(jnp.bfloat16)
    tail = (rest - middle.astype(jnp.float32)).astype(jnp.bfloat16)
    column = lax.broadcasted_iota(jnp.int32, (PAIR, STEP), 0)
    lane = lax.broadcasted_iota(jnp.int32, (PAIR, STEP), 1)
    select = jnp.where(column == at * (STEP // HD) + lane // HD, 1.0, 0.0).astype(jnp.bfloat16)
    pieces = jnp.concatenate([high, middle, tail], 1)
    return jnp.dot(
        pieces, jnp.concatenate([select] * 3, 0), preferred_element_type=jnp.float32
    )


def merge_kernel(polar_ref, near_ref, own_ref, other_ref, *refs):
    stats, out_ref = refs[0:3], refs[3]
    at = pl.program_id(0)

    @pl.when(polar_ref[0] == 1)
    def _():
        heads = lax.broadcasted_iota(jnp.int32, (TILE, PAIR), 1) < D // HD
        stat = [ref[...] for ref in stats]
        top = jnp.maximum(stat[0], jnp.maximum(stat[1], stat[2]))
        masses = [
            jnp.exp2((each - top) * LOG2E) * pltpu.roll(each, PAIR - TOTALS, 1) for each in stat
        ]
        whole = masses[0] + masses[1] + masses[2]
        result = None
        for mass, ref in zip(masses, (near_ref, own_ref, other_ref)):
            share = jnp.where(heads, mass / whole, 0.0)
            part = ref[...].astype(jnp.float32) * spread(share, at)
            result = part if result is None else result + part
        out_ref[...] = result.astype(out_ref.dtype)

    @pl.when(polar_ref[0] == 0)
    def _():
        out_ref[...] = near_ref[...].astype(out_ref.dtype)


COLUMN = pl.BlockSpec((TILE, STEP), lambda p, *_: (0, p))
STAT = pl.BlockSpec((TILE, PAIR), lambda p, *_: (0, 0))
PARAMS = pltpu.CompilerParams(vmem_limit_bytes=60 << 20)


def band_attention(polar, q_own, q_other, band_k, band_v):
    def polar_column(rows):
        return pl.BlockSpec((rows, STEP), lambda p, polar_ref: (0, p * polar_ref[0]))

    return pl.pallas_call(
        band_kernel,
        out_shape=[jax.ShapeDtypeStruct((TILE, D), jnp.bfloat16)] * 2
        + [jax.ShapeDtypeStruct((TILE, PAIR), jnp.float32)] * 2,
        grid_spec=pltpu.PrefetchScalarGridSpec(
            num_scalar_prefetch=1,
            grid=(D // STEP,),
            in_specs=[polar_column(TILE)] * 2
            + [polar_column(part.shape[0]) for part in (*band_k, *band_v)],
            out_specs=[COLUMN] * 2 + [STAT] * 2,
        ),
        compiler_params=PARAMS,
        cost_estimate=pl.CostEstimate(
            flops=6 * 10 ** 10, transcendentals=0, bytes_accessed=TILE * D * 30
        ),
        name="band_attention",
    )(polar, q_own, q_other, *band_k, *band_v)


def near_attention(lists, queries, keys, values):
    return pl.pallas_call(
        near_kernel,
        out_shape=[
            jax.ShapeDtypeStruct((TILE, D), jnp.float32),
            jax.ShapeDtypeStruct((TILE, PAIR), jnp.float32),
        ],
        grid_spec=pltpu.PrefetchScalarGridSpec(
            num_scalar_prefetch=1,
            grid=(D // STEP,),
            in_specs=[COLUMN] * 11,
            out_specs=[COLUMN, STAT],
            scratch_shapes=[pltpu.VMEM((2 * len(keys), BS, STEP), jnp.bfloat16)] * 2,
        ),
        compiler_params=PARAMS,
        name="near_attention",
    )(lists, queries, *keys, *values)


def merge(polar, outs, stats):
    return pl.pallas_call(
        merge_kernel,
        out_shape=jax.ShapeDtypeStruct((TILE, D), jnp.bfloat16),
        grid_spec=pltpu.PrefetchScalarGridSpec(
            num_scalar_prefetch=1,
            grid=(D // STEP,),
            in_specs=[COLUMN] * 3 + [STAT] * 3,
            out_specs=COLUMN,
        ),
        compiler_params=PARAMS,
        name="merge",
    )(polar, *outs, *stats)


def local(queries, key_tokens, value_tokens, block_lists, band_rows):
    q = queries.reshape(TILE, D)
    k = key_tokens.reshape(TILE, D)
    v = value_tokens.reshape(TILE, D)
    lists = block_lists.reshape(2 * NB)
    lat_at = lax.axis_index("lat")
    is_polar = (lat_at == 0) | (lat_at == lax.axis_size("lat") - 1)
    polar = is_polar.astype(jnp.int32).reshape(1)
    fence = lax.optimization_barrier

    picked = jnp.where(is_polar, k[band_rows[0]], core_move(v[band_rows[0]], False))
    k_west, k_east = step_lon(k, 1), step_lon(k, -1)
    k_west, k_east, v_sent = fence((k_west, k_east, v))
    v_west, v_east = step_lon(v_sent, 1), step_lon(v_sent, -1)
    k_west, k_east, v_west, v_east = fence((k_west, k_east, v_west, v_east))
    k_west2, k_east2 = step_lon(k_west, 1), step_lon(k_east, -1)
    v_west, v_east, k_west2, k_east2 = fence((v_west, v_east, k_west2, k_east2))
    v_west2, v_east2 = step_lon(v_west, 1), step_lon(v_east, -1)

    q_other = polar_move(q, across_x)
    line = share(picked, Z_LINES)
    south, north = move(line, along_y(1)), move(line, along_y(-1))
    half = TILE // 4
    z_at = lax.axis_index("lon") & 7
    first = jnp.where(z_at == 0, north[:half], south[:half])
    second = jnp.where(z_at == 7, south[half:], north[half:])
    south2 = move(first, lambda lon: along_y(1 if lon & 7 else -1)(lon))
    north2 = move(second, lambda lon: along_y(1 if lon & 7 == 7 else -1)(lon))
    band = [line, south, north, south2, north2]
    band_v = [core_move(part, True) for part in band]
    own_out, other_out, own_stat, other_stat = band_attention(polar, q, q_other, band, band_v)
    near_out, near_stat = near_attention(
        lists,
        q,
        (k_west2, k_west, k, k_east, k_east2),
        (v_west2, v_west, v, v_east, v_east2),
    )
    other_out, other_stat = polar_move(other_out, across_x), polar_move(other_stat, across_x)
    near_out, other_out, other_stat = fence((near_out, other_out, other_stat))
    out = merge(
        polar, (near_out, own_out, other_out), (near_stat, own_stat, other_stat)
    )
    return out.reshape(queries.shape)


def solution(mesh):
    return jax.shard_map(
        local,
        mesh=mesh,
        in_specs=(
            P("lat", "lon", None),
            P("lat", "lon", None),
            P("lat", "lon", None),
            P("lat", "lon", None),
            P("lat", "lon"),
        ),
        out_specs=P("lat", "lon", None),
        check_vma=False,
    )
```

time: 162 us -> 158 us (0.975); the launches traced: 162 us -> 155 us
  waiting for transfers between devices: 84.6 us -> 51.8 us
  starting transfers between devices: 44.3 us -> 57.7 us
  Pallas kernels: 23.5 us -> 33.8 us
    ppermute x5 -> x4, waiting for transfers between devices: 40.5 us -> 25.8 us  [move(): lax.ppermute(value, 'lon', [(lon, target_of(lon)) for lon in range(N_LON)])]
    ppermute x8, starting transfers between devices: 19.4 us -> 33.4 us  [step_lon(): return lax.ppermute(value, 'lon', pairs)]
    pallas_call x1 -> x3, Pallas kernels: 23.5 us -> 33.8 us  [the longest x1 14.4 us: near_attention(): pl.pallas_call(near_kernel, out_shape=[jax.ShapeDtypeStruct((TILE, D), jn...]
    ppermute x8, waiting for transfers between devices: 35.9 us -> 26 us  [step_lon(): return lax.ppermute(value, 'lon', pairs)]
    ppermute x0 -> x3, starting transfers between devices: none -> 9.75 us  [polar_move(): return lax.ppermute(value, ('lat', 'lon'), pairs)]
    all_to_all x1, waiting for transfers between devices: 6.94 us -> 0.01 us  [share(): got = lax.all_to_all(copies, 'lon', 0, 0, axis_index_groups=groups)]
    ppermute x5 -> x4, starting transfers between devices: 9.72 us -> 3.4 us  [move(): lax.ppermute(value, 'lon', [(lon, target_of(lon)) for lon in range(N_LON)])]
    all_to_all x1, starting transfers between devices: 7.18 us -> 3.45 us  [share(): got = lax.all_to_all(copies, 'lon', 0, 0, axis_index_groups=groups)]
  transfers between devices with their start and end apart: 20 -> 22, of which waited for: 11 -> 6; matrix products, arithmetic and copies ran while one was open for 2% -> 4% of each run, Pallas kernels for 0% -> 18%
where the time goes in v3:
time: 158 us; the launch traced here: 155 us
  starting transfers between devices  57.7 us (37%)
  waiting for transfers between devices  51.8 us (33%)
  Pallas kernels  33.8 us (21%)
  local copies, waits for them, and re-layouts  8.51 us (5%)
  other arithmetic  2.68 us (2%)
    ppermute x8, starting transfers between devices, step_lon(): return lax.ppermute(value, 'lon', pairs)  33.4 us
    ppermute x8, waiting for transfers between devices, step_lon(): return lax.ppermute(value, 'lon', pairs)  26 us
    ppermute x4, waiting for transfers between devices, move(): lax.ppermute(value, 'lon', [(lon, target_of(lon)) for lon in range(N_LON)])  25.8 us
    pallas_call x1, Pallas kernels, near_attention(): pl.pallas_call(near_kernel, out_shape=[jax.ShapeDtypeStruct((TILE, D), jn...  14.4 us
    pallas_call x1, Pallas kernels, band_attention(): pl.pallas_call(band_kernel, out_shape=[jax.ShapeDtypeStruct((TILE, D), jn...  13.3 us
    ppermute x3, starting transfers between devices, polar_move(): return lax.ppermute(value, ('lat', 'lon'), pairs)  9.75 us
    ppermute x6, starting transfers between devices, core_move(): return lax.ppermute(value, ('lat', 'lon'), pairs)  7.72 us
    pallas_call x1, Pallas kernels, merge(): pl.pallas_call(merge_kernel, out_shape=jax.ShapeDtypeStruct((TILE, D), jn...  6.14 us
  transfers between devices with their start and end apart: 22, of which 6 were waited for; matrix products, arithmetic and copies ran while one was open for 4% of the time, Pallas kernels for 18%

profile of v3, /device:TPU:0, one launch (start us, length us, event | category | flops | bytes accessed | tf_op | source)
XLA Modules:
  0.0 154.9 jit_solution(9076407536978343974)
XLA Ops:
  0.8 1.9 %gather_fusion.1 = bf16[16,1536]{1,0:T(8,128)(2,1)S(1)} fusion(bf16[256,1536]{1,0:T(8,128)(2,1)} %bitcast.14, s32[1024]{0:T(1024)S(1)} %pad_clamp_fusion), kind=kCustom, calls=%fused_computation.1 | custom fusion | bytes 98368 | tf_op jit(solution)/shard_map/gather | solution.py:262
  2.7 1.3 collective-permute-start.9
  4.7 8.9 %collective-permute-start.1 = (bf16[256,1536]{1,0:T(8,128)(2,1)}, bf16[256,1536]{1,0:T(8,128)(2,1)S(1)}, u32[]{:S(2)}, u32[]{:S(2)}) collective-permute-start(bf16[256,1536]{1,0:T(8,128)(2,1)} %bitcast.11), channel_id=1, source_target_pairs={{0,63},{1,0},{2,1},{3,2},{4,3},{5,4},{6,5},{7,6},{8,7},{9,8},{10,9... | collective-permute-start | bytes 2359304 | tf_op jit(solution)/shard_map/ppermute | solution.py:26
  13.6 1.9 %gather_fusion = bf16[16,1536]{1,0:T(8,128)(2,1)S(1)} fusion(bf16[256,1536]{1,0:T(8,128)(2,1)} %bitcast.12, s32[1024]{0:T(1024)S(1)} %pad_clamp_fusion), kind=kCustom, calls=%fused_computation | custom fusion | bytes 98368 | tf_op jit(solution)/shard_map/gather | solution.py:262
  16.3 3.5 %all-to-all-start = ((bf16[8,16,1536]{2,1,0:T(8,128)(2,1)}), bf16[8,16,1536]{2,1,0:T(8,128)(2,1)S(1)}, u32[]{:S(2)}, u32[]{:S(2)}) async-start(bf16[8,16,1536]{2,1,0:T(8,128)(2,1)} %broadcast_in_dim.2), calls=%async_computation | async-start | bytes 786432 | tf_op jit(solution)/shard_map/all_to_all | solution.py:42
  19.8 13.8 %collective-permute-done.refs_2_ = bf16[256,1536]{1,0:T(8,128)(2,1)S(1)} collective-permute-done((bf16[256,1536]{1,0:T(8,128)(2,1)}, bf16[256,1536]{1,0:T(8,128)(2,1)S(1)}, u32[]{:S(2)}, u32[]{:S(2)}) %collective-permute-start) | collective-permute-done | bytes 786464 | tf_op jit(solution)/shard_map/ppermute | solution.py:26
  33.6 3.5 %collective-permute-done.1.refs_4_ = bf16[256,1536]{1,0:T(8,128)(2,1)S(1)} collective-permute-done((bf16[256,1536]{1,0:T(8,128)(2,1)}, bf16[256,1536]{1,0:T(8,128)(2,1)S(1)}, u32[]{:S(2)}, u32[]{:S(2)}) %collective-permute-start.1) | collective-permute-done | bytes 786464 | tf_op jit(solution)/shard_map/ppermute | solution.py:26
  37.1 8.2 %collective-permute-start.3 = (bf16[256,1536]{1,0:T(8,128)(2,1)S(1)}, bf16[256,1536]{1,0:T(8,128)(2,1)}, u32[]{:S(2)}, u32[]{:S(2)}) collective-permute-start(bf16[256,1536]{1,0:T(8,128)(2,1)S(1)} %bitcast.17), channel_id=1, source_target_pairs={{0,63},{1,0},{2,1},{3,2},{4,3},{5,4},{6,5},{7,6},{8,7},{9,8},{10,9... | collective-permute-start | bytes 2359304 | tf_op jit(solution)/shard_map/ppermute | solution.py:26
  45.3 3.2 %collective-permute-start.11 = (bf16[128,1536]{1,0:T(8,128)(2,1)S(1)}, bf16[128,1536]{1,0:T(8,128)(2,1)}, u32[]{:S(2)}, u32[]{:S(2)}) collective-permute-start(bf16[128,1536]{1,0:T(8,128)(2,1)S(1)} %bitcast.22), channel_id=1, source_target_pairs={{0,24},{1,25},{2,26},{3,27},{4,28},{5,29},{6,30},{7,31},{8,0},{9,1... | collective-permute-start | bytes 1179656 | tf_op jit(solution)/shard_map/ppermute | solution.py:50
  48.6 2.4 %collective-permute-start.8 = (bf16[256,1536]{1,0:T(8,128)(2,1)S(1)}, bf16[256,1536]{1,0:T(8,128)(2,1)}, u32[]{:S(2)}, u32[]{:S(2)}) collective-permute-start(bf16[256,1536]{1,0:T(8,128)(2,1)S(1)} %bitcast.20), channel_id=1, source_target_pairs={{0,32},{1,33},{2,34},{3,35},{4,36},{5,37},{6,38},{7,39},{8,40},{9,... | collective-permute-start | bytes 2359304 | tf_op jit(solution)/shard_map/ppermute | solution.py:59
  51.0 8.7 %collective-permute-done.2.refs_7_ = bf16[256,1536]{1,0:T(8,128)(2,1)} collective-permute-done((bf16[256,1536]{1,0:T(8,128)(2,1)S(1)}, bf16[256,1536]{1,0:T(8,128)(2,1)}, u32[]{:S(2)}, u32[]{:S(2)}) %collective-permute-start.2) | collective-permute-done | bytes 786464 | tf_op jit(solution)/shard_map/ppermute | solution.py:26
  59.7 7.7 %collective-permute-start.5 = (bf16[256,1536]{1,0:T(8,128)(2,1)S(1)}, bf16[256,1536]{1,0:T(8,128)(2,1)S(1)}, u32[]{:S(2)}, u32[]{:S(2)}) collective-permute-start(bf16[256,1536]{1,0:T(8,128)(2,1)S(1)} %collective-permute-done.1.refs_4_), channel_id=1, source_target_pairs={{0,63},{1,0},{2,1},{3,2},{4,3},{5,4},{6,5},{7,6},{8,7},{9,8},{10,9... | collective-permute-start | bytes 2359304 | tf_op jit(solution)/shard_map/ppermute | solution.py:26
  67.4 17.3 %collective-permute-done.10.refs_1_ = bf16[128,1536]{1,0:T(8,128)(2,1)} collective-permute-done((bf16[128,1536]{1,0:T(8,128)(2,1)S(1)}, bf16[128,1536]{1,0:T(8,128)(2,1)}, u32[]{:S(2)}, u32[]{:S(2)}) %collective-permute-start.10) | collective-permute-done | bytes 393248 | tf_op jit(solution)/shard_map/ppermute | solution.py:50
  86.2 1.3 collective-permute-start.14
  87.5 6.4 %collective-permute-done.12.refs_3_ = bf16[64,1536]{1,0:T(8,128)(2,1)} collective-permute-done((bf16[64,1536]{1,0:T(8,128)(2,1)S(1)}, bf16[64,1536]{1,0:T(8,128)(2,1)}, u32[]{:S(2)}, u32[]{:S(2)}) %collective-permute-start.12) | collective-permute-done | bytes 196640 | tf_op jit(solution)/shard_map/ppermute | solution.py:50
  94.0 1.3 collective-permute-start.15
  95.2 2.0 %collective-permute-done.13.refs_4_ = bf16[64,1536]{1,0:T(8,128)(2,1)} collective-permute-done((bf16[64,1536]{1,0:T(8,128)(2,1)S(1)}, bf16[64,1536]{1,0:T(8,128)(2,1)}, u32[]{:S(2)}, u32[]{:S(2)}) %collective-permute-start.13) | collective-permute-done | bytes 196640 | tf_op jit(solution)/shard_map/ppermute | solution.py:50
  98.5 1.3 collective-permute-start.17
  102.1 7.7 %collective-permute-start.7 = (bf16[256,1536]{1,0:T(8,128)(2,1)}, bf16[256,1536]{1,0:T(8,128)(2,1)}, u32[]{:S(2)}, u32[]{:S(2)}) collective-permute-start(bf16[256,1536]{1,0:T(8,128)(2,1)} %collective-permute-done.3.refs_9_), channel_id=1, source_target_pairs={{0,63},{1,0},{2,1},{3,2},{4,3},{5,4},{6,5},{7,6},{8,7},{9,8},{10,9... | collective-permute-start | bytes 2359304 | tf_op jit(solution)/shard_map/ppermute | solution.py:26
  109.9 13.3 %band_attention.1 = (bf16[256,1536]{1,0:T(8,128)(2,1)}, bf16[256,1536]{1,0:T(8,128)(2,1)}, f32[256,128]{1,0:T(8,128)}, f32[256,128]{1,0:T(8,128)}) custom-call(s32[1]{0:T(128)} %bitcast.polar_ref, bf16[256,1536]{1,0:T(8,128)(2,1)} %bitcast.18, bf16[256,1536]{1,0:T(8,128)(2,1)} %collective-permute-done.8.q_other, bf16[128,1536]{1,0:T(8,128)(2,1)} %bitcast.24, ...), custom_call_target="tpu_custom_call" | custom-call | flops 60000002048 | bytes 11796480 | tf_op jit(solution)/shard_map/band_attention/pallas_call | solution.py:199
  123.2 2.4 %collective-permute-start.19 = (bf16[256,1536]{1,0:T(8,128)(2,1)}, bf16[256,1536]{1,0:T(8,128)(2,1)S(1)}, u32[]{:S(2)}, u32[]{:S(2)}) collective-permute-start(bf16[256,1536]{1,0:T(8,128)(2,1)} %get-tuple-element.37), channel_id=1, source_target_pairs={{0,32},{1,33},{2,34},{3,35},{4,36},{5,37},{6,38},{7,39},{8,40},{9,... | collective-permute-start | bytes 2359304 | tf_op jit(solution)/shard_map/ppermute | solution.py:59
  125.6 5.0 %collective-permute-start.20 = (f32[256,128]{1,0:T(8,128)}, f32[256,128]{1,0:T(8,128)S(1)}, u32[]{:S(2)}, u32[]{:S(2)}) collective-permute-start(f32[256,128]{1,0:T(8,128)} %get-tuple-element.38), channel_id=1, source_target_pairs={{0,32},{1,33},{2,34},{3,35},{4,36},{5,37},{6,38},{7,39},{8,40},{9,... | collective-permute-start | bytes 393224 | tf_op jit(solution)/shard_map/ppermute | solution.py:59
  133.4 14.4 %near_attention.1 = (f32[256,1536]{1,0:T(8,128)}, f32[256,128]{1,0:T(8,128)}) custom-call(s32[16]{0:T(128)} %reshape.53.lists_ref, bf16[256,1536]{1,0:T(8,128)(2,1)} %bitcast.19, bf16[256,1536]{1,0:T(8,128)(2,1)} %copy-done.4, bf16[256,1536]{1,0:T(8,128)(2,1)} %copy-done.2, bf16[256,1536]{1,0:T(8,128)(2,1)} %bitcast.13, bf16[256,1536]{1,0:T(8,128)(2,1)} %copy-done.3, ...), custom_call_target="tpu_custom_call" | custom-call | tf_op jit(solution)/shard_map/near_attention/pallas_call | solution.py:219
  148.7 6.1 %merge.1 = bf16[256,1536]{1,0:T(8,128)(2,1)} custom-call(s32[1]{0:T(128)} %bitcast.polar_ref, f32[256,1536]{1,0:T(8,128)} %get-tuple-element.39.near_ref, bf16[256,1536]{1,0:T(8,128)(2,1)} %get-tuple-element.40.own_ref, bf16[256,1536]{1,0:T(8,128)(2,1)} %copy-done.7, f32[256,128]{1,0:T(8,128)} %get-tuple-element.42.refs_0_, ...), custom_call_target="tpu_custom_call" | custom-call | tf_op jit(solution)/shard_map/merge/pallas_call | solution.py:238
  (55 shorter events, 11.0 us)
Async XLA Ops:
  2.7 12.9 %collective-permute-start.9 = (bf16[16,1536]{1,0:T(8,128)(2,1)S(1)}, bf16[16,1536]{1,0:T(8,128)(2,1)S(1)}, u32[]{:S(2)}, u32[]{:S(2)}) collective-permute-start(bf16[16,1536]{1,0:T(8,128)(2,1)S(1)} %gather_fusion.1), channel_id=1, source_target_pairs={{0,64},{1,65},{2,66},{3,67},{4,68},{5,69},{6,70},{7,71},{8,72},{9,... | collective-permute-start | bytes 147464 | tf_op jit(solution)/shard_map/ppermute | solution.py:37
  4.0 29.6 %collective-permute-start = (bf16[256,1536]{1,0:T(8,128)(2,1)}, bf16[256,1536]{1,0:T(8,128)(2,1)S(1)}, u32[]{:S(2)}, u32[]{:S(2)}) collective-permute-start(bf16[256,1536]{1,0:T(8,128)(2,1)} %bitcast.10), channel_id=1, source_target_pairs={{0,1},{1,2},{2,3},{3,4},{4,5},{5,6},{6,7},{7,8},{8,9},{9,10},{10,1... | collective-permute-start | bytes 2359304 | tf_op jit(solution)/shard_map/ppermute | solution.py:26
  4.7 32.5 %collective-permute-start.1 = (bf16[256,1536]{1,0:T(8,128)(2,1)}, bf16[256,1536]{1,0:T(8,128)(2,1)S(1)}, u32[]{:S(2)}, u32[]{:S(2)}) collective-permute-start(bf16[256,1536]{1,0:T(8,128)(2,1)} %bitcast.11), channel_id=1, source_target_pairs={{0,63},{1,0},{2,1},{3,2},{4,3},{5,4},{6,5},{7,6},{8,7},{9,8},{10,9... | collective-permute-start | bytes 2359304 | tf_op jit(solution)/shard_map/ppermute | solution.py:26
  16.3 29.0 %all-to-all-start = ((bf16[8,16,1536]{2,1,0:T(8,128)(2,1)}), bf16[8,16,1536]{2,1,0:T(8,128)(2,1)S(1)}, u32[]{:S(2)}, u32[]{:S(2)}) async-start(bf16[8,16,1536]{2,1,0:T(8,128)(2,1)} %broadcast_in_dim.2), calls=%async_computation | async-start | bytes 786432 | tf_op jit(solution)/shard_map/all_to_all | solution.py:42
  33.6 89.6 %copy-start.2 = (bf16[256,1536]{1,0:T(8,128)(2,1)}, bf16[256,1536]{1,0:T(8,128)(2,1)S(1)}, u32[]{:S(2)}) copy-start(bf16[256,1536]{1,0:T(8,128)(2,1)S(1)} %collective-permute-done.refs_2_) | copy-start | bytes 2359300
  37.1 86.1 %copy-start.3 = (bf16[256,1536]{1,0:T(8,128)(2,1)}, bf16[256,1536]{1,0:T(8,128)(2,1)S(1)}, u32[]{:S(2)}) copy-start(bf16[256,1536]{1,0:T(8,128)(2,1)S(1)} %collective-permute-done.1.refs_4_) | copy-start | bytes 2359300
  37.1 22.5 %collective-permute-start.2 = (bf16[256,1536]{1,0:T(8,128)(2,1)S(1)}, bf16[256,1536]{1,0:T(8,128)(2,1)}, u32[]{:S(2)}, u32[]{:S(2)}) collective-permute-start(bf16[256,1536]{1,0:T(8,128)(2,1)S(1)} %bitcast.16), channel_id=1, source_target_pairs={{0,1},{1,2},{2,3},{3,4},{4,5},{5,6},{6,7},{7,8},{8,9},{9,10},{10,1... | collective-permute-start | bytes 2359304 | tf_op jit(solution)/shard_map/ppermute | solution.py:26
  37.1 22.5 %collective-permute-start.3 = (bf16[256,1536]{1,0:T(8,128)(2,1)S(1)}, bf16[256,1536]{1,0:T(8,128)(2,1)}, u32[]{:S(2)}, u32[]{:S(2)}) collective-permute-start(bf16[256,1536]{1,0:T(8,128)(2,1)S(1)} %bitcast.17), channel_id=1, source_target_pairs={{0,63},{1,0},{2,1},{3,2},{4,3},{5,4},{6,5},{7,6},{8,7},{9,8},{10,9... | collective-permute-start | bytes 2359304 | tf_op jit(solution)/shard_map/ppermute | solution.py:26
  45.3 39.4 %collective-permute-start.10 = (bf16[128,1536]{1,0:T(8,128)(2,1)S(1)}, bf16[128,1536]{1,0:T(8,128)(2,1)}, u32[]{:S(2)}, u32[]{:S(2)}) collective-permute-start(bf16[128,1536]{1,0:T(8,128)(2,1)S(1)} %bitcast.21), channel_id=1, source_target_pairs={{0,8},{1,9},{2,10},{3,11},{4,12},{5,13},{6,14},{7,15},{8,16},{9,17... | collective-permute-start | bytes 1179656 | tf_op jit(solution)/shard_map/ppermute | solution.py:50
  45.3 39.4 %collective-permute-start.11 = (bf16[128,1536]{1,0:T(8,128)(2,1)S(1)}, bf16[128,1536]{1,0:T(8,128)(2,1)}, u32[]{:S(2)}, u32[]{:S(2)}) collective-permute-start(bf16[128,1536]{1,0:T(8,128)(2,1)S(1)} %bitcast.22), channel_id=1, source_target_pairs={{0,24},{1,25},{2,26},{3,27},{4,28},{5,29},{6,30},{7,31},{8,0},{9,1... | collective-permute-start | bytes 1179656 | tf_op jit(solution)/shard_map/ppermute | solution.py:50
  48.6 37.6 %collective-permute-start.8 = (bf16[256,1536]{1,0:T(8,128)(2,1)S(1)}, bf16[256,1536]{1,0:T(8,128)(2,1)}, u32[]{:S(2)}, u32[]{:S(2)}) collective-permute-start(bf16[256,1536]{1,0:T(8,128)(2,1)S(1)} %bitcast.20), channel_id=1, source_target_pairs={{0,32},{1,33},{2,34},{3,35},{4,36},{5,37},{6,38},{7,39},{8,40},{9,... | collective-permute-start | bytes 2359304 | tf_op jit(solution)/shard_map/ppermute | solution.py:59
  59.7 38.9 %collective-permute-start.4 = (bf16[256,1536]{1,0:T(8,128)(2,1)S(1)}, bf16[256,1536]{1,0:T(8,128)(2,1)S(1)}, u32[]{:S(2)}, u32[]{:S(2)}) collective-permute-start(bf16[256,1536]{1,0:T(8,128)(2,1)S(1)} %collective-permute-done.refs_2_), channel_id=1, source_target_pairs={{0,1},{1,2},{2,3},{3,4},{4,5},{5,6},{6,7},{7,8},{8,9},{9,10},{10,1... | collective-permute-start | bytes 2359304 | tf_op jit(solution)/shard_map/ppermute | solution.py:26
  59.7 40.2 %collective-permute-start.5 = (bf16[256,1536]{1,0:T(8,128)(2,1)S(1)}, bf16[256,1536]{1,0:T(8,128)(2,1)S(1)}, u32[]{:S(2)}, u32[]{:S(2)}) collective-permute-start(bf16[256,1536]{1,0:T(8,128)(2,1)S(1)} %collective-permute-done.1.refs_4_), channel_id=1, source_target_pairs={{0,63},{1,0},{2,1},{3,2},{4,3},{5,4},{6,5},{7,6},{8,7},{9,8},{10,9... | collective-permute-start | bytes 2359304 | tf_op jit(solution)/shard_map/ppermute | solution.py:26
  86.0 7.9 %collective-permute-start.12 = (bf16[64,1536]{1,0:T(8,128)(2,1)S(1)}, bf16[64,1536]{1,0:T(8,128)(2,1)}, u32[]{:S(2)}, u32[]{:S(2)}) collective-permute-start(bf16[64,1536]{1,0:T(8,128)(2,1)S(1)} %get-tuple-element.46), channel_id=1, source_target_pairs={{0,24},{1,9},{2,10},{3,11},{4,12},{5,13},{6,14},{7,15},{8,0},{9,17... | collective-permute-start | bytes 589832 | tf_op jit(solution)/shard_map/ppermute | solution.py:50
  86.1 11.1 %collective-permute-start.13 = (bf16[64,1536]{1,0:T(8,128)(2,1)S(1)}, bf16[64,1536]{1,0:T(8,128)(2,1)}, u32[]{:S(2)}, u32[]{:S(2)}) collective-permute-start(bf16[64,1536]{1,0:T(8,128)(2,1)S(1)} %get-tuple-element.45), channel_id=1, source_target_pairs={{0,24},{1,25},{2,26},{3,27},{4,28},{5,29},{6,30},{7,15},{8,0},{9,1... | collective-permute-start | bytes 589832 | tf_op jit(solution)/shard_map/ppermute | solution.py:50
  86.2 15.8 %collective-permute-start.14 = (bf16[128,1536]{1,0:T(8,128)(2,1)S(1)}, bf16[128,1536]{1,0:T(8,128)(2,1)}, u32[]{:S(2)}, u32[]{:S(2)}) collective-permute-start(bf16[128,1536]{1,0:T(8,128)(2,1)S(1)} %bitcast.23), channel_id=1, source_target_pairs={{64,0},{65,1},{66,2},{67,3},{68,4},{69,5},{70,6},{71,7},{72,8},{73... | collective-permute-start | bytes 1179656 | tf_op jit(solution)/shard_map/ppermute | solution.py:37
  94.0 8.2 %collective-permute-start.15 = (bf16[128,1536]{1,0:T(8,128)(2,1)}, bf16[128,1536]{1,0:T(8,128)(2,1)}, u32[]{:S(2)}, u32[]{:S(2)}) collective-permute-start(bf16[128,1536]{1,0:T(8,128)(2,1)} %collective-permute-done.10.refs_1_), channel_id=1, source_target_pairs={{64,0},{65,1},{66,2},{67,3},{68,4},{69,5},{70,6},{71,7},{72,8},{73... | collective-permute-start | bytes 1179656 | tf_op jit(solution)/shard_map/ppermute | solution.py:37
  97.2 12.6 %collective-permute-start.16 = (bf16[128,1536]{1,0:T(8,128)(2,1)}, bf16[128,1536]{1,0:T(8,128)(2,1)}, u32[]{:S(2)}, u32[]{:S(2)}) collective-permute-start(bf16[128,1536]{1,0:T(8,128)(2,1)} %collective-permute-done.11.refs_2_), channel_id=1, source_target_pairs={{64,0},{65,1},{66,2},{67,3},{68,4},{69,5},{70,6},{71,7},{72,8},{73... | collective-permute-start | bytes 1179656 | tf_op jit(solution)/shard_map/ppermute | solution.py:37
  98.5 11.3 %collective-permute-start.17 = (bf16[64,1536]{1,0:T(8,128)(2,1)}, bf16[64,1536]{1,0:T(8,128)(2,1)}, u32[]{:S(2)}, u32[]{:S(2)}) collective-permute-start(bf16[64,1536]{1,0:T(8,128)(2,1)} %collective-permute-done.12.refs_3_), channel_id=1, source_target_pairs={{64,0},{65,1},{66,2},{67,3},{68,4},{69,5},{70,6},{71,7},{72,8},{73... | collective-permute-start | bytes 589832 | tf_op jit(solution)/shard_map/ppermute | solution.py:37
  100.7 9.1 %collective-permute-start.18 = (bf16[64,1536]{1,0:T(8,128)(2,1)}, bf16[64,1536]{1,0:T(8,128)(2,1)}, u32[]{:S(2)}, u32[]{:S(2)}) collective-permute-start(bf16[64,1536]{1,0:T(8,128)(2,1)} %collective-permute-done.13.refs_4_), channel_id=1, source_target_pairs={{64,0},{65,1},{66,2},{67,3},{68,4},{69,5},{70,6},{71,7},{72,8},{73... | collective-permute-start | bytes 589832 | tf_op jit(solution)/shard_map/ppermute | solution.py:37
  102.0 30.4 %collective-permute-start.6 = (bf16[256,1536]{1,0:T(8,128)(2,1)}, bf16[256,1536]{1,0:T(8,128)(2,1)S(1)}, u32[]{:S(2)}, u32[]{:S(2)}) collective-permute-start(bf16[256,1536]{1,0:T(8,128)(2,1)} %collective-permute-done.2.refs_7_), channel_id=1, source_target_pairs={{0,1},{1,2},{2,3},{3,4},{4,5},{5,6},{6,7},{7,8},{8,9},{9,10},{10,1... | collective-permute-start | bytes 2359304 | tf_op jit(solution)/shard_map/ppermute | solution.py:26
  102.1 30.3 %collective-permute-start.7 = (bf16[256,1536]{1,0:T(8,128)(2,1)}, bf16[256,1536]{1,0:T(8,128)(2,1)}, u32[]{:S(2)}, u32[]{:S(2)}) collective-permute-start(bf16[256,1536]{1,0:T(8,128)(2,1)} %collective-permute-done.3.refs_9_), channel_id=1, source_target_pairs={{0,63},{1,0},{2,1},{3,2},{4,3},{5,4},{6,5},{7,6},{8,7},{9,8},{10,9... | collective-permute-start | bytes 2359304 | tf_op jit(solution)/shard_map/ppermute | solution.py:26
  123.2 24.5 %collective-permute-start.19 = (bf16[256,1536]{1,0:T(8,128)(2,1)}, bf16[256,1536]{1,0:T(8,128)(2,1)S(1)}, u32[]{:S(2)}, u32[]{:S(2)}) collective-permute-start(bf16[256,1536]{1,0:T(8,128)(2,1)} %get-tuple-element.37), channel_id=1, source_target_pairs={{0,32},{1,33},{2,34},{3,35},{4,36},{5,37},{6,38},{7,39},{8,40},{9,... | collective-permute-start | bytes 2359304 | tf_op jit(solution)/shard_map/ppermute | solution.py:59
  125.6 22.2 %collective-permute-start.20 = (f32[256,128]{1,0:T(8,128)}, f32[256,128]{1,0:T(8,128)S(1)}, u32[]{:S(2)}, u32[]{:S(2)}) collective-permute-start(f32[256,128]{1,0:T(8,128)} %get-tuple-element.38), channel_id=1, source_target_pairs={{0,32},{1,33},{2,34},{3,35},{4,36},{5,37},{6,38},{7,39},{8,40},{9,... | collective-permute-start | bytes 393224 | tf_op jit(solution)/shard_map/ppermute | solution.py:59
  (9 other events, 199.6 us)

commit v4 on v3

--- a/solution.py
+++ b/solution.py
@@ -15,7 +15,7 @@
 CAND = 10
 N_LON = 64
 LOG2E = 1.4426950408889634
-STEP = 2 * PAIR
+STEP = 3 * PAIR
 TOTALS = 32
 POLAR_LATS = (0, 3)
 POLAR_LATS = (0, 3)

time: 158 us -> 155 us (0.981)
  Pallas kernels: 33.8 us -> 31.6 us
  transfers between devices with their start and end apart: 22 -> 22, of which waited for: 6 -> 6; matrix products, arithmetic and copies ran while one was open for 4% -> 4% of each run, Pallas kernels for 18% -> 17%
where the time goes in v4:
time: 155 us; the launch traced here: 153 us
  starting transfers between devices  57.7 us (37%)
  waiting for transfers between devices  51.8 us (33%)
  Pallas kernels  31.6 us (20%)
  local copies, waits for them, and re-layouts  8.51 us (5%)
  other arithmetic  2.68 us (2%)
    ppermute x8, starting transfers between devices, step_lon(): return lax.ppermute(value, 'lon', pairs)  33.4 us
    ppermute x8, waiting for transfers between devices, step_lon(): return lax.ppermute(value, 'lon', pairs)  26 us
    ppermute x4, waiting for transfers between devices, move(): lax.ppermute(value, 'lon', [(lon, target_of(lon)) for lon in range(N_LON)])  25.8 us
    pallas_call x1, Pallas kernels, near_attention(): pl.pallas_call(near_kernel, out_shape=[jax.ShapeDtypeStruct((TILE, D), jn...  13.6 us
    pallas_call x1, Pallas kernels, band_attention(): pl.pallas_call(band_kernel, out_shape=[jax.ShapeDtypeStruct((TILE, D), jn...  12.7 us
    ppermute x3, starting transfers between devices, polar_move(): return lax.ppermute(value, ('lat', 'lon'), pairs)  9.75 us
    ppermute x6, starting transfers between devices, core_move(): return lax.ppermute(value, ('lat', 'lon'), pairs)  7.72 us
    pallas_call x1, Pallas kernels, merge(): pl.pallas_call(merge_kernel, out_shape=jax.ShapeDtypeStruct((TILE, D), jn...  5.29 us
  transfers between devices with their start and end apart: 22, of which 6 were waited for; matrix products, arithmetic and copies ran while one was open for 4% of the time, Pallas kernels for 17%

profile of v4, /device:TPU:0, one launch (start us, length us, event | category | flops | bytes accessed | tf_op | source)
XLA Modules:
  0.0 152.6 jit_solution(6803752361482262755)
XLA Ops:
  0.8 1.9 %gather_fusion.1 = bf16[16,1536]{1,0:T(8,128)(2,1)S(1)} fusion(bf16[256,1536]{1,0:T(8,128)(2,1)} %bitcast.14, s32[1024]{0:T(1024)S(1)} %pad_clamp_fusion), kind=kCustom, calls=%fused_computation.1 | custom fusion | bytes 98368 | tf_op jit(solution)/shard_map/gather | solution.py:262
  2.7 1.3 collective-permute-start.9
  4.7 8.9 %collective-permute-start.1 = (bf16[256,1536]{1,0:T(8,128)(2,1)}, bf16[256,1536]{1,0:T(8,128)(2,1)S(1)}, u32[]{:S(2)}, u32[]{:S(2)}) collective-permute-start(bf16[256,1536]{1,0:T(8,128)(2,1)} %bitcast.11), channel_id=1, source_target_pairs={{0,63},{1,0},{2,1},{3,2},{4,3},{5,4},{6,5},{7,6},{8,7},{9,8},{10,9... | collective-permute-start | bytes 2359304 | tf_op jit(solution)/shard_map/ppermute | solution.py:26
  13.6 1.9 %gather_fusion = bf16[16,1536]{1,0:T(8,128)(2,1)S(1)} fusion(bf16[256,1536]{1,0:T(8,128)(2,1)} %bitcast.12, s32[1024]{0:T(1024)S(1)} %pad_clamp_fusion), kind=kCustom, calls=%fused_computation | custom fusion | bytes 98368 | tf_op jit(solution)/shard_map/gather | solution.py:262
  16.3 3.5 %all-to-all-start = ((bf16[8,16,1536]{2,1,0:T(8,128)(2,1)}), bf16[8,16,1536]{2,1,0:T(8,128)(2,1)S(1)}, u32[]{:S(2)}, u32[]{:S(2)}) async-start(bf16[8,16,1536]{2,1,0:T(8,128)(2,1)} %broadcast_in_dim.2), calls=%async_computation | async-start | bytes 786432 | tf_op jit(solution)/shard_map/all_to_all | solution.py:42
  19.8 13.8 %collective-permute-done.refs_2_ = bf16[256,1536]{1,0:T(8,128)(2,1)S(1)} collective-permute-done((bf16[256,1536]{1,0:T(8,128)(2,1)}, bf16[256,1536]{1,0:T(8,128)(2,1)S(1)}, u32[]{:S(2)}, u32[]{:S(2)}) %collective-permute-start) | collective-permute-done | bytes 786464 | tf_op jit(solution)/shard_map/ppermute | solution.py:26
  33.6 3.5 %collective-permute-done.1.refs_4_ = bf16[256,1536]{1,0:T(8,128)(2,1)S(1)} collective-permute-done((bf16[256,1536]{1,0:T(8,128)(2,1)}, bf16[256,1536]{1,0:T(8,128)(2,1)S(1)}, u32[]{:S(2)}, u32[]{:S(2)}) %collective-permute-start.1) | collective-permute-done | bytes 786464 | tf_op jit(solution)/shard_map/ppermute | solution.py:26
  37.1 8.2 %collective-permute-start.3 = (bf16[256,1536]{1,0:T(8,128)(2,1)S(1)}, bf16[256,1536]{1,0:T(8,128)(2,1)}, u32[]{:S(2)}, u32[]{:S(2)}) collective-permute-start(bf16[256,1536]{1,0:T(8,128)(2,1)S(1)} %bitcast.17), channel_id=1, source_target_pairs={{0,63},{1,0},{2,1},{3,2},{4,3},{5,4},{6,5},{7,6},{8,7},{9,8},{10,9... | collective-permute-start | bytes 2359304 | tf_op jit(solution)/shard_map/ppermute | solution.py:26
  45.3 3.2 %collective-permute-start.11 = (bf16[128,1536]{1,0:T(8,128)(2,1)S(1)}, bf16[128,1536]{1,0:T(8,128)(2,1)}, u32[]{:S(2)}, u32[]{:S(2)}) collective-permute-start(bf16[128,1536]{1,0:T(8,128)(2,1)S(1)} %bitcast.22), channel_id=1, source_target_pairs={{0,24},{1,25},{2,26},{3,27},{4,28},{5,29},{6,30},{7,31},{8,0},{9,1... | collective-permute-start | bytes 1179656 | tf_op jit(solution)/shard_map/ppermute | solution.py:50
  48.6 2.4 %collective-permute-start.8 = (bf16[256,1536]{1,0:T(8,128)(2,1)S(1)}, bf16[256,1536]{1,0:T(8,128)(2,1)}, u32[]{:S(2)}, u32[]{:S(2)}) collective-permute-start(bf16[256,1536]{1,0:T(8,128)(2,1)S(1)} %bitcast.20), channel_id=1, source_target_pairs={{0,32},{1,33},{2,34},{3,35},{4,36},{5,37},{6,38},{7,39},{8,40},{9,... | collective-permute-start | bytes 2359304 | tf_op jit(solution)/shard_map/ppermute | solution.py:59
  51.0 8.7 %collective-permute-done.2.refs_7_ = bf16[256,1536]{1,0:T(8,128)(2,1)} collective-permute-done((bf16[256,1536]{1,0:T(8,128)(2,1)S(1)}, bf16[256,1536]{1,0:T(8,128)(2,1)}, u32[]{:S(2)}, u32[]{:S(2)}) %collective-permute-start.2) | collective-permute-done | bytes 786464 | tf_op jit(solution)/shard_map/ppermute | solution.py:26
  59.7 7.7 %collective-permute-start.5 = (bf16[256,1536]{1,0:T(8,128)(2,1)S(1)}, bf16[256,1536]{1,0:T(8,128)(2,1)S(1)}, u32[]{:S(2)}, u32[]{:S(2)}) collective-permute-start(bf16[256,1536]{1,0:T(8,128)(2,1)S(1)} %collective-permute-done.1.refs_4_), channel_id=1, source_target_pairs={{0,63},{1,0},{2,1},{3,2},{4,3},{5,4},{6,5},{7,6},{8,7},{9,8},{10,9... | collective-permute-start | bytes 2359304 | tf_op jit(solution)/shard_map/ppermute | solution.py:26
  67.4 17.3 %collective-permute-done.10.refs_1_ = bf16[128,1536]{1,0:T(8,128)(2,1)} collective-permute-done((bf16[128,1536]{1,0:T(8,128)(2,1)S(1)}, bf16[128,1536]{1,0:T(8,128)(2,1)}, u32[]{:S(2)}, u32[]{:S(2)}) %collective-permute-start.10) | collective-permute-done | bytes 393248 | tf_op jit(solution)/shard_map/ppermute | solution.py:50
  86.2 1.3 collective-permute-start.14
  87.5 6.4 %collective-permute-done.12.refs_3_ = bf16[64,1536]{1,0:T(8,128)(2,1)} collective-permute-done((bf16[64,1536]{1,0:T(8,128)(2,1)S(1)}, bf16[64,1536]{1,0:T(8,128)(2,1)}, u32[]{:S(2)}, u32[]{:S(2)}) %collective-permute-start.12) | collective-permute-done | bytes 196640 | tf_op jit(solution)/shard_map/ppermute | solution.py:50
  94.0 1.3 collective-permute-start.15
  95.2 2.0 %collective-permute-done.13.refs_4_ = bf16[64,1536]{1,0:T(8,128)(2,1)} collective-permute-done((bf16[64,1536]{1,0:T(8,128)(2,1)S(1)}, bf16[64,1536]{1,0:T(8,128)(2,1)}, u32[]{:S(2)}, u32[]{:S(2)}) %collective-permute-start.13) | collective-permute-done | bytes 196640 | tf_op jit(solution)/shard_map/ppermute | solution.py:50
  98.5 1.3 collective-permute-start.17
  102.1 7.7 %collective-permute-start.7 = (bf16[256,1536]{1,0:T(8,128)(2,1)}, bf16[256,1536]{1,0:T(8,128)(2,1)}, u32[]{:S(2)}, u32[]{:S(2)}) collective-permute-start(bf16[256,1536]{1,0:T(8,128)(2,1)} %collective-permute-done.3.refs_9_), channel_id=1, source_target_pairs={{0,63},{1,0},{2,1},{3,2},{4,3},{5,4},{6,5},{7,6},{8,7},{9,8},{10,9... | collective-permute-start | bytes 2359304 | tf_op jit(solution)/shard_map/ppermute | solution.py:26
  109.9 12.7 %band_attention.1 = (bf16[256,1536]{1,0:T(8,128)(2,1)}, bf16[256,1536]{1,0:T(8,128)(2,1)}, f32[256,128]{1,0:T(8,128)}, f32[256,128]{1,0:T(8,128)}) custom-call(s32[1]{0:T(128)} %bitcast.polar_ref, bf16[256,1536]{1,0:T(8,128)(2,1)} %bitcast.18, bf16[256,1536]{1,0:T(8,128)(2,1)} %collective-permute-done.8.q_other, bf16[128,1536]{1,0:T(8,128)(2,1)} %bitcast.24, ...), custom_call_target="tpu_custom_call" | custom-call | flops 60000002048 | bytes 11796480 | tf_op jit(solution)/shard_map/band_attention/pallas_call | solution.py:199
  122.7 2.4 %collective-permute-start.19 = (bf16[256,1536]{1,0:T(8,128)(2,1)}, bf16[256,1536]{1,0:T(8,128)(2,1)S(1)}, u32[]{:S(2)}, u32[]{:S(2)}) collective-permute-start(bf16[256,1536]{1,0:T(8,128)(2,1)} %get-tuple-element.37), channel_id=1, source_target_pairs={{0,32},{1,33},{2,34},{3,35},{4,36},{5,37},{6,38},{7,39},{8,40},{9,... | collective-permute-start | bytes 2359304 | tf_op jit(solution)/shard_map/ppermute | solution.py:59
  125.0 5.0 %collective-permute-start.20 = (f32[256,128]{1,0:T(8,128)}, f32[256,128]{1,0:T(8,128)S(1)}, u32[]{:S(2)}, u32[]{:S(2)}) collective-permute-start(f32[256,128]{1,0:T(8,128)} %get-tuple-element.38), channel_id=1, source_target_pairs={{0,32},{1,33},{2,34},{3,35},{4,36},{5,37},{6,38},{7,39},{8,40},{9,... | collective-permute-start | bytes 393224 | tf_op jit(solution)/shard_map/ppermute | solution.py:59
  132.8 13.6 %near_attention.1 = (f32[256,1536]{1,0:T(8,128)}, f32[256,128]{1,0:T(8,128)}) custom-call(s32[16]{0:T(128)} %reshape.53.lists_ref, bf16[256,1536]{1,0:T(8,128)(2,1)} %bitcast.19, bf16[256,1536]{1,0:T(8,128)(2,1)} %copy-done.4, bf16[256,1536]{1,0:T(8,128)(2,1)} %copy-done.2, bf16[256,1536]{1,0:T(8,128)(2,1)} %bitcast.13, bf16[256,1536]{1,0:T(8,128)(2,1)} %copy-done.3, ...), custom_call_target="tpu_custom_call" | custom-call | tf_op jit(solution)/shard_map/near_attention/pallas_call | solution.py:219
  147.3 5.3 %merge.1 = bf16[256,1536]{1,0:T(8,128)(2,1)} custom-call(s32[1]{0:T(128)} %bitcast.polar_ref, f32[256,1536]{1,0:T(8,128)} %get-tuple-element.39.near_ref, bf16[256,1536]{1,0:T(8,128)(2,1)} %get-tuple-element.40.own_ref, bf16[256,1536]{1,0:T(8,128)(2,1)} %copy-done.7, f32[256,128]{1,0:T(8,128)} %get-tuple-element.42.refs_0_, ...), custom_call_target="tpu_custom_call" | custom-call | tf_op jit(solution)/shard_map/merge/pallas_call | solution.py:238
  (55 shorter events, 11.0 us)
Async XLA Ops:
  2.7 12.9 %collective-permute-start.9 = (bf16[16,1536]{1,0:T(8,128)(2,1)S(1)}, bf16[16,1536]{1,0:T(8,128)(2,1)S(1)}, u32[]{:S(2)}, u32[]{:S(2)}) collective-permute-start(bf16[16,1536]{1,0:T(8,128)(2,1)S(1)} %gather_fusion.1), channel_id=1, source_target_pairs={{0,64},{1,65},{2,66},{3,67},{4,68},{5,69},{6,70},{7,71},{8,72},{9,... | collective-permute-start | bytes 147464 | tf_op jit(solution)/shard_map/ppermute | solution.py:37
  4.0 29.6 %collective-permute-start = (bf16[256,1536]{1,0:T(8,128)(2,1)}, bf16[256,1536]{1,0:T(8,128)(2,1)S(1)}, u32[]{:S(2)}, u32[]{:S(2)}) collective-permute-start(bf16[256,1536]{1,0:T(8,128)(2,1)} %bitcast.10), channel_id=1, source_target_pairs={{0,1},{1,2},{2,3},{3,4},{4,5},{5,6},{6,7},{7,8},{8,9},{9,10},{10,1... | collective-permute-start | bytes 2359304 | tf_op jit(solution)/shard_map/ppermute | solution.py:26
  4.7 32.5 %collective-permute-start.1 = (bf16[256,1536]{1,0:T(8,128)(2,1)}, bf16[256,1536]{1,0:T(8,128)(2,1)S(1)}, u32[]{:S(2)}, u32[]{:S(2)}) collective-permute-start(bf16[256,1536]{1,0:T(8,128)(2,1)} %bitcast.11), channel_id=1, source_target_pairs={{0,63},{1,0},{2,1},{3,2},{4,3},{5,4},{6,5},{7,6},{8,7},{9,8},{10,9... | collective-permute-start | bytes 2359304 | tf_op jit(solution)/shard_map/ppermute | solution.py:26
  16.3 29.0 %all-to-all-start = ((bf16[8,16,1536]{2,1,0:T(8,128)(2,1)}), bf16[8,16,1536]{2,1,0:T(8,128)(2,1)S(1)}, u32[]{:S(2)}, u32[]{:S(2)}) async-start(bf16[8,16,1536]{2,1,0:T(8,128)(2,1)} %broadcast_in_dim.2), calls=%async_computation | async-start | bytes 786432 | tf_op jit(solution)/shard_map/all_to_all | solution.py:42
  33.6 89.0 %copy-start.2 = (bf16[256,1536]{1,0:T(8,128)(2,1)}, bf16[256,1536]{1,0:T(8,128)(2,1)S(1)}, u32[]{:S(2)}) copy-start(bf16[256,1536]{1,0:T(8,128)(2,1)S(1)} %collective-permute-done.refs_2_) | copy-start | bytes 2359300
  37.1 85.5 %copy-start.3 = (bf16[256,1536]{1,0:T(8,128)(2,1)}, bf16[256,1536]{1,0:T(8,128)(2,1)S(1)}, u32[]{:S(2)}) copy-start(bf16[256,1536]{1,0:T(8,128)(2,1)S(1)} %collective-permute-done.1.refs_4_) | copy-start | bytes 2359300
  37.1 22.5 %collective-permute-start.2 = (bf16[256,1536]{1,0:T(8,128)(2,1)S(1)}, bf16[256,1536]{1,0:T(8,128)(2,1)}, u32[]{:S(2)}, u32[]{:S(2)}) collective-permute-start(bf16[256,1536]{1,0:T(8,128)(2,1)S(1)} %bitcast.16), channel_id=1, source_target_pairs={{0,1},{1,2},{2,3},{3,4},{4,5},{5,6},{6,7},{7,8},{8,9},{9,10},{10,1... | collective-permute-start | bytes 2359304 | tf_op jit(solution)/shard_map/ppermute | solution.py:26
  37.1 22.5 %collective-permute-start.3 = (bf16[256,1536]{1,0:T(8,128)(2,1)S(1)}, bf16[256,1536]{1,0:T(8,128)(2,1)}, u32[]{:S(2)}, u32[]{:S(2)}) collective-permute-start(bf16[256,1536]{1,0:T(8,128)(2,1)S(1)} %bitcast.17), channel_id=1, source_target_pairs={{0,63},{1,0},{2,1},{3,2},{4,3},{5,4},{6,5},{7,6},{8,7},{9,8},{10,9... | collective-permute-start | bytes 2359304 | tf_op jit(solution)/shard_map/ppermute | solution.py:26
  45.3 39.4 %collective-permute-start.10 = (bf16[128,1536]{1,0:T(8,128)(2,1)S(1)}, bf16[128,1536]{1,0:T(8,128)(2,1)}, u32[]{:S(2)}, u32[]{:S(2)}) collective-permute-start(bf16[128,1536]{1,0:T(8,128)(2,1)S(1)} %bitcast.21), channel_id=1, source_target_pairs={{0,8},{1,9},{2,10},{3,11},{4,12},{5,13},{6,14},{7,15},{8,16},{9,17... | collective-permute-start | bytes 1179656 | tf_op jit(solution)/shard_map/ppermute | solution.py:50
  45.3 39.4 %collective-permute-start.11 = (bf16[128,1536]{1,0:T(8,128)(2,1)S(1)}, bf16[128,1536]{1,0:T(8,128)(2,1)}, u32[]{:S(2)}, u32[]{:S(2)}) collective-permute-start(bf16[128,1536]{1,0:T(8,128)(2,1)S(1)} %bitcast.22), channel_id=1, source_target_pairs={{0,24},{1,25},{2,26},{3,27},{4,28},{5,29},{6,30},{7,31},{8,0},{9,1... | collective-permute-start | bytes 1179656 | tf_op jit(solution)/shard_map/ppermute | solution.py:50
  48.6 37.6 %collective-permute-start.8 = (bf16[256,1536]{1,0:T(8,128)(2,1)S(1)}, bf16[256,1536]{1,0:T(8,128)(2,1)}, u32[]{:S(2)}, u32[]{:S(2)}) collective-permute-start(bf16[256,1536]{1,0:T(8,128)(2,1)S(1)} %bitcast.20), channel_id=1, source_target_pairs={{0,32},{1,33},{2,34},{3,35},{4,36},{5,37},{6,38},{7,39},{8,40},{9,... | collective-permute-start | bytes 2359304 | tf_op jit(solution)/shard_map/ppermute | solution.py:59
  59.7 38.9 %collective-permute-start.4 = (bf16[256,1536]{1,0:T(8,128)(2,1)S(1)}, bf16[256,1536]{1,0:T(8,128)(2,1)S(1)}, u32[]{:S(2)}, u32[]{:S(2)}) collective-permute-start(bf16[256,1536]{1,0:T(8,128)(2,1)S(1)} %collective-permute-done.refs_2_), channel_id=1, source_target_pairs={{0,1},{1,2},{2,3},{3,4},{4,5},{5,6},{6,7},{7,8},{8,9},{9,10},{10,1... | collective-permute-start | bytes 2359304 | tf_op jit(solution)/shard_map/ppermute | solution.py:26
  59.7 40.2 %collective-permute-start.5 = (bf16[256,1536]{1,0:T(8,128)(2,1)S(1)}, bf16[256,1536]{1,0:T(8,128)(2,1)S(1)}, u32[]{:S(2)}, u32[]{:S(2)}) collective-permute-start(bf16[256,1536]{1,0:T(8,128)(2,1)S(1)} %collective-permute-done.1.refs_4_), channel_id=1, source_target_pairs={{0,63},{1,0},{2,1},{3,2},{4,3},{5,4},{6,5},{7,6},{8,7},{9,8},{10,9... | collective-permute-start | bytes 2359304 | tf_op jit(solution)/shard_map/ppermute | solution.py:26
  86.0 7.9 %collective-permute-start.12 = (bf16[64,1536]{1,0:T(8,128)(2,1)S(1)}, bf16[64,1536]{1,0:T(8,128)(2,1)}, u32[]{:S(2)}, u32[]{:S(2)}) collective-permute-start(bf16[64,1536]{1,0:T(8,128)(2,1)S(1)} %get-tuple-element.46), channel_id=1, source_target_pairs={{0,24},{1,9},{2,10},{3,11},{4,12},{5,13},{6,14},{7,15},{8,0},{9,17... | collective-permute-start | bytes 589832 | tf_op jit(solution)/shard_map/ppermute | solution.py:50
  86.1 11.1 %collective-permute-start.13 = (bf16[64,1536]{1,0:T(8,128)(2,1)S(1)}, bf16[64,1536]{1,0:T(8,128)(2,1)}, u32[]{:S(2)}, u32[]{:S(2)}) collective-permute-start(bf16[64,1536]{1,0:T(8,128)(2,1)S(1)} %get-tuple-element.45), channel_id=1, source_target_pairs={{0,24},{1,25},{2,26},{3,27},{4,28},{5,29},{6,30},{7,15},{8,0},{9,1... | collective-permute-start | bytes 589832 | tf_op jit(solution)/shard_map/ppermute | solution.py:50
  86.2 15.8 %collective-permute-start.14 = (bf16[128,1536]{1,0:T(8,128)(2,1)S(1)}, bf16[128,1536]{1,0:T(8,128)(2,1)}, u32[]{:S(2)}, u32[]{:S(2)}) collective-permute-start(bf16[128,1536]{1,0:T(8,128)(2,1)S(1)} %bitcast.23), channel_id=1, source_target_pairs={{64,0},{65,1},{66,2},{67,3},{68,4},{69,5},{70,6},{71,7},{72,8},{73... | collective-permute-start | bytes 1179656 | tf_op jit(solution)/shard_map/ppermute | solution.py:37
  94.0 8.2 %collective-permute-start.15 = (bf16[128,1536]{1,0:T(8,128)(2,1)}, bf16[128,1536]{1,0:T(8,128)(2,1)}, u32[]{:S(2)}, u32[]{:S(2)}) collective-permute-start(bf16[128,1536]{1,0:T(8,128)(2,1)} %collective-permute-done.10.refs_1_), channel_id=1, source_target_pairs={{64,0},{65,1},{66,2},{67,3},{68,4},{69,5},{70,6},{71,7},{72,8},{73... | collective-permute-start | bytes 1179656 | tf_op jit(solution)/shard_map/ppermute | solution.py:37
  97.2 12.6 %collective-permute-start.16 = (bf16[128,1536]{1,0:T(8,128)(2,1)}, bf16[128,1536]{1,0:T(8,128)(2,1)}, u32[]{:S(2)}, u32[]{:S(2)}) collective-permute-start(bf16[128,1536]{1,0:T(8,128)(2,1)} %collective-permute-done.11.refs_2_), channel_id=1, source_target_pairs={{64,0},{65,1},{66,2},{67,3},{68,4},{69,5},{70,6},{71,7},{72,8},{73... | collective-permute-start | bytes 1179656 | tf_op jit(solution)/shard_map/ppermute | solution.py:37
  98.5 11.3 %collective-permute-start.17 = (bf16[64,1536]{1,0:T(8,128)(2,1)}, bf16[64,1536]{1,0:T(8,128)(2,1)}, u32[]{:S(2)}, u32[]{:S(2)}) collective-permute-start(bf16[64,1536]{1,0:T(8,128)(2,1)} %collective-permute-done.12.refs_3_), channel_id=1, source_target_pairs={{64,0},{65,1},{66,2},{67,3},{68,4},{69,5},{70,6},{71,7},{72,8},{73... | collective-permute-start | bytes 589832 | tf_op jit(solution)/shard_map/ppermute | solution.py:37
  100.7 9.1 %collective-permute-start.18 = (bf16[64,1536]{1,0:T(8,128)(2,1)}, bf16[64,1536]{1,0:T(8,128)(2,1)}, u32[]{:S(2)}, u32[]{:S(2)}) collective-permute-start(bf16[64,1536]{1,0:T(8,128)(2,1)} %collective-permute-done.13.refs_4_), channel_id=1, source_target_pairs={{64,0},{65,1},{66,2},{67,3},{68,4},{69,5},{70,6},{71,7},{72,8},{73... | collective-permute-start | bytes 589832 | tf_op jit(solution)/shard_map/ppermute | solution.py:37
  102.0 29.8 %collective-permute-start.6 = (bf16[256,1536]{1,0:T(8,128)(2,1)}, bf16[256,1536]{1,0:T(8,128)(2,1)S(1)}, u32[]{:S(2)}, u32[]{:S(2)}) collective-permute-start(bf16[256,1536]{1,0:T(8,128)(2,1)} %collective-permute-done.2.refs_7_), channel_id=1, source_target_pairs={{0,1},{1,2},{2,3},{3,4},{4,5},{5,6},{6,7},{7,8},{8,9},{9,10},{10,1... | collective-permute-start | bytes 2359304 | tf_op jit(solution)/shard_map/ppermute | solution.py:26
  102.1 29.7 %collective-permute-start.7 = (bf16[256,1536]{1,0:T(8,128)(2,1)}, bf16[256,1536]{1,0:T(8,128)(2,1)}, u32[]{:S(2)}, u32[]{:S(2)}) collective-permute-start(bf16[256,1536]{1,0:T(8,128)(2,1)} %collective-permute-done.3.refs_9_), channel_id=1, source_target_pairs={{0,63},{1,0},{2,1},{3,2},{4,3},{5,4},{6,5},{7,6},{8,7},{9,8},{10,9... | collective-permute-start | bytes 2359304 | tf_op jit(solution)/shard_map/ppermute | solution.py:26
  122.7 23.8 %collective-permute-start.19 = (bf16[256,1536]{1,0:T(8,128)(2,1)}, bf16[256,1536]{1,0:T(8,128)(2,1)S(1)}, u32[]{:S(2)}, u32[]{:S(2)}) collective-permute-start(bf16[256,1536]{1,0:T(8,128)(2,1)} %get-tuple-element.37), channel_id=1, source_target_pairs={{0,32},{1,33},{2,34},{3,35},{4,36},{5,37},{6,38},{7,39},{8,40},{9,... | collective-permute-start | bytes 2359304 | tf_op jit(solution)/shard_map/ppermute | solution.py:59
  125.0 21.4 %collective-permute-start.20 = (f32[256,128]{1,0:T(8,128)}, f32[256,128]{1,0:T(8,128)S(1)}, u32[]{:S(2)}, u32[]{:S(2)}) collective-permute-start(f32[256,128]{1,0:T(8,128)} %get-tuple-element.38), channel_id=1, source_target_pairs={{0,32},{1,33},{2,34},{3,35},{4,36},{5,37},{6,38},{7,39},{8,40},{9,... | collective-permute-start | bytes 393224 | tf_op jit(solution)/shard_map/ppermute | solution.py:59
  (9 other events, 198.4 us)

commit v5 on v4

--- a/solution.py
+++ b/solution.py
@@ -15,7 +15,7 @@
 CAND = 10
 N_LON = 64
 LOG2E = 1.4426950408889634
-STEP = 3 * PAIR
+STEP = 4 * PAIR
 TOTALS = 32
 POLAR_LATS = (0, 3)
 POLAR_LATS = (0, 3)

time: 155 us -> 154 us (level)
  Pallas kernels: 31.6 us -> 29.9 us
where the time goes in v5:
time: 154 us; the launch traced here: 151 us
  starting transfers between devices  57.7 us (37%)
  waiting for transfers between devices  51.8 us (34%)
  Pallas kernels  29.9 us (19%)
  local copies, waits for them, and re-layouts  8.51 us (6%)
  other arithmetic  2.68 us (2%)
    ppermute x8, starting transfers between devices, step_lon(): return lax.ppermute(value, 'lon', pairs)  33.4 us
    ppermute x8, waiting for transfers between devices, step_lon(): return lax.ppermute(value, 'lon', pairs)  26 us
    ppermute x4, waiting for transfers between devices, move(): lax.ppermute(value, 'lon', [(lon, target_of(lon)) for lon in range(N_LON)])  25.8 us
    pallas_call x1, Pallas kernels, near_attention(): pl.pallas_call(near_kernel, out_shape=[jax.ShapeDtypeStruct((TILE, D), jn...  12.8 us
    pallas_call x1, Pallas kernels, band_attention(): pl.pallas_call(band_kernel, out_shape=[jax.ShapeDtypeStruct((TILE, D), jn...  12.3 us
    ppermute x3, starting transfers between devices, polar_move(): return lax.ppermute(value, ('lat', 'lon'), pairs)  9.75 us
    ppermute x6, starting transfers between devices, core_move(): return lax.ppermute(value, ('lat', 'lon'), pairs)  7.72 us
    pallas_call x1, Pallas kernels, merge(): pl.pallas_call(merge_kernel, out_shape=jax.ShapeDtypeStruct((TILE, D), jn...  4.76 us
  transfers between devices with their start and end apart: 22, of which 6 were waited for; matrix products, arithmetic and copies ran while one was open for 4% of the time, Pallas kernels for 17%

profile of v5, /device:TPU:0, one launch (start us, length us, event | category | flops | bytes accessed | tf_op | source)
XLA Modules:
  0.0 150.9 jit_solution(15545438959209623928)
XLA Ops:
  0.8 1.9 %gather_fusion.1 = bf16[16,1536]{1,0:T(8,128)(2,1)S(1)} fusion(bf16[256,1536]{1,0:T(8,128)(2,1)} %bitcast.14, s32[1024]{0:T(1024)S(1)} %pad_clamp_fusion), kind=kCustom, calls=%fused_computation.1 | custom fusion | bytes 98368 | tf_op jit(solution)/shard_map/gather | solution.py:262
  2.7 1.3 collective-permute-start.9
  4.7 8.9 %collective-permute-start.1 = (bf16[256,1536]{1,0:T(8,128)(2,1)}, bf16[256,1536]{1,0:T(8,128)(2,1)S(1)}, u32[]{:S(2)}, u32[]{:S(2)}) collective-permute-start(bf16[256,1536]{1,0:T(8,128)(2,1)} %bitcast.11), channel_id=1, source_target_pairs={{0,63},{1,0},{2,1},{3,2},{4,3},{5,4},{6,5},{7,6},{8,7},{9,8},{10,9... | collective-permute-start | bytes 2359304 | tf_op jit(solution)/shard_map/ppermute | solution.py:26
  13.6 1.9 %gather_fusion = bf16[16,1536]{1,0:T(8,128)(2,1)S(1)} fusion(bf16[256,1536]{1,0:T(8,128)(2,1)} %bitcast.12, s32[1024]{0:T(1024)S(1)} %pad_clamp_fusion), kind=kCustom, calls=%fused_computation | custom fusion | bytes 98368 | tf_op jit(solution)/shard_map/gather | solution.py:262
  16.3 3.5 %all-to-all-start = ((bf16[8,16,1536]{2,1,0:T(8,128)(2,1)}), bf16[8,16,1536]{2,1,0:T(8,128)(2,1)S(1)}, u32[]{:S(2)}, u32[]{:S(2)}) async-start(bf16[8,16,1536]{2,1,0:T(8,128)(2,1)} %broadcast_in_dim.2), calls=%async_computation | async-start | bytes 786432 | tf_op jit(solution)/shard_map/all_to_all | solution.py:42
  19.8 13.8 %collective-permute-done.refs_2_ = bf16[256,1536]{1,0:T(8,128)(2,1)S(1)} collective-permute-done((bf16[256,1536]{1,0:T(8,128)(2,1)}, bf16[256,1536]{1,0:T(8,128)(2,1)S(1)}, u32[]{:S(2)}, u32[]{:S(2)}) %collective-permute-start) | collective-permute-done | bytes 786464 | tf_op jit(solution)/shard_map/ppermute | solution.py:26
  33.6 3.5 %collective-permute-done.1.refs_4_ = bf16[256,1536]{1,0:T(8,128)(2,1)S(1)} collective-permute-done((bf16[256,1536]{1,0:T(8,128)(2,1)}, bf16[256,1536]{1,0:T(8,128)(2,1)S(1)}, u32[]{:S(2)}, u32[]{:S(2)}) %collective-permute-start.1) | collective-permute-done | bytes 786464 | tf_op jit(solution)/shard_map/ppermute | solution.py:26
  37.1 8.2 %collective-permute-start.3 = (bf16[256,1536]{1,0:T(8,128)(2,1)S(1)}, bf16[256,1536]{1,0:T(8,128)(2,1)}, u32[]{:S(2)}, u32[]{:S(2)}) collective-permute-start(bf16[256,1536]{1,0:T(8,128)(2,1)S(1)} %bitcast.17), channel_id=1, source_target_pairs={{0,63},{1,0},{2,1},{3,2},{4,3},{5,4},{6,5},{7,6},{8,7},{9,8},{10,9... | collective-permute-start | bytes 2359304 | tf_op jit(solution)/shard_map/ppermute | solution.py:26
  45.3 3.2 %collective-permute-start.11 = (bf16[128,1536]{1,0:T(8,128)(2,1)S(1)}, bf16[128,1536]{1,0:T(8,128)(2,1)}, u32[]{:S(2)}, u32[]{:S(2)}) collective-permute-start(bf16[128,1536]{1,0:T(8,128)(2,1)S(1)} %bitcast.22), channel_id=1, source_target_pairs={{0,24},{1,25},{2,26},{3,27},{4,28},{5,29},{6,30},{7,31},{8,0},{9,1... | collective-permute-start | bytes 1179656 | tf_op jit(solution)/shard_map/ppermute | solution.py:50
  48.6 2.4 %collective-permute-start.8 = (bf16[256,1536]{1,0:T(8,128)(2,1)S(1)}, bf16[256,1536]{1,0:T(8,128)(2,1)}, u32[]{:S(2)}, u32[]{:S(2)}) collective-permute-start(bf16[256,1536]{1,0:T(8,128)(2,1)S(1)} %bitcast.20), channel_id=1, source_target_pairs={{0,32},{1,33},{2,34},{3,35},{4,36},{5,37},{6,38},{7,39},{8,40},{9,... | collective-permute-start | bytes 2359304 | tf_op jit(solution)/shard_map/ppermute | solution.py:59
  51.0 8.7 %collective-permute-done.2.refs_7_ = bf16[256,1536]{1,0:T(8,128)(2,1)} collective-permute-done((bf16[256,1536]{1,0:T(8,128)(2,1)S(1)}, bf16[256,1536]{1,0:T(8,128)(2,1)}, u32[]{:S(2)}, u32[]{:S(2)}) %collective-permute-start.2) | collective-permute-done | bytes 786464 | tf_op jit(solution)/shard_map/ppermute | solution.py:26
  59.7 7.7 %collective-permute-start.5 = (bf16[256,1536]{1,0:T(8,128)(2,1)S(1)}, bf16[256,1536]{1,0:T(8,128)(2,1)S(1)}, u32[]{:S(2)}, u32[]{:S(2)}) collective-permute-start(bf16[256,1536]{1,0:T(8,128)(2,1)S(1)} %collective-permute-done.1.refs_4_), channel_id=1, source_target_pairs={{0,63},{1,0},{2,1},{3,2},{4,3},{5,4},{6,5},{7,6},{8,7},{9,8},{10,9... | collective-permute-start | bytes 2359304 | tf_op jit(solution)/shard_map/ppermute | solution.py:26
  67.4 17.3 %collective-permute-done.10.refs_1_ = bf16[128,1536]{1,0:T(8,128)(2,1)} collective-permute-done((bf16[128,1536]{1,0:T(8,128)(2,1)S(1)}, bf16[128,1536]{1,0:T(8,128)(2,1)}, u32[]{:S(2)}, u32[]{:S(2)}) %collective-permute-start.10) | collective-permute-done | bytes 393248 | tf_op jit(solution)/shard_map/ppermute | solution.py:50
  86.2 1.3 collective-permute-start.14
  87.5 6.4 %collective-permute-done.12.refs_3_ = bf16[64,1536]{1,0:T(8,128)(2,1)} collective-permute-done((bf16[64,1536]{1,0:T(8,128)(2,1)S(1)}, bf16[64,1536]{1,0:T(8,128)(2,1)}, u32[]{:S(2)}, u32[]{:S(2)}) %collective-permute-start.12) | collective-permute-done | bytes 196640 | tf_op jit(solution)/shard_map/ppermute | solution.py:50
  94.0 1.3 collective-permute-start.15
  95.2 2.0 %collective-permute-done.13.refs_4_ = bf16[64,1536]{1,0:T(8,128)(2,1)} collective-permute-done((bf16[64,1536]{1,0:T(8,128)(2,1)S(1)}, bf16[64,1536]{1,0:T(8,128)(2,1)}, u32[]{:S(2)}, u32[]{:S(2)}) %collective-permute-start.13) | collective-permute-done | bytes 196640 | tf_op jit(solution)/shard_map/ppermute | solution.py:50
  98.5 1.3 collective-permute-start.17
  102.1 7.7 %collective-permute-start.7 = (bf16[256,1536]{1,0:T(8,128)(2,1)}, bf16[256,1536]{1,0:T(8,128)(2,1)}, u32[]{:S(2)}, u32[]{:S(2)}) collective-permute-start(bf16[256,1536]{1,0:T(8,128)(2,1)} %collective-permute-done.3.refs_9_), channel_id=1, source_target_pairs={{0,63},{1,0},{2,1},{3,2},{4,3},{5,4},{6,5},{7,6},{8,7},{9,8},{10,9... | collective-permute-start | bytes 2359304 | tf_op jit(solution)/shard_map/ppermute | solution.py:26
  109.9 12.3 %band_attention.1 = (bf16[256,1536]{1,0:T(8,128)(2,1)}, bf16[256,1536]{1,0:T(8,128)(2,1)}, f32[256,128]{1,0:T(8,128)}, f32[256,128]{1,0:T(8,128)}) custom-call(s32[1]{0:T(128)} %bitcast.polar_ref, bf16[256,1536]{1,0:T(8,128)(2,1)} %bitcast.18, bf16[256,1536]{1,0:T(8,128)(2,1)} %collective-permute-done.8.q_other, bf16[128,1536]{1,0:T(8,128)(2,1)} %bitcast.24, ...), custom_call_target="tpu_custom_call" | custom-call | flops 60000002048 | bytes 11796480 | tf_op jit(solution)/shard_map/band_attention/pallas_call | solution.py:199
  122.3 2.4 %collective-permute-start.19 = (bf16[256,1536]{1,0:T(8,128)(2,1)}, bf16[256,1536]{1,0:T(8,128)(2,1)S(1)}, u32[]{:S(2)}, u32[]{:S(2)}) collective-permute-start(bf16[256,1536]{1,0:T(8,128)(2,1)} %get-tuple-element.37), channel_id=1, source_target_pairs={{0,32},{1,33},{2,34},{3,35},{4,36},{5,37},{6,38},{7,39},{8,40},{9,... | collective-permute-start | bytes 2359304 | tf_op jit(solution)/shard_map/ppermute | solution.py:59
  124.6 5.0 %collective-permute-start.20 = (f32[256,128]{1,0:T(8,128)}, f32[256,128]{1,0:T(8,128)S(1)}, u32[]{:S(2)}, u32[]{:S(2)}) collective-permute-start(f32[256,128]{1,0:T(8,128)} %get-tuple-element.38), channel_id=1, source_target_pairs={{0,32},{1,33},{2,34},{3,35},{4,36},{5,37},{6,38},{7,39},{8,40},{9,... | collective-permute-start | bytes 393224 | tf_op jit(solution)/shard_map/ppermute | solution.py:59
  132.4 12.8 %near_attention.1 = (f32[256,1536]{1,0:T(8,128)}, f32[256,128]{1,0:T(8,128)}) custom-call(s32[16]{0:T(128)} %reshape.53.lists_ref, bf16[256,1536]{1,0:T(8,128)(2,1)} %bitcast.19, bf16[256,1536]{1,0:T(8,128)(2,1)} %copy-done.4, bf16[256,1536]{1,0:T(8,128)(2,1)} %copy-done.2, bf16[256,1536]{1,0:T(8,128)(2,1)} %bitcast.13, bf16[256,1536]{1,0:T(8,128)(2,1)} %copy-done.3, ...), custom_call_target="tpu_custom_call" | custom-call | tf_op jit(solution)/shard_map/near_attention/pallas_call | solution.py:219
  146.2 4.8 %merge.1 = bf16[256,1536]{1,0:T(8,128)(2,1)} custom-call(s32[1]{0:T(128)} %bitcast.polar_ref, f32[256,1536]{1,0:T(8,128)} %get-tuple-element.39.near_ref, bf16[256,1536]{1,0:T(8,128)(2,1)} %get-tuple-element.40.own_ref, bf16[256,1536]{1,0:T(8,128)(2,1)} %copy-done.7, f32[256,128]{1,0:T(8,128)} %get-tuple-element.42.refs_0_, ...), custom_call_target="tpu_custom_call" | custom-call | tf_op jit(solution)/shard_map/merge/pallas_call | solution.py:238
  (55 shorter events, 11.0 us)
Async XLA Ops:
  2.7 12.9 %collective-permute-start.9 = (bf16[16,1536]{1,0:T(8,128)(2,1)S(1)}, bf16[16,1536]{1,0:T(8,128)(2,1)S(1)}, u32[]{:S(2)}, u32[]{:S(2)}) collective-permute-start(bf16[16,1536]{1,0:T(8,128)(2,1)S(1)} %gather_fusion.1), channel_id=1, source_target_pairs={{0,64},{1,65},{2,66},{3,67},{4,68},{5,69},{6,70},{7,71},{8,72},{9,... | collective-permute-start | bytes 147464 | tf_op jit(solution)/shard_map/ppermute | solution.py:37
  4.0 29.6 %collective-permute-start = (bf16[256,1536]{1,0:T(8,128)(2,1)}, bf16[256,1536]{1,0:T(8,128)(2,1)S(1)}, u32[]{:S(2)}, u32[]{:S(2)}) collective-permute-start(bf16[256,1536]{1,0:T(8,128)(2,1)} %bitcast.10), channel_id=1, source_target_pairs={{0,1},{1,2},{2,3},{3,4},{4,5},{5,6},{6,7},{7,8},{8,9},{9,10},{10,1... | collective-permute-start | bytes 2359304 | tf_op jit(solution)/shard_map/ppermute | solution.py:26
  4.7 32.5 %collective-permute-start.1 = (bf16[256,1536]{1,0:T(8,128)(2,1)}, bf16[256,1536]{1,0:T(8,128)(2,1)S(1)}, u32[]{:S(2)}, u32[]{:S(2)}) collective-permute-start(bf16[256,1536]{1,0:T(8,128)(2,1)} %bitcast.11), channel_id=1, source_target_pairs={{0,63},{1,0},{2,1},{3,2},{4,3},{5,4},{6,5},{7,6},{8,7},{9,8},{10,9... | collective-permute-start | bytes 2359304 | tf_op jit(solution)/shard_map/ppermute | solution.py:26
  16.3 29.0 %all-to-all-start = ((bf16[8,16,1536]{2,1,0:T(8,128)(2,1)}), bf16[8,16,1536]{2,1,0:T(8,128)(2,1)S(1)}, u32[]{:S(2)}, u32[]{:S(2)}) async-start(bf16[8,16,1536]{2,1,0:T(8,128)(2,1)} %broadcast_in_dim.2), calls=%async_computation | async-start | bytes 786432 | tf_op jit(solution)/shard_map/all_to_all | solution.py:42
  33.6 88.7 %copy-start.2 = (bf16[256,1536]{1,0:T(8,128)(2,1)}, bf16[256,1536]{1,0:T(8,128)(2,1)S(1)}, u32[]{:S(2)}) copy-start(bf16[256,1536]{1,0:T(8,128)(2,1)S(1)} %collective-permute-done.refs_2_) | copy-start | bytes 2359300
  37.1 85.1 %copy-start.3 = (bf16[256,1536]{1,0:T(8,128)(2,1)}, bf16[256,1536]{1,0:T(8,128)(2,1)S(1)}, u32[]{:S(2)}) copy-start(bf16[256,1536]{1,0:T(8,128)(2,1)S(1)} %collective-permute-done.1.refs_4_) | copy-start | bytes 2359300
  37.1 22.5 %collective-permute-start.2 = (bf16[256,1536]{1,0:T(8,128)(2,1)S(1)}, bf16[256,1536]{1,0:T(8,128)(2,1)}, u32[]{:S(2)}, u32[]{:S(2)}) collective-permute-start(bf16[256,1536]{1,0:T(8,128)(2,1)S(1)} %bitcast.16), channel_id=1, source_target_pairs={{0,1},{1,2},{2,3},{3,4},{4,5},{5,6},{6,7},{7,8},{8,9},{9,10},{10,1... | collective-permute-start | bytes 2359304 | tf_op jit(solution)/shard_map/ppermute | solution.py:26
  37.1 22.5 %collective-permute-start.3 = (bf16[256,1536]{1,0:T(8,128)(2,1)S(1)}, bf16[256,1536]{1,0:T(8,128)(2,1)}, u32[]{:S(2)}, u32[]{:S(2)}) collective-permute-start(bf16[256,1536]{1,0:T(8,128)(2,1)S(1)} %bitcast.17), channel_id=1, source_target_pairs={{0,63},{1,0},{2,1},{3,2},{4,3},{5,4},{6,5},{7,6},{8,7},{9,8},{10,9... | collective-permute-start | bytes 2359304 | tf_op jit(solution)/shard_map/ppermute | solution.py:26
  45.3 39.4 %collective-permute-start.10 = (bf16[128,1536]{1,0:T(8,128)(2,1)S(1)}, bf16[128,1536]{1,0:T(8,128)(2,1)}, u32[]{:S(2)}, u32[]{:S(2)}) collective-permute-start(bf16[128,1536]{1,0:T(8,128)(2,1)S(1)} %bitcast.21), channel_id=1, source_target_pairs={{0,8},{1,9},{2,10},{3,11},{4,12},{5,13},{6,14},{7,15},{8,16},{9,17... | collective-permute-start | bytes 1179656 | tf_op jit(solution)/shard_map/ppermute | solution.py:50
  45.3 39.4 %collective-permute-start.11 = (bf16[128,1536]{1,0:T(8,128)(2,1)S(1)}, bf16[128,1536]{1,0:T(8,128)(2,1)}, u32[]{:S(2)}, u32[]{:S(2)}) collective-permute-start(bf16[128,1536]{1,0:T(8,128)(2,1)S(1)} %bitcast.22), channel_id=1, source_target_pairs={{0,24},{1,25},{2,26},{3,27},{4,28},{5,29},{6,30},{7,31},{8,0},{9,1... | collective-permute-start | bytes 1179656 | tf_op jit(solution)/shard_map/ppermute | solution.py:50
  48.6 37.6 %collective-permute-start.8 = (bf16[256,1536]{1,0:T(8,128)(2,1)S(1)}, bf16[256,1536]{1,0:T(8,128)(2,1)}, u32[]{:S(2)}, u32[]{:S(2)}) collective-permute-start(bf16[256,1536]{1,0:T(8,128)(2,1)S(1)} %bitcast.20), channel_id=1, source_target_pairs={{0,32},{1,33},{2,34},{3,35},{4,36},{5,37},{6,38},{7,39},{8,40},{9,... | collective-permute-start | bytes 2359304 | tf_op jit(solution)/shard_map/ppermute | solution.py:59
  59.7 38.9 %collective-permute-start.4 = (bf16[256,1536]{1,0:T(8,128)(2,1)S(1)}, bf16[256,1536]{1,0:T(8,128)(2,1)S(1)}, u32[]{:S(2)}, u32[]{:S(2)}) collective-permute-start(bf16[256,1536]{1,0:T(8,128)(2,1)S(1)} %collective-permute-done.refs_2_), channel_id=1, source_target_pairs={{0,1},{1,2},{2,3},{3,4},{4,5},{5,6},{6,7},{7,8},{8,9},{9,10},{10,1... | collective-permute-start | bytes 2359304 | tf_op jit(solution)/shard_map/ppermute | solution.py:26
  59.7 40.2 %collective-permute-start.5 = (bf16[256,1536]{1,0:T(8,128)(2,1)S(1)}, bf16[256,1536]{1,0:T(8,128)(2,1)S(1)}, u32[]{:S(2)}, u32[]{:S(2)}) collective-permute-start(bf16[256,1536]{1,0:T(8,128)(2,1)S(1)} %collective-permute-done.1.refs_4_), channel_id=1, source_target_pairs={{0,63},{1,0},{2,1},{3,2},{4,3},{5,4},{6,5},{7,6},{8,7},{9,8},{10,9... | collective-permute-start | bytes 2359304 | tf_op jit(solution)/shard_map/ppermute | solution.py:26
  86.0 7.9 %collective-permute-start.12 = (bf16[64,1536]{1,0:T(8,128)(2,1)S(1)}, bf16[64,1536]{1,0:T(8,128)(2,1)}, u32[]{:S(2)}, u32[]{:S(2)}) collective-permute-start(bf16[64,1536]{1,0:T(8,128)(2,1)S(1)} %get-tuple-element.46), channel_id=1, source_target_pairs={{0,24},{1,9},{2,10},{3,11},{4,12},{5,13},{6,14},{7,15},{8,0},{9,17... | collective-permute-start | bytes 589832 | tf_op jit(solution)/shard_map/ppermute | solution.py:50
  86.1 11.1 %collective-permute-start.13 = (bf16[64,1536]{1,0:T(8,128)(2,1)S(1)}, bf16[64,1536]{1,0:T(8,128)(2,1)}, u32[]{:S(2)}, u32[]{:S(2)}) collective-permute-start(bf16[64,1536]{1,0:T(8,128)(2,1)S(1)} %get-tuple-element.45), channel_id=1, source_target_pairs={{0,24},{1,25},{2,26},{3,27},{4,28},{5,29},{6,30},{7,15},{8,0},{9,1... | collective-permute-start | bytes 589832 | tf_op jit(solution)/shard_map/ppermute | solution.py:50
  86.2 15.8 %collective-permute-start.14 = (bf16[128,1536]{1,0:T(8,128)(2,1)S(1)}, bf16[128,1536]{1,0:T(8,128)(2,1)}, u32[]{:S(2)}, u32[]{:S(2)}) collective-permute-start(bf16[128,1536]{1,0:T(8,128)(2,1)S(1)} %bitcast.23), channel_id=1, source_target_pairs={{64,0},{65,1},{66,2},{67,3},{68,4},{69,5},{70,6},{71,7},{72,8},{73... | collective-permute-start | bytes 1179656 | tf_op jit(solution)/shard_map/ppermute | solution.py:37
  94.0 8.2 %collective-permute-start.15 = (bf16[128,1536]{1,0:T(8,128)(2,1)}, bf16[128,1536]{1,0:T(8,128)(2,1)}, u32[]{:S(2)}, u32[]{:S(2)}) collective-permute-start(bf16[128,1536]{1,0:T(8,128)(2,1)} %collective-permute-done.10.refs_1_), channel_id=1, source_target_pairs={{64,0},{65,1},{66,2},{67,3},{68,4},{69,5},{70,6},{71,7},{72,8},{73... | collective-permute-start | bytes 1179656 | tf_op jit(solution)/shard_map/ppermute | solution.py:37
  97.2 12.6 %collective-permute-start.16 = (bf16[128,1536]{1,0:T(8,128)(2,1)}, bf16[128,1536]{1,0:T(8,128)(2,1)}, u32[]{:S(2)}, u32[]{:S(2)}) collective-permute-start(bf16[128,1536]{1,0:T(8,128)(2,1)} %collective-permute-done.11.refs_2_), channel_id=1, source_target_pairs={{64,0},{65,1},{66,2},{67,3},{68,4},{69,5},{70,6},{71,7},{72,8},{73... | collective-permute-start | bytes 1179656 | tf_op jit(solution)/shard_map/ppermute | solution.py:37
  98.5 11.3 %collective-permute-start.17 = (bf16[64,1536]{1,0:T(8,128)(2,1)}, bf16[64,1536]{1,0:T(8,128)(2,1)}, u32[]{:S(2)}, u32[]{:S(2)}) collective-permute-start(bf16[64,1536]{1,0:T(8,128)(2,1)} %collective-permute-done.12.refs_3_), channel_id=1, source_target_pairs={{64,0},{65,1},{66,2},{67,3},{68,4},{69,5},{70,6},{71,7},{72,8},{73... | collective-permute-start | bytes 589832 | tf_op jit(solution)/shard_map/ppermute | solution.py:37
  100.7 9.1 %collective-permute-start.18 = (bf16[64,1536]{1,0:T(8,128)(2,1)}, bf16[64,1536]{1,0:T(8,128)(2,1)}, u32[]{:S(2)}, u32[]{:S(2)}) collective-permute-start(bf16[64,1536]{1,0:T(8,128)(2,1)} %collective-permute-done.13.refs_4_), channel_id=1, source_target_pairs={{64,0},{65,1},{66,2},{67,3},{68,4},{69,5},{70,6},{71,7},{72,8},{73... | collective-permute-start | bytes 589832 | tf_op jit(solution)/shard_map/ppermute | solution.py:37
  102.0 29.4 %collective-permute-start.6 = (bf16[256,1536]{1,0:T(8,128)(2,1)}, bf16[256,1536]{1,0:T(8,128)(2,1)S(1)}, u32[]{:S(2)}, u32[]{:S(2)}) collective-permute-start(bf16[256,1536]{1,0:T(8,128)(2,1)} %collective-permute-done.2.refs_7_), channel_id=1, source_target_pairs={{0,1},{1,2},{2,3},{3,4},{4,5},{5,6},{6,7},{7,8},{8,9},{9,10},{10,1... | collective-permute-start | bytes 2359304 | tf_op jit(solution)/shard_map/ppermute | solution.py:26
  102.1 29.3 %collective-permute-start.7 = (bf16[256,1536]{1,0:T(8,128)(2,1)}, bf16[256,1536]{1,0:T(8,128)(2,1)}, u32[]{:S(2)}, u32[]{:S(2)}) collective-permute-start(bf16[256,1536]{1,0:T(8,128)(2,1)} %collective-permute-done.3.refs_9_), channel_id=1, source_target_pairs={{0,63},{1,0},{2,1},{3,2},{4,3},{5,4},{6,5},{7,6},{8,7},{9,8},{10,9... | collective-permute-start | bytes 2359304 | tf_op jit(solution)/shard_map/ppermute | solution.py:26
  122.3 23.0 %collective-permute-start.19 = (bf16[256,1536]{1,0:T(8,128)(2,1)}, bf16[256,1536]{1,0:T(8,128)(2,1)S(1)}, u32[]{:S(2)}, u32[]{:S(2)}) collective-permute-start(bf16[256,1536]{1,0:T(8,128)(2,1)} %get-tuple-element.37), channel_id=1, source_target_pairs={{0,32},{1,33},{2,34},{3,35},{4,36},{5,37},{6,38},{7,39},{8,40},{9,... | collective-permute-start | bytes 2359304 | tf_op jit(solution)/shard_map/ppermute | solution.py:59
  124.6 20.6 %collective-permute-start.20 = (f32[256,128]{1,0:T(8,128)}, f32[256,128]{1,0:T(8,128)S(1)}, u32[]{:S(2)}, u32[]{:S(2)}) collective-permute-start(f32[256,128]{1,0:T(8,128)} %get-tuple-element.38), channel_id=1, source_target_pairs={{0,32},{1,33},{2,34},{3,35},{4,36},{5,37},{6,38},{7,39},{8,40},{9,... | collective-permute-start | bytes 393224 | tf_op jit(solution)/shard_map/ppermute | solution.py:59
  (9 other events, 197.7 us)
